TPU v7x, 256 devices: a whole 4x4x8 slice. The times are simulated.
256 devices in a mesh: tok: 8 (over z), out: 16 (over y_lo, x, core), grp: 2 (over y_hi).
Axes of the slice: x: 4, y: 4 (y_hi: 2, y_lo: 2; y = y_hi * 2 + y_lo), z: 8, core: 2. Of those that a mesh axis runs over, the one named last changes fastest.
Arguments:
- activations: bfloat16 [2048, 2, 2048], P(('tok', 'grp'), None, 'out'), may hold values from -16 to 16
- out_grads: bfloat16 [2048, 2, 2048], P(('tok', 'grp'), None, 'out'), may hold values from -16 to 16
- weight: bfloat16 [2, 2048, 4096], P(None, 'out'), may hold values from -0.09375 to 0.09375
Outputs:
- update: bfloat16 [4096, 2, 2048], P(('tok', 'grp'), None, 'out')
- input_grad: bfloat16 [2048, 2, 2048], P(('tok', 'grp'), None, 'out')
All inputs are finite; a program needn't handle non-finite values.
Results may differ from a plain program's by a relative error of at most 0.0092.
Values may be sent and summed in bfloat16 or wider, within the bound.
No kernel may reach another device: no remote copies, remote signals or barrier semaphores. Data moves between devices by JAX's collectives and lax.ppermute only.
A program may use at most 64 MiB of HBM per device.

v0:
```python
import math

import jax
import jax.numpy as jnp
from jax import lax
from jax.sharding import Mesh
from jax.sharding import PartitionSpec as P

POWER = 3
OUT = ("out_0", "out_1", "out_2")
TOK_OUT = ("tok", "out_0", "out_1", "out_2")


DAMPING = 0.1
HIGH = lax.Precision.HIGHEST


def own_rows(so_far, axes):
    for axis in axes:
        so_far = lax.psum_scatter(so_far, axis, scatter_dimension=0, tiled=True)
    return so_far


def in_order(pieces, dim):
    lengths = list(pieces.shape[1:])
    lengths[dim] *= pieces.shape[0]
    return jnp.moveaxis(pieces, 0, dim).reshape(lengths)


def copy_for_each(array, axis):
    peers = lax.axis_size(axis)
    return lax.all_to_all(
        jnp.broadcast_to(array[None], (peers, *array.shape)), axis, 0, 0, tiled=True
    )


def gather_directly(array, axis, dim):
    return in_order(copy_for_each(array, axis), dim)


def one_axis_at_a_time(array, axes):
    for axis in axes:
        array = lax.psum(array, axis)
    return array


def swapped(array, axis, stride):
    return lax.ppermute(array, axis, [(i, i ^ 1 << stride) for i in range(lax.axis_size(axis))])


def spread(piece):
    return lax.all_gather(piece, OUT, axis=2, tiled=True)


def token_sums(maker, rows):
    return own_rows(maker(jnp.int32(0), rows * lax.axis_size(("tok", "grp"))), ("tok", "grp"))


def owner_rows(piece):
    return gather_directly(piece, "tok", 0)


def owner_total(vector):
    return one_axis_at_a_time(vector, TOK_OUT)


def diagonal_mask(rows, width, row_start, col_start):
    row_ids = row_start + lax.broadcasted_iota(jnp.int32, (rows, 1, width), 0)
    col_ids = col_start + lax.broadcasted_iota(jnp.int32, (rows, 1, width), 2)
    return jnp.where(row_ids == col_ids, 1.0, 0.0).astype(jnp.float32)


def multiply(left, right, gather_columns):
    row_band = spread(left)
    column_band = gather_columns(right)
    return jnp.einsum("rkj,jkc->rkc", row_band, column_band, preferred_element_type=jnp.float32)


def inverse_roots(tile, row_start, col_start, gather_columns, total):
    rows, count, width = tile.shape
    block = width * lax.axis_size(OUT)
    mask = diagonal_mask(rows, width, row_start, col_start)
    vector = jnp.ones((count, block), jnp.float32)
    image = vector
    for step in range(POWER):
        columns = lax.dynamic_slice_in_dim(vector, col_start, width, 1)
        part = jnp.einsum("rkc,kc->kr", tile, columns, precision=HIGH)
        placed = lax.dynamic_update_slice_in_dim(
            jnp.zeros((count, block), jnp.float32), part, row_start, 1
        )
        image = total(placed)
        if step + 1 < POWER:
            vector = image / jnp.sqrt(jnp.sum(image * image, axis=1, keepdims=True))
    scale = jnp.sum(vector * image, axis=1) / jnp.sum(vector * vector, axis=1)
    start = tile / scale[None, :, None]
    start_low = start.astype(jnp.bfloat16)
    first_low = ((3.0 * mask - start) / 2.0).astype(jnp.bfloat16)
    square_low = multiply(first_low, first_low, gather_columns).astype(jnp.bfloat16)
    moved = multiply(square_low, start_low, gather_columns)
    second_low = ((3.0 * mask - moved) / 2.0).astype(jnp.bfloat16)
    roots = multiply(first_low, second_low, gather_columns) / jnp.sqrt(scale)[None, :, None]
    return roots.astype(jnp.bfloat16)


def local(activations, out_grads, weight):
    tok_dev, blocks, width = activations.shape
    block = width * lax.axis_size(OUT)
    token_count = tok_dev * lax.axis_size("tok") * lax.axis_size("grp")
    col_start = lax.axis_index(OUT) * width
    local_sides = jnp.concatenate([activations, out_grads], axis=1)
    whole_sides = spread(local_sides)
    grads_whole = whole_sides[:, blocks:, :]
    weight_rows = weight.reshape(blocks, width, blocks, block)
    input_grad = jnp.einsum(
        "tjq,bcjq->tbc", grads_whole, weight_rows, preferred_element_type=jnp.float32
    ).astype(jnp.bfloat16)
    rows = block // lax.axis_size("tok")
    row_start = lax.axis_index("tok") * rows
    paired = whole_sides.reshape(tok_dev, 2, blocks, block)
    own_cols = local_sides.reshape(tok_dev, 2, blocks, width)

    def side_terms(start, span):

        def one_group(group):
            side = group % 2
            piece = group // 2
            row_part = lax.dynamic_slice(
                paired, (0, side, 0, piece * rows), (tok_dev, 1, blocks, rows)
            )[:, 0]
            col_part = lax.dynamic_slice(own_cols, (0, side, 0, 0), (tok_dev, 1, blocks, width))[
                :, 0
            ]
            return jnp.einsum(
                "tbr,tbc->rbc", row_part, col_part, preferred_element_type=jnp.float32
            )

        groups = jnp.arange(span // rows, dtype=jnp.int32)
        return lax.map(one_group, groups).reshape(span, blocks, width)

    sums = token_sums(side_terms, rows)
    tile = sums / token_count + DAMPING * diagonal_mask(rows, width, row_start, col_start)
    roots = inverse_roots(tile, row_start, col_start, owner_rows, owner_total)
    own_band = owner_rows(roots)
    other_band = swapped(own_band, "grp", 0)
    first_side = lax.axis_index("grp") == 0
    bands = jnp.concatenate(
        [jnp.where(first_side, own_band, other_band), jnp.where(first_side, other_band, own_band)],
        axis=1,
    )
    whitened = jnp.einsum(
        "tkj,jkc->tkc", whole_sides, bands, preferred_element_type=jnp.float32
    ).astype(jnp.bfloat16)
    acts_whole = spread(whitened[:, :blocks, :]).reshape(tok_dev, blocks * block)
    grads_low = whitened[:, blocks:, :]
    owned_acts = lax.all_to_all(acts_whole, ("tok", "grp"), split_axis=1, concat_axis=0, tiled=True)
    update = jnp.einsum(
        "ta,tbc->abc",
        owned_acts,
        gather_directly(grads_low, ("tok", "grp"), 0),
        preferred_element_type=jnp.float32,
    )
    update = (update / math.sqrt(token_count)).astype(jnp.bfloat16)
    return (update, input_grad)


def solution(mesh):
    split = Mesh(
        mesh.devices.reshape(mesh.shape["tok"], 2, 4, 2, mesh.shape["grp"]),
        ("tok", "out_0", "out_1", "out_2", "grp"),
    )
    in_specs = (P(("tok", "grp"), None, OUT), P(("tok", "grp"), None, OUT), P(None, OUT, None))
    out_specs = (P(("tok", "grp"), None, OUT), P(("tok", "grp"), None, OUT))
    return jax.shard_map(local, mesh=split, in_specs=in_specs, out_specs=out_specs, check_vma=False)
```

profile of v0, /device:TPU:64, one launch (start us, length us, event | category | flops | bytes accessed | tf_op | source)
XLA Modules:
  0.0 647.7 jit_solution(17056723738061298160)
XLA Ops:
  9.7 42.8 %all-gather.5.cloned.1.call-done = bf16[128,4,2048]{2,0,1:T(8,128)(2,1)} async-done(((bf16[128,4,128]{2,0,1:T(8,128)(2,1)}), bf16[128,4,2048]{2,0,1:T(8,128)(2,1)}) %all-gather.5.cloned.1.call-update) | async-done | bytes 2097168 | tf_op jit(solution)/shard_map/all_gather | solution.py:52
  52.4 79.2 %while.12 = (s32[]{:T(128)}, f32[16,256,2,128]{3,1,0,2:T(8,128)}, s32[16]{0:T(128)S(1)}, bf16[128,2,2,128]{3,0,2,1:T(8,128)(2,1)}, bf16[128,2,2,2048]{3,0,2,1:T(...) while((s32[]{:T(128)}, f32[16,256,2,128]{3,1,0,2:T(8,128)}, ...), condition=%wide.region_1.2_spmd, body=%wide.region_0.1_spmd.sunk | while | flops 16777244 | bytes 1509764 | solution.py:138
  131.8 53.8 %reduce-scatter.3.cloned.1.call-done = f32[512,2,128]{2,0,1:T(8,128)} async-done(((f32[4096,2,128]{2,0,1:T(8,128)}), f32[512,2,128]{2,0,1:T(8,128)}) %reduce-scatter.3.cloned.1.call-update) | async-done | bytes 524304 | tf_op jit(solution)/shard_map/reduce_scatter | solution.py:20
  185.8 23.9 %reduce-scatter.5.cloned.1.call-done = f32[256,2,128]{2,0,1:T(8,128)} async-done(((f32[512,2,128]{2,0,1:T(8,128)}), f32[256,2,128]{2,0,1:T(8,128)}) %reduce-scatter.5.cloned.1.call-update) | async-done | bytes 262160 | tf_op jit(solution)/shard_map/reduce_scatter | solution.py:20
  211.0 28.0 %psum.84 = f32[2,2048]{1,0:T(2,128)S(1)} all-reduce(f32[2,2048]{1,0:T(2,128)S(1)} %bitcast_dynamic-update-slice_fusion.2), channel_id=1, replica_groups=mesh['tok'=8,'out_0'=2,'out_1'=4,'out_2'=2,'grp'=2] {'tok'}, use_global_device_ids=true, to_apply=%region_4.5 | all-reduce | flops 4096 | bytes 32768 | tf_op jit(solution)/shard_map/psum | solution.py:43
  238.9 7.2 %psum.85 = f32[2,2048]{1,0:T(2,128)S(1)} all-reduce(f32[2,2048]{1,0:T(2,128)S(1)} %psum.84), channel_id=1, replica_groups=mesh['tok'=8,'out_0'=2,'out_1'=4,'out_2'=2,'grp'=2] {'out_0'}, use_global_device_ids=true, to_apply=%region_5.6 | all-reduce | flops 4096 | bytes 32768 | tf_op jit(solution)/shard_map/psum | solution.py:43
  246.1 16.8 %psum.86 = f32[2,2048]{1,0:T(2,128)S(1)} all-reduce(f32[2,2048]{1,0:T(2,128)S(1)} %psum.85), channel_id=1, replica_groups=mesh['tok'=8,'out_0'=2,'out_1'=4,'out_2'=2,'grp'=2] {'out_1'}, use_global_device_ids=true, to_apply=%region_6.7 | all-reduce | flops 4096 | bytes 32768 | tf_op jit(solution)/shard_map/psum | solution.py:43
  267.9 27.0 %psum.88 = f32[2,2048]{1,0:T(2,128)S(1)} all-reduce(f32[2,2048]{1,0:T(2,128)S(1)} %bitcast_dynamic-update-slice_fusion.1), channel_id=1, replica_groups=mesh['tok'=8,'out_0'=2,'out_1'=4,'out_2'=2,'grp'=2] {'tok'}, use_global_device_ids=true, to_apply=%region_9.10 | all-reduce | flops 4096 | bytes 32768 | tf_op jit(solution)/shard_map/psum | solution.py:43
  294.9 8.1 %psum.89 = f32[2,2048]{1,0:T(2,128)S(1)} all-reduce(f32[2,2048]{1,0:T(2,128)S(1)} %psum.88), channel_id=1, replica_groups=mesh['tok'=8,'out_0'=2,'out_1'=4,'out_2'=2,'grp'=2] {'out_0'}, use_global_device_ids=true, to_apply=%region_10.11 | all-reduce | flops 4096 | bytes 32768 | tf_op jit(solution)/shard_map/psum | solution.py:43
  303.0 14.3 %psum.90 = f32[2,2048]{1,0:T(2,128)S(1)} all-reduce(f32[2,2048]{1,0:T(2,128)S(1)} %psum.89), channel_id=1, replica_groups=mesh['tok'=8,'out_0'=2,'out_1'=4,'out_2'=2,'grp'=2] {'out_1'}, use_global_device_ids=true, to_apply=%region_11.12 | all-reduce | flops 4096 | bytes 32768 | tf_op jit(solution)/shard_map/psum | solution.py:43
  322.2 27.6 %psum.92 = f32[2,2048]{1,0:T(2,128)S(1)} all-reduce(f32[2,2048]{1,0:T(2,128)S(1)} %bitcast_dynamic-update-slice_fusion), channel_id=1, replica_groups=mesh['tok'=8,'out_0'=2,'out_1'=4,'out_2'=2,'grp'=2] {'tok'}, use_global_device_ids=true, to_apply=%region_14.15 | all-reduce | flops 4096 | bytes 32768 | tf_op jit(solution)/shard_map/psum | solution.py:43
  349.8 7.2 %psum.93 = f32[2,2048]{1,0:T(2,128)S(1)} all-reduce(f32[2,2048]{1,0:T(2,128)S(1)} %psum.92), channel_id=1, replica_groups=mesh['tok'=8,'out_0'=2,'out_1'=4,'out_2'=2,'grp'=2] {'out_0'}, use_global_device_ids=true, to_apply=%region_15.16 | all-reduce | flops 4096 | bytes 32768 | tf_op jit(solution)/shard_map/psum | solution.py:43
  357.0 15.4 %psum.94 = f32[2,2048]{1,0:T(2,128)S(1)} all-reduce(f32[2,2048]{1,0:T(2,128)S(1)} %psum.93), channel_id=1, replica_groups=mesh['tok'=8,'out_0'=2,'out_1'=4,'out_2'=2,'grp'=2] {'out_1'}, use_global_device_ids=true, to_apply=%region_16.17 | all-reduce | flops 4096 | bytes 32768 | tf_op jit(solution)/shard_map/psum | solution.py:43
  378.9 33.0 %all_to_all.41 = bf16[8,256,2,128]{1,3,2,0:T(8,128)(2,1)S(1)} all-to-all(bf16[8,256,2,128]{1,3,2,0:T(8,128)(2,1)S(1)} %broadcast_in_dim.58), channel_id=1, replica_groups=mesh['tok'=8,'out_0'=2,'out_1'=4,'out_2'=2,'grp'=2] {'tok'}, dimensions={0} | all-to-all | bytes 2097152 | tf_op jit(solution)/shard_map/all_to_all | solution.py:32
  412.0 3.6 all-gather.7.cloned.1.call-done
  419.0 33.3 %all_to_all.42 = bf16[8,256,2,128]{1,3,2,0:T(8,128)(2,1)S(1)} all-to-all(bf16[8,256,2,128]{1,3,2,0:T(8,128)(2,1)S(1)} %broadcast_in_dim.57), channel_id=1, replica_groups=mesh['tok'=8,'out_0'=2,'out_1'=4,'out_2'=2,'grp'=2] {'tok'}, dimensions={0} | all-to-all | bytes 2097152 | tf_op jit(solution)/shard_map/all_to_all | solution.py:32
  458.1 33.3 %all_to_all.43 = bf16[8,256,2,128]{1,3,2,0:T(8,128)(2,1)S(1)} all-to-all(bf16[8,256,2,128]{1,3,2,0:T(8,128)(2,1)S(1)} %broadcast_in_dim.59), channel_id=1, replica_groups=mesh['tok'=8,'out_0'=2,'out_1'=4,'out_2'=2,'grp'=2] {'tok'}, dimensions={0} | all-to-all | bytes 2097152 | tf_op jit(solution)/shard_map/all_to_all | solution.py:32
  492.6 31.3 %all_to_all.44 = bf16[8,256,2,128]{1,3,2,0:T(8,128)(2,1)S(1)} all-to-all(bf16[8,256,2,128]{1,3,2,0:T(8,128)(2,1)S(1)} %broadcast_in_dim.60), channel_id=1, replica_groups=mesh['tok'=8,'out_0'=2,'out_1'=4,'out_2'=2,'grp'=2] {'tok'}, dimensions={0} | all-to-all | bytes 2097152 | tf_op jit(solution)/shard_map/all_to_all | solution.py:32
  527.1 20.9 %collective-permute-done = bf16[2048,2,128]{0,2,1:T(8,128)(2,1)S(1)} collective-permute-done((bf16[2048,2,128]{0,2,1:T(8,128)(2,1)S(1)}, bf16[2048,2,128]{0,2,1:T(8,128)(2,1)S(1)}, u32[]{:S(2)}, u32[]{:S(2)}) %collective-permute-start) | collective-permute-done | bytes 1048608 | tf_op jit(solution)/shard_map/ppermute | solution.py:48
  550.9 8.8 %all-to-all-start.5 = ((bf16[16,128,2,128]{3,1,2,0:T(8,128)(2,1)}), bf16[16,128,2,128]{3,1,2,0:T(8,128)(2,1)S(1)}, u32[]{:S(2)}, u32[]{:S(2)}) async-start(bf16[16,128,2,128]{3,1,2,0:T(8,128)(2,1)} %broadcast_in_dim.61), calls=%async_computation.7 | async-start | bytes 2097152 | tf_op jit(solution)/shard_map/all_to_all | solution.py:32
  560.3 25.8 %all-to-all-done.5 = bf16[16,128,2,128]{3,1,2,0:T(8,128)(2,1)S(1)} async-done(((bf16[16,128,2,128]{3,1,2,0:T(8,128)(2,1)}), bf16[16,128,2,128]{3,1,2,0:T(8,128)(2,1)S(1)}, u32[]{:S(2)}, u32[]{:S(2)}) %all-to-all-start.5) | async-done | bytes 1048608 | tf_op jit(solution)/shard_map/all_to_all | solution.py:32
  586.2 15.2 %all-gather.11.cloned.1.call-done = bf16[128,2,2048]{0,2,1:T(8,128)(2,1)} async-done(((bf16[128,2,128]{0,2,1:T(8,128)(2,1)}), bf16[128,2,2048]{0,2,1:T(8,128)(2,1)}) %all-gather.11.cloned.1.call-update) | async-done | bytes 1048592 | tf_op jit(solution)/shard_map/all_gather | solution.py:52
  601.4 10.2 %all-to-all-start.4 = ((bf16[128,16,256]{0,2,1:T(8,128)(2,1)}), bf16[128,16,256]{0,2,1:T(8,128)(2,1)S(1)}, u32[]{:S(2)}, u32[]{:S(2)}) async-start(bf16[128,16,256]{0,2,1:T(8,128)(2,1)} %bitcast.112), calls=%async_computation.6 | async-start | bytes 2097152 | tf_op jit(solution)/shard_map/all_to_all | solution.py:155
  615.0 24.7 %all-to-all-done.4 = bf16[128,16,256]{0,2,1:T(8,128)(2,1)S(1)} async-done(((bf16[128,16,256]{0,2,1:T(8,128)(2,1)}), bf16[128,16,256]{0,2,1:T(8,128)(2,1)S(1)}, u32[]{:S(2)}, u32[]{:S(2)}) %all-to-all-start.4) | async-done | bytes 1048608 | tf_op jit(solution)/shard_map/all_to_all | solution.py:155
  (137 shorter events, 83.6 us)
Async XLA Ops:
  7.2 45.3 %all-gather.5.cloned.1.call-start = ((), (), s32[]{:S(2)}) async-start(), calls=%async_computation.8 | async-start | bytes 2228224 | tf_op jit(solution)/shard_map/all_gather | solution.py:52
  8.9 0.7 copy-start.1
  9.6 175.9 %reduce-scatter.3.cloned.1.call-start = ((), (), s32[]{:S(2)}) async-start(), calls=%async_computation.9 | async-start | bytes 4718592 | tf_op jit(solution)/shard_map/reduce_scatter | solution.py:20
  131.7 77.9 %reduce-scatter.5.cloned.1.call-start = ((), (), s32[]{:S(2)}) async-start(), calls=%async_computation.10 | async-start | bytes 786432 | tf_op jit(solution)/shard_map/reduce_scatter | solution.py:20
  185.6 230.1 %all-gather.7.cloned.1.call-start = ((), (), s32[]{:S(2)}) async-start(), calls=%async_computation.11 | async-start | bytes 2228224 | tf_op jit(solution)/shard_map/all_gather | solution.py:52
  377.7 77.6 %all-gather.9.cloned.1.call-start = ((), (), s32[]{:S(2)}) async-start(), calls=%async_computation.12 | async-start | bytes 2228224 | tf_op jit(solution)/shard_map/all_gather | solution.py:52
  458.1 33.5 %copy-start = (bf16[256,2,2048]{2,0,1:T(8,128)(2,1)S(1)}, bf16[256,2,2048]{2,0,1:T(8,128)(2,1)}, u32[]{:S(2)}) copy-start(bf16[256,2,2048]{2,0,1:T(8,128)(2,1)} %all-gather.7.cloned.1.call-done) | copy-start | bytes 6291460
  524.0 24.0 %collective-permute-start = (bf16[2048,2,128]{0,2,1:T(8,128)(2,1)S(1)}, bf16[2048,2,128]{0,2,1:T(8,128)(2,1)S(1)}, u32[]{:S(2)}, u32[]{:S(2)}) collective-permute-start(bf16[2048,2,128]{0,2,1:T(8,128)(2,1)S(1)} %bitcast.102), channel_id=1, source_target_pairs={{0,1},{1,0},{2,3},{3,2},{4,5},{5,4},{6,7},{7,6},{8,9},{9,8},{10,11... | collective-permute-start | bytes 3145736 | tf_op jit(solution)/shard_map/ppermute | solution.py:48
  527.1 21.1 %copy-start.2 = (bf16[128,2,2,2048]{3,0,2,1:T(8,128)(2,1)S(1)}, bf16[128,2,2,2048]{3,0,2,1:T(8,128)(2,1)}, u32[]{:S(2)}) copy-start(bf16[128,2,2,2048]{3,0,2,1:T(8,128)(2,1)} %get-tuple-element.215) | copy-start | bytes 6291460
  550.9 35.3 %all-to-all-start.5 = ((bf16[16,128,2,128]{3,1,2,0:T(8,128)(2,1)}), bf16[16,128,2,128]{3,1,2,0:T(8,128)(2,1)S(1)}, u32[]{:S(2)}, u32[]{:S(2)}) async-start(bf16[16,128,2,128]{3,1,2,0:T(8,128)(2,1)} %broadcast_in_dim.61), calls=%async_computation.7 | async-start | bytes 2097152 | tf_op jit(solution)/shard_map/all_to_all | solution.py:32
  559.8 41.6 %all-gather.11.cloned.1.call-start = ((), (), s32[]{:S(2)}) async-start(), calls=%async_computation.13 | async-start | bytes 1114112 | tf_op jit(solution)/shard_map/all_gather | solution.py:52
  601.4 38.3 %all-to-all-start.4 = ((bf16[128,16,256]{0,2,1:T(8,128)(2,1)}), bf16[128,16,256]{0,2,1:T(8,128)(2,1)S(1)}, u32[]{:S(2)}, u32[]{:S(2)}) async-start(bf16[128,16,256]{0,2,1:T(8,128)(2,1)} %bitcast.112), calls=%async_computation.6 | async-start | bytes 2097152 | tf_op jit(solution)/shard_map/all_to_all | solution.py:155
Sparse Core Ops, SparseCore 0:
  10.3 42.0 all-gather.4
  131.8 53.6 reduce-scatter.2
  188.0 21.5 reduce-scatter.4
  377.8 37.7 all-gather.6
  418.9 36.4 all-gather.8
  562.8 38.5 all-gather.10
where the time goes:
time: 652 us; the launch traced here: 648 us
  blocking collectives  293 us (45%)
  waiting for transfers between devices  214 us (33%)
  loops' own time  37.5 us (6%)
  matrix products  33 us (5%)
  local copies, waits for them, and re-layouts  31.1 us (5%)
  starting transfers between devices  22.3 us (3%)
  between operations  14.4 us (2%)
    psum x12, blocking collectives, one_axis_at_a_time(): array = lax.psum(array, axis)  162 us
    all_to_all x4, blocking collectives, copy_for_each(): lax.all_to_all(jnp.broadcast_to(array[None], (peers, *array.shape)), axis...  131 us
    reduce_scatter x2, waiting for transfers between devices, own_rows(): so_far = lax.psum_scatter(so_far, axis, scatter_dimension=0, tiled=True)  77.7 us
    all_gather x4, waiting for transfers between devices, spread(): return lax.all_gather(piece, OUT, axis=2, tiled=True)  64.5 us
    another operation x1, loops' own time, side_terms(): return lax.map(one_group, groups).reshape(span, blocks, width)  37.5 us
    all_to_all x1, waiting for transfers between devices, copy_for_each(): lax.all_to_all(jnp.broadcast_to(array[None], (peers, *array.shape)), axis...  25.8 us
    all_to_all x1, waiting for transfers between devices, local(): lax.all_to_all(acts_whole, ('tok', 'grp'), split_axis=1, concat_axis=0, t...  24.7 us
    ppermute x1, waiting for transfers between devices, swapped(): lax.ppermute(array, axis, [(i, i ^ 1 << stride) for i in range(lax.axis_s...  20.9 us
  transfers between devices with their start and end apart: 9, of which 9 were waited for; matrix products, arithmetic and copies ran while one was open for 1% of the time, Pallas kernels for 0%

commit v1 on v0

v1 whole, which is shorter than its diff:
```python
import math

import jax
import jax.numpy as jnp
from jax import lax
from jax.sharding import Mesh
from jax.sharding import PartitionSpec as P

DAMPING = 0.1
COLUMNS = 64
SIDE_AT = (3, 0, 0, 2, 2, 1, 1, 3)
F32 = jnp.float32
BF16 = jnp.bfloat16


def split2(value):
    high = value.astype(BF16)
    low = (value - high.astype(F32)).astype(BF16)
    return high, low


def split3(value):
    high = value.astype(BF16)
    rest = value - high.astype(F32)
    middle = rest.astype(BF16)
    low = (rest - middle.astype(F32)).astype(BF16)
    return high, middle, low


def packed(rows, probe):
    return jnp.concatenate([*split2(rows), *split3(probe)], axis=0)


def unpacked(product):
    rows = product[:COLUMNS] + product[COLUMNS : 2 * COLUMNS]
    probe = product[2 * COLUMNS :]
    return rows, probe[0:1] + probe[1:2] + probe[2:3]


def by_tokens(rows, side):
    return jnp.einsum("nf,tf->nt", rows, side, preferred_element_type=F32)


def by_features(rows, side):
    return jnp.einsum("nt,tf->nf", rows, side, preferred_element_type=F32)


def whitened_columns(side, first, second):
    tokens, block = side.shape
    half = COLUMNS // 2
    row = lax.broadcasted_iota(jnp.int32, (COLUMNS, block), 0)
    wanted = jnp.where(row < half, first + row, second + row - half)
    unit = jnp.where(lax.broadcasted_iota(jnp.int32, (COLUMNS, block), 1) == wanted, 1.0, 0.0)

    def applied(rows, probe):
        return unpacked(by_tokens(packed(rows, probe), side))

    def back(rows, probe, z_rows, z_probe):
        f_rows, f_probe = unpacked(by_features(packed(z_rows, z_probe), side))
        return f_rows / tokens + DAMPING * rows, f_probe / tokens + DAMPING * probe

    ones = jnp.ones((1, block), F32)
    f1, u1 = back(unit, ones, *applied(unit, ones))
    f2, u2 = back(f1, u1, *applied(f1, u1))
    z2, zu = applied(f2, u2)
    norm = jnp.sum(u2 * u2)
    scale = (jnp.sum(zu * zu) / tokens + DAMPING * norm) / norm
    a1 = f1 / scale
    a2 = f2 / (scale * scale)
    f3 = by_features(jnp.concatenate(split2(z2), axis=0), side)
    f3 = (f3[:COLUMNS] + f3[COLUMNS:]) / tokens + DAMPING * f2
    a3 = f3 / (scale * scale * scale)

    def once(rows):
        z = by_tokens(jnp.concatenate(split2(rows), axis=0), side)
        return z[:COLUMNS] + z[COLUMNS:]

    f4 = by_features(jnp.concatenate(split2(once(a3)), axis=0), side)
    a4 = ((f4[:COLUMNS] + f4[COLUMNS:]) / tokens + DAMPING * a3) / scale
    root = (36.0 * unit - 39.0 * a1 + 27.0 * a2 - 9.0 * a3 + a4) / (16.0 * jnp.sqrt(scale))
    return once(root).astype(BF16)


def local(activations, out_grads, weight):
    tok_dev, blocks, width = activations.shape
    outs = lax.axis_size(("yl", "x", "c"))
    block = width * outs
    z, yl, x, c, yh = (lax.axis_index(a) for a in ("z", "yl", "x", "c", "yh"))
    token_count = tok_dev * lax.axis_size("z") * lax.axis_size("yh")

    pieces = [activations[:, 0], activations[:, 1], out_grads[:, 0], out_grads[:, 1]]
    mine = lax.all_to_all(jnp.stack([pieces[k] for k in SIDE_AT]), "z", 0, 0, tiled=True)
    mine = mine.reshape(8 * tok_dev, width)
    parts = lax.all_gather(mine, ("yl", "x", "c", "yh"), axis=0, tiled=False)
    side = parts.reshape(outs, 2, 8 * tok_dev, width).transpose(1, 2, 0, 3).reshape(token_count, block)

    is_act = jnp.logical_or(z % 4 == 1, z % 4 == 2)
    sub = (x * 2 + c) * 32
    act_first = ((z % 4) * 2 + yh) * 256 + sub
    act_second = (((z ^ 1) % 4) * 2 + yh) * 256 + sub
    upper = jnp.logical_or(z == 4, z == 0).astype(jnp.int32)
    grad_first = ((yl * 4 + x) * 2 + c) * width + upper * COLUMNS
    first = jnp.where(is_act, act_first, grad_first)
    second = jnp.where(is_act, act_second, grad_first + 32)
    done = whitened_columns(side, first, second)

    sent = lax.ppermute(done[32:], "z", [(1, 0), (2, 3), (5, 4), (6, 7)])
    act_part = jnp.where(is_act, done[:32], sent)
    acts = lax.all_gather(act_part, ("x", "c"), axis=0, tiled=True)
    got = {m: lax.ppermute(done, "z", [(s, s ^ m) for s in (0, 3, 4, 7)]) for m in range(1, 8)}
    slots = [jnp.where(is_act, got[m ^ 1], done if m == 0 else got[m]) for m in (0, 3, 4, 7)]
    tiles = [
        jnp.einsum("at,bt->ab", acts, slot, preferred_element_type=F32) / math.sqrt(token_count)
        for slot in slots
    ]
    base = jnp.where(is_act, z ^ 1, z)
    low_bit = base % 4 == 3
    high_bit = base >= 4
    t0, t3, t4, t7 = tiles
    t0, t3, t4, t7 = (jnp.where(low_bit, b, a) for a, b in ((t0, t3), (t3, t0), (t4, t7), (t7, t4)))
    t0, t3, t4, t7 = (jnp.where(high_bit, b, a) for a, b in ((t0, t4), (t3, t7), (t4, t0), (t7, t3)))
    update = jnp.stack(
        [jnp.concatenate([t3, t4], axis=1), jnp.concatenate([t7, t0], axis=1)], axis=1
    ).astype(BF16)

    grads_whole = lax.all_gather(out_grads, ("yl", "x", "c"), axis=2, tiled=True)
    input_grad = jnp.einsum(
        "tjq,bcjq->tbc",
        grads_whole,
        weight.reshape(blocks, width, blocks, block),
        preferred_element_type=F32,
    ).astype(BF16)
    return update, input_grad


def solution(mesh):
    split = Mesh(
        mesh.devices.reshape(mesh.shape["tok"], 2, 4, 2, mesh.shape["grp"]),
        ("z", "yl", "x", "c", "yh"),
    )
    out = ("yl", "x", "c")
    in_specs = (P(("z", "yh"), None, out), P(("z", "yh"), None, out), P(None, out, None))
    out_specs = (P(("z", "yh"), None, out), P(("z", "yh"), None, out))
    return jax.shard_map(local, mesh=split, in_specs=in_specs, out_specs=out_specs, check_vma=False)
```

time: 652 us -> 251 us (0.38)
  blocking collectives: 293 us -> 17 us
  waiting for transfers between devices: 214 us -> 125 us
  loops' own time: 37.5 us -> 0 us
  matrix products: 33 us -> 60.1 us
  local copies, waits for them, and re-layouts: 31.1 us -> 16.9 us
  starting transfers between devices: 22.3 us -> 10.8 us
    psum x12 -> x0, blocking collectives: 162 us -> none  [one_axis_at_a_time(): array = lax.psum(array, axis)]
    all_to_all x4 -> x1, blocking collectives: 131 us -> 17 us  [local(): lax.all_to_all(jnp.stack([pieces[k] for k in SIDE_AT]), 'z', 0, 0, tiled=...]
    reduce_scatter x2 -> x0, waiting for transfers between devices: 77.7 us -> none  [own_rows(): so_far = lax.psum_scatter(so_far, axis, scatter_dimension=0, tiled=True)]
    all_to_all x2 -> x0, waiting for transfers between devices: 50.5 us -> none  [the longest x1 25.8 us: copy_for_each(): lax.all_to_all(jnp.broadcast_to(array[None], (peers, *array.shape)), axis...]
    all_gather x4 -> x3, waiting for transfers between devices: 64.5 us -> 110 us  [the longest x1 93 us: local(): parts = lax.all_gather(mine, ('yl', 'x', 'c', 'yh'), axis=0, tiled=False)]
    another operation x1 -> x0, loops' own time: 37.5 us -> none  [side_terms(): return lax.map(one_group, groups).reshape(span, blocks, width)]
    dot_general x25 -> x14, matrix products: 33 us -> 60.1 us  [the longest x5 31.8 us: by_tokens(): return jnp.einsum('nf,tf->nt', rows, side, preferred_element_type=F32)]
    all_to_all x2 -> x0, starting transfers between devices: 19 us -> none  [the longest x1 10.2 us: local(): lax.all_to_all(acts_whole, ('tok', 'grp'), split_axis=1, concat_axis=0, t...]
  transfers between devices with their start and end apart: 9 -> 11, of which waited for: 9 -> 5; matrix products, arithmetic and copies ran while one was open for 1% -> 30% of each run, Pallas kernels for 0% -> 0%
where the time goes in v1:
time: 251 us; the launch traced here: 250 us
  waiting for transfers between devices  125 us (50%)
  matrix products  60.1 us (24%)
  blocking collectives  17 us (7%)
  local copies, waits for them, and re-layouts  16.9 us (7%)
  between operations  16.3 us (6%)
  starting transfers between devices  10.8 us (4%)
  other arithmetic  3.58 us (1%)
    all_gather x1, waiting for transfers between devices, local(): parts = lax.all_gather(mine, ('yl', 'x', 'c', 'yh'), axis=0, tiled=False)  93 us
    dot_general x5, matrix products, by_tokens(): return jnp.einsum('nf,tf->nt', rows, side, preferred_element_type=F32)  31.8 us
    dot_general x4, matrix products, by_features(): return jnp.einsum('nt,tf->nf', rows, side, preferred_element_type=F32)  19.5 us
    all_to_all x1, blocking collectives, local(): lax.all_to_all(jnp.stack([pieces[k] for k in SIDE_AT]), 'z', 0, 0, tiled=...  17 us
    all_gather x1, waiting for transfers between devices, local(): acts = lax.all_gather(act_part, ('x', 'c'), axis=0, tiled=True)  17 us
    transpose x1, local copies, waits for them, and re-layouts, local(): parts.reshape(outs, 2, 8 * tok_dev, width).transpose(1, 2, 0, 3)  12 us
    ppermute x7, waiting for transfers between devices, local(): lax.ppermute(done, 'z', [(s, s ^ m) for s in (0, 3, 4, 7)])  11.2 us
    ppermute x7, starting transfers between devices, local(): lax.ppermute(done, 'z', [(s, s ^ m) for s in (0, 3, 4, 7)])  7.18 us
  transfers between devices with their start and end apart: 11, of which 5 were waited for; matrix products, arithmetic and copies ran while one was open for 30% of the time, Pallas kernels for 0%

profile of v1, /device:TPU:64, one launch (start us, length us, event | category | flops | bytes accessed | tf_op | source)
XLA Modules:
  0.0 249.7 jit_solution(133291315447249740)
XLA Ops:
  9.2 17.0 %all_to_all.5 = bf16[8,128,128]{2,1,0:T(8,128)(2,1)} all-to-all(bf16[8,128,128]{2,1,0:T(8,128)(2,1)S(1)} %fusion.86), channel_id=1, replica_groups=mesh['z'=8,'yl'=2,'x'=4,'c'=2,'yh'=2] {'z'}, dimensions={0} | all-to-all | bytes 524288 | tf_op jit(solution)/shard_map/all_to_all | solution.py:92
  27.4 93.0 %all-gather.4.cloned.1.call-done = bf16[32,1024,128]{2,1,0:T(8,128)(2,1)} async-done(((bf16[1,1024,128]{2,1,0:T(8,128)(2,1)}), bf16[32,1024,128]{2,1,0:T(8,128)(2,1)}) %all-gather.4.cloned.1.call-update) | async-done | bytes 8388624 | tf_op jit(solution)/shard_map/all_gather | solution.py:94
  120.5 12.0 %copy.33 = bf16[2,1024,16,128]{3,2,1,0:T(8,128)(2,1)} copy(bf16[2,1024,16,128]{3,1,0,2:T(8,128)(2,1)} %bitcast.78) | data formatting | bytes 16777216 | tf_op jit(solution)/shard_map/transpose | solution.py:95
  132.5 6.4 %fusion.16 = f32[131,2048]{1,0:T(8,128)S(1)} fusion(bf16[64,2048]{1,0:T(8,128)(2,1)S(1)} %get-tuple-element.53, bf16[64,2048]{1,0:T(8,128)(2,1)S(1)} %get-tuple-element.52, bf16[256,8,16,128]{3,2,1,0:T(8,128)(2,1)} %bitcast.79, bf16[131]{0:T(256)(128)(2,1)S(1)} %pad.17.clone, bf16[131]{0:T(256)(128)(2,1)S(1)} %pad.16.clone), kind=kOutput, calls=%fused_computation.16 | convolution fusion | flops 1101053952 | bytes 9986572 | tf_op jit(solution)/shard_map/nf,tf->nt/dot_general | solution.py:41
  139.4 4.9 %fusion.14 = f32[131,2048]{1,0:T(8,128)S(1)} fusion(bf16[131,2048]{1,0:T(8,128)(2,1)S(1)} %concatenate.40, bf16[256,8,16,128]{3,2,1,0:T(8,128)(2,1)} %bitcast.80), kind=kOutput, calls=%fused_computation.14 | convolution fusion | flops 1098907648 | bytes 9998336 | tf_op jit(solution)/shard_map/nt,tf->nf/dot_general | solution.py:45
  144.8 6.4 %fusion.12 = f32[131,2048]{1,0:T(8,128)S(1)} fusion(bf16[131,2048]{1,0:T(8,128)(2,1)S(1)} %concatenate.41, bf16[256,8,16,128]{3,2,1,0:T(8,128)(2,1)} %bitcast.81), kind=kOutput, calls=%fused_computation.12 | convolution fusion | flops 1098907648 | bytes 9998336 | tf_op jit(solution)/shard_map/nf,tf->nt/dot_general | solution.py:41
  151.6 4.9 %fusion.10 = f32[131,2048]{1,0:T(8,128)S(1)} fusion(bf16[131,2048]{1,0:T(8,128)(2,1)S(1)} %concatenate.42, bf16[256,8,16,128]{3,2,1,0:T(8,128)(2,1)} %bitcast.82), kind=kOutput, calls=%fused_computation.10 | convolution fusion | flops 1098907648 | bytes 9998336 | tf_op jit(solution)/shard_map/nt,tf->nf/dot_general | solution.py:45
  157.8 6.4 %fusion.8 = f32[131,2048]{1,0:T(8,128)S(1)} fusion(bf16[131,2048]{1,0:T(8,128)(2,1)S(1)} %concatenate.43, bf16[256,8,16,128]{3,2,1,0:T(8,128)(2,1)} %bitcast.83), kind=kOutput, calls=%fused_computation.8 | convolution fusion | flops 1098907648 | bytes 9998336 | tf_op jit(solution)/shard_map/nf,tf->nt/dot_general | solution.py:41
  166.9 4.8 %fusion.6 = f32[128,2048]{1,0:T(8,128)S(1)} fusion(bf16[64,2048]{1,0:T(8,128)(2,1)S(1)} %get-tuple-element.19, bf16[64,2048]{1,0:T(8,128)(2,1)S(1)} %get-tuple-element.20, bf16[256,8,16,128]{3,2,1,0:T(8,128)(2,1)} %bitcast.84), kind=kOutput, calls=%fused_computation.6 | convolution fusion | flops 1074790400 | bytes 9961472 | tf_op jit(solution)/shard_map/nt,tf->nf/dot_general | solution.py:45
  171.9 6.3 %fusion.4 = f32[128,2048]{1,0:T(8,128)S(1)} fusion(bf16[64,2048]{1,0:T(8,128)(2,1)S(1)} %get-tuple-element.14, bf16[64,2048]{1,0:T(8,128)(2,1)S(1)} %get-tuple-element.15, bf16[256,8,16,128]{3,2,1,0:T(8,128)(2,1)} %bitcast.85), kind=kOutput, calls=%fused_computation.4 | convolution fusion | flops 1074790400 | bytes 9961472 | tf_op jit(solution)/shard_map/nf,tf->nt/dot_general | solution.py:41
  178.3 4.8 %fusion.2 = f32[128,2048]{1,0:T(8,128)S(1)} fusion(bf16[64,2048]{1,0:T(8,128)(2,1)S(1)} %get-tuple-element.12, bf16[64,2048]{1,0:T(8,128)(2,1)S(1)} %get-tuple-element.13, bf16[256,8,16,128]{3,2,1,0:T(8,128)(2,1)} %bitcast.86), kind=kOutput, calls=%fused_computation.2 | convolution fusion | flops 1074790400 | bytes 9961472 | tf_op jit(solution)/shard_map/nt,tf->nf/dot_general | solution.py:45
  183.5 6.4 %fusion = f32[128,2048]{1,0:T(8,128)S(1)} fusion(bf16[64,2048]{1,0:T(8,128)(2,1)S(1)} %get-tuple-element.10, bf16[64,2048]{1,0:T(8,128)(2,1)S(1)} %get-tuple-element.11, bf16[256,8,16,128]{3,2,1,0:T(8,128)(2,1)} %bitcast.87), kind=kOutput, calls=%fused_computation | convolution fusion | flops 1074790400 | bytes 9961472 | tf_op jit(solution)/shard_map/nf,tf->nt/dot_general | solution.py:41
  190.1 3.5 %collective-permute-start = (bf16[32,2048]{1,0:T(8,128)(2,1)S(1)}, bf16[32,2048]{1,0:T(8,128)(2,1)S(1)}, u32[]{:S(2)}, u32[]{:S(2)}) collective-permute-start(bf16[32,2048]{1,0:T(8,128)(2,1)S(1)} %slice.212), channel_id=1, source_target_pairs={{32,0},{64,96},{160,128},{192,224},{33,1},{65,97},{161,129},{193,2... | collective-permute-start | bytes 393224 | tf_op jit(solution)/shard_map/ppermute | solution.py:107
  193.5 3.2 %collective-permute-done = bf16[32,2048]{1,0:T(8,128)(2,1)S(1)} collective-permute-done((bf16[32,2048]{1,0:T(8,128)(2,1)S(1)}, bf16[32,2048]{1,0:T(8,128)(2,1)S(1)}, u32[]{:S(2)}, u32[]{:S(2)}) %collective-permute-start) | collective-permute-done | bytes 131104 | tf_op jit(solution)/shard_map/ppermute | solution.py:107
  198.8 2.1 fusion.24
  202.2 1.3 collective-permute-start.6
  204.2 1.3 collective-permute-start.3
  205.5 2.4 collective-permute-done.5
  208.6 17.0 %all-gather.6.cloned.1.call-done = bf16[256,2048]{1,0:T(8,128)(2,1)} async-done(((bf16[32,2048]{1,0:T(8,128)(2,1)}), bf16[256,2048]{1,0:T(8,128)(2,1)}) %all-gather.6.cloned.1.call-update) | async-done | bytes 1048592 | tf_op jit(solution)/shard_map/all_gather | solution.py:109
  225.6 1.7 convolution_multiply_fusion.1
  228.6 1.7 convolution_multiply_fusion
  230.3 1.7 convolution_multiply_fusion.2
  232.0 8.7 %collective-permute-done.1 = bf16[64,2048]{1,0:T(8,128)(2,1)S(1)} collective-permute-done((bf16[64,2048]{1,0:T(8,128)(2,1)S(1)}, bf16[64,2048]{1,0:T(8,128)(2,1)S(1)}, u32[]{:S(2)}, u32[]{:S(2)}) %collective-permute-start.1) | collective-permute-done | bytes 262176 | tf_op jit(solution)/shard_map/ppermute | solution.py:110
  240.7 1.7 select_convert_fusion.4
  (66 shorter events, 13.9 us)
Async XLA Ops:
  7.2 113.3 %all-gather.4.cloned.1.call-start = ((), (), s32[]{:S(2)}) async-start(), calls=%async_computation.1 | async-start | bytes 8650752 | tf_op jit(solution)/shard_map/all_gather | solution.py:94
  8.1 18.3 %copy-start = (bf16[128,2,128]{2,0,1:T(8,128)(2,1)}, bf16[128,2,128]{2,0,1:T(8,128)(2,1)S(1)}, u32[]{:S(2)}) copy-start(bf16[128,2,128]{2,0,1:T(8,128)(2,1)S(1)} %copy.29) | copy-start | bytes 196612
  26.3 172.5 %all-gather.8.cloned.1.call-start = ((), (), s32[]{:S(2)}) async-start(), calls=%async_computation.3 | async-start | bytes 1114112 | tf_op jit(solution)/shard_map/all_gather | solution.py:126
  27.0 198.6 %all-gather.6.cloned.1.call-start = ((), (), s32[]{:S(2)}) async-start(), calls=%async_computation.2 | async-start | bytes 1179648 | tf_op jit(solution)/shard_map/all_gather | solution.py:109
  183.5 15.2 %copy-start.1 = (bf16[2,128,4096]{2,1,0:T(8,128)(2,1)S(1)}, bf16[2,128,4096]{2,1,0:T(8,128)(2,1)}, u32[]{:S(2)}) copy-start(bf16[2,128,4096]{2,1,0:T(8,128)(2,1)} %param.5) | copy-start | bytes 6291460
  190.1 6.6 %collective-permute-start = (bf16[32,2048]{1,0:T(8,128)(2,1)S(1)}, bf16[32,2048]{1,0:T(8,128)(2,1)S(1)}, u32[]{:S(2)}, u32[]{:S(2)}) collective-permute-start(bf16[32,2048]{1,0:T(8,128)(2,1)S(1)} %slice.212), channel_id=1, source_target_pairs={{32,0},{64,96},{160,128},{192,224},{33,1},{65,97},{161,129},{193,2... | collective-permute-start | bytes 393224 | tf_op jit(solution)/shard_map/ppermute | solution.py:107
  197.4 10.5 %collective-permute-start.5 = (bf16[64,2048]{1,0:T(8,128)(2,1)S(1)}, bf16[64,2048]{1,0:T(8,128)(2,1)S(1)}, u32[]{:S(2)}, u32[]{:S(2)}) collective-permute-start(bf16[64,2048]{1,0:T(8,128)(2,1)S(1)} %fusion.40), channel_id=1, source_target_pairs={{0,32},{96,64},{128,160},{224,192},{1,33},{97,65},{129,161},{225,1... | collective-permute-start | bytes 786440 | tf_op jit(solution)/shard_map/ppermute | solution.py:110
  201.5 25.7 %collective-permute-start.7 = (bf16[64,2048]{1,0:T(8,128)(2,1)S(1)}, bf16[64,2048]{1,0:T(8,128)(2,1)S(1)}, u32[]{:S(2)}, u32[]{:S(2)}) collective-permute-start(bf16[64,2048]{1,0:T(8,128)(2,1)S(1)} %fusion.40), channel_id=1, source_target_pairs={{0,96},{96,0},{128,224},{224,128},{1,97},{97,1},{129,225},{225,129... | collective-permute-start | bytes 786440 | tf_op jit(solution)/shard_map/ppermute | solution.py:110
  202.2 26.4 %collective-permute-start.6 = (bf16[64,2048]{1,0:T(8,128)(2,1)S(1)}, bf16[64,2048]{1,0:T(8,128)(2,1)S(1)}, u32[]{:S(2)}, u32[]{:S(2)}) collective-permute-start(bf16[64,2048]{1,0:T(8,128)(2,1)S(1)} %fusion.40), channel_id=1, source_target_pairs={{0,64},{96,32},{128,192},{224,160},{1,65},{97,33},{129,193},{225,1... | collective-permute-start | bytes 786440 | tf_op jit(solution)/shard_map/ppermute | solution.py:110
  203.5 26.8 %collective-permute-start.4 = (bf16[64,2048]{1,0:T(8,128)(2,1)S(1)}, bf16[64,2048]{1,0:T(8,128)(2,1)S(1)}, u32[]{:S(2)}, u32[]{:S(2)}) collective-permute-start(bf16[64,2048]{1,0:T(8,128)(2,1)S(1)} %fusion.40), channel_id=1, source_target_pairs={{0,224},{96,128},{128,96},{224,0},{1,225},{97,129},{129,97},{225,1... | collective-permute-start | bytes 786440 | tf_op jit(solution)/shard_map/ppermute | solution.py:110
  204.2 26.1 %collective-permute-start.3 = (bf16[64,2048]{1,0:T(8,128)(2,1)S(1)}, bf16[64,2048]{1,0:T(8,128)(2,1)S(1)}, u32[]{:S(2)}, u32[]{:S(2)}) collective-permute-start(bf16[64,2048]{1,0:T(8,128)(2,1)S(1)} %fusion.40), channel_id=1, source_target_pairs={{0,192},{96,160},{128,64},{224,32},{1,193},{97,161},{129,65},{225,... | collective-permute-start | bytes 786440 | tf_op jit(solution)/shard_map/ppermute | solution.py:110
  208.0 24.0 %collective-permute-start.2 = (bf16[64,2048]{1,0:T(8,128)(2,1)S(1)}, bf16[64,2048]{1,0:T(8,128)(2,1)S(1)}, u32[]{:S(2)}, u32[]{:S(2)}) collective-permute-start(bf16[64,2048]{1,0:T(8,128)(2,1)S(1)} %fusion.40), channel_id=1, source_target_pairs={{0,128},{96,224},{128,0},{224,96},{1,129},{97,225},{129,1},{225,97... | collective-permute-start | bytes 786440 | tf_op jit(solution)/shard_map/ppermute | solution.py:110
  227.3 13.4 %collective-permute-start.1 = (bf16[64,2048]{1,0:T(8,128)(2,1)S(1)}, bf16[64,2048]{1,0:T(8,128)(2,1)S(1)}, u32[]{:S(2)}, u32[]{:S(2)}) collective-permute-start(bf16[64,2048]{1,0:T(8,128)(2,1)S(1)} %fusion.40), channel_id=1, source_target_pairs={{0,160},{96,192},{128,32},{224,64},{1,161},{97,193},{129,33},{225,... | collective-permute-start | bytes 786440 | tf_op jit(solution)/shard_map/ppermute | solution.py:110
Sparse Core Ops, SparseCore 0:
  26.4 94.0 all-gather.3
  122.8 37.6 all-gather.7
  197.5 28.0 all-gather.5

commit v2 on v1

v2 whole, which is shorter than its diff:
```python
import math

import jax
import jax.numpy as jnp
from jax import lax
from jax.experimental import pallas as pl
from jax.experimental.pallas import tpu as pltpu
from jax.sharding import Mesh
from jax.sharding import PartitionSpec as P

DAMPING = 0.1
COLUMNS = 64
TILE = 512
SIDE_AT = (3, 0, 0, 2, 2, 1, 1, 3)
F32 = jnp.float32
BF16 = jnp.bfloat16


def split2(value):
    high = value.astype(BF16)
    low = (value - high.astype(F32)).astype(BF16)
    return high, low


def split3(value):
    high = value.astype(BF16)
    rest = value - high.astype(F32)
    middle = rest.astype(BF16)
    low = (rest - middle.astype(F32)).astype(BF16)
    return high, middle, low


def chain_kernel(*refs):
    where, pieces = refs[0], refs[1:17]
    out, side, turned, now, later, unit, f1, f2, a3, u1, u2, zu, sems = refs[17:]
    block, tokens = turned.shape
    half = COLUMNS // 2
    copies = []
    for at, (source, spot) in enumerate(placed(pieces)):
        row, col = spot
        to = side.at[row : row + 512, col : col + 128]
        copies.append((pltpu.make_async_copy(source, to, sems.at[at]), row, col))
        copies[-1][0].start()

    row_id = lax.broadcasted_iota(jnp.int32, (COLUMNS, block), 0)
    wanted = jnp.where(row_id < half, where[0] + row_id, where[1] + row_id - half)
    col_id = lax.broadcasted_iota(jnp.int32, (COLUMNS, block), 1)
    unit[...] = jnp.where(col_id == wanted, 1.0, 0.0)
    now[...] = jnp.zeros_like(now)
    now[:COLUMNS] = unit[...].astype(BF16)
    now[2 * COLUMNS : 2 * COLUMNS + 16] = jnp.where(
        lax.broadcasted_iota(jnp.int32, (16, block), 0) == 0, 1.0, 0.0
    ).astype(BF16)
    later[...] = jnp.zeros_like(later)
    for copy, row, col in copies:
        copy.wait()
        turned[col : col + 128, row : row + 512] = side[row : row + 512, col : col + 128].T

    def sweep(source, matrix, use):
        def tile(at, carry):
            cols = pl.ds(pl.multiple_of(at * TILE, TILE), TILE)
            product = jnp.dot(source[...], matrix[:, cols], preferred_element_type=F32)
            rows = product[:COLUMNS] + product[COLUMNS : 2 * COLUMNS]
            probe = product[2 * COLUMNS : 2 * COLUMNS + 1]
            probe += product[2 * COLUMNS + 1 : 2 * COLUMNS + 2]
            probe += product[2 * COLUMNS + 2 : 2 * COLUMNS + 3]
            use(at, cols, rows, probe)
            return carry

        lax.fori_loop(0, matrix.shape[1] // TILE, tile, 0)

    def keep(target, cols, rows, probe=None):
        target[:COLUMNS, cols], target[COLUMNS : 2 * COLUMNS, cols] = split2(rows)
        if probe is not None:
            high, middle, low = split3(probe)
            at = lax.broadcasted_iota(jnp.int32, (16, TILE), 0)
            stacked = jnp.where(at == 0, high.astype(F32), jnp.where(at == 1, middle.astype(F32), low.astype(F32)))
            target[2 * COLUMNS : 2 * COLUMNS + 16, cols] = jnp.where(at < 3, stacked, 0.0).astype(BF16)

    def to_later(_, cols, rows, probe):
        keep(later, cols, rows, probe)

    def first_power(_, cols, rows, probe):
        rows = rows / tokens + DAMPING * unit[:, cols]
        probe = probe / tokens + DAMPING
        f1[:, cols], u1[:, cols] = rows, probe
        keep(now, cols, rows, probe)

    def second_power(_, cols, rows, probe):
        rows = rows / tokens + DAMPING * f1[:, cols]
        probe = probe / tokens + DAMPING * u1[:, cols]
        f2[:, cols], u2[:, cols] = rows, probe
        keep(now, cols, rows, probe)

    def rayleigh(_, cols, rows, probe):
        keep(later, cols, rows)
        zu[:, cols] = probe

    sweep(now, turned, to_later)
    sweep(later, side, first_power)
    sweep(now, turned, to_later)
    sweep(later, side, second_power)
    sweep(now, turned, rayleigh)
    norm = jnp.sum(u2[...] * u2[...], axis=1, keepdims=True)
    scale = (jnp.sum(zu[...] * zu[...], axis=1, keepdims=True) / tokens + DAMPING * norm) / norm
    inverse = 1.0 / scale
    inverse2 = inverse * inverse
    final = 1.0 / (16.0 * jnp.sqrt(scale))

    def third_power(_, cols, rows, probe):
        rows = (rows / tokens + DAMPING * f2[:, cols]) * (inverse2 * inverse)
        a3[:, cols] = rows
        keep(now, cols, rows)

    def root(_, cols, rows, probe):
        a4 = (rows / tokens + DAMPING * a3[:, cols]) * inverse
        rows = 36.0 * unit[:, cols] - 39.0 * (f1[:, cols] * inverse) + 27.0 * (f2[:, cols] * inverse2)
        rows = (rows - 9.0 * a3[:, cols] + a4) * final
        keep(now, cols, rows)

    def result(at, cols, rows, probe):
        spot = (at + where[2] * (tokens // TILE // 2)) % (tokens // TILE)
        out[:, pl.ds(pl.multiple_of(spot * TILE, TILE), TILE)] = rows.astype(BF16)

    sweep(later, side, third_power)
    sweep(now, turned, lambda _, cols, rows, probe: keep(later, cols, rows))
    sweep(later, side, root)
    sweep(now, turned, result)


def placed(pieces):
    for core in range(2):
        for at in range(4):
            by_y, by_x = pieces[core * 8 + at], pieces[core * 8 + 4 + at]
            for inner in range(4):
                part = pl.ds(inner * 512, 512)
                yield by_y.at[part], (at // 2 * 1024, ((at % 2) * 8 + inner * 2 + core) * 128)
                yield by_x.at[part], (inner // 2 * 1024 + 512, ((inner % 2) * 8 + at * 2 + core) * 128)


def whitened_columns(pieces, where, block, tokens):
    rows = 2 * COLUMNS + 16
    passes = 9 * 2 * rows * block * tokens
    return pl.pallas_call(
        chain_kernel,
        name="whiten",
        out_shape=jax.ShapeDtypeStruct((COLUMNS, tokens), BF16),
        in_specs=[pl.BlockSpec(memory_space=pltpu.SMEM)] + [pl.BlockSpec(memory_space=pl.ANY)] * 16,
        out_specs=pl.BlockSpec(memory_space=pltpu.VMEM),
        scratch_shapes=[
            pltpu.VMEM((tokens, block), BF16),
            pltpu.VMEM((block, tokens), BF16),
            pltpu.VMEM((rows, block), BF16),
            pltpu.VMEM((rows, tokens), BF16),
            *[pltpu.VMEM((COLUMNS, block), F32)] * 4,
            *[pltpu.VMEM((1, block), F32)] * 3,
            pltpu.SemaphoreType.DMA((64,)),
        ],
        compiler_params=pltpu.CompilerParams(vmem_limit_bytes=32 * 2**20),
        cost_estimate=pl.CostEstimate(flops=passes, bytes_accessed=2 * block * tokens, transcendentals=0),
    )(where, *pieces)


def xor_swap(array, axes, mask, order=lambda i: i, back=lambda i: i):
    count = lax.axis_size(axes)
    return lax.ppermute(array, axes, [(i, back(order(i) ^ mask)) for i in range(count)])


def y_of(i):
    return i % 2 * 2 + i // 2


def side_pieces(mine):
    lower, upper = mine[:512], mine[512:]
    masks = (1, 3, 2)
    lower_x, upper_y = {0: lower}, {0: upper}
    for m in masks:
        lower_x[m] = xor_swap(lower, "x", m)
        upper_y[m] = xor_swap(upper, ("yl", "yh"), m, y_of, y_of)
    by_y = {0: jnp.concatenate([lower_x[m] for m in range(4)])}
    by_x = {0: jnp.concatenate([upper_y[m] for m in range(4)])}
    for m in masks:
        by_y[m] = xor_swap(by_y[0], ("yl", "yh"), m, y_of, y_of)
        by_x[m] = xor_swap(by_x[0], "x", m)
    own = [by_y[m] for m in range(4)] + [by_x[m] for m in range(4)]
    return own + [xor_swap(piece, "c", 1) for piece in own]


def local(activations, out_grads, weight):
    tok_dev, blocks, width = activations.shape
    outs = lax.axis_size(("yl", "x", "c"))
    block = width * outs
    z, yl, x, c, yh = (lax.axis_index(a) for a in ("z", "yl", "x", "c", "yh"))
    token_count = tok_dev * lax.axis_size("z") * lax.axis_size("yh")

    pieces = [activations[:, 0], activations[:, 1], out_grads[:, 0], out_grads[:, 1]]
    mine = lax.all_to_all(jnp.stack([pieces[k] for k in SIDE_AT]), "z", 0, 0, tiled=True)
    mine = mine.reshape(8 * tok_dev, width)
    pieces = side_pieces(mine)

    is_act = jnp.logical_or(z % 4 == 1, z % 4 == 2)
    sub = (x * 2 + c) * 32
    act_first = ((z % 4) * 2 + yh) * 256 + sub
    act_second = (((z ^ 1) % 4) * 2 + yh) * 256 + sub
    upper = jnp.logical_or(z == 4, z == 0).astype(jnp.int32)

    def relative(column):
        place = column // width
        return (((place // 8) ^ yl) * 8 + ((place // 2 % 4) ^ x) * 2 + ((place % 2) ^ c)) * width + column % width

    first = jnp.where(is_act, relative(act_first), upper * COLUMNS)
    second = jnp.where(is_act, relative(act_second), upper * COLUMNS + 32)
    done = whitened_columns(pieces, jnp.stack([first, second, yh]), block, token_count)

    sent = lax.ppermute(done[32:], "z", [(1, 0), (2, 3), (5, 4), (6, 7)])
    act_part = jnp.where(is_act, done[:32], sent)
    acts = lax.all_gather(act_part, ("x", "c"), axis=0, tiled=True)
    got = {m: lax.ppermute(done, "z", [(s, s ^ m) for s in (0, 3, 4, 7)]) for m in range(1, 8)}
    slots = [jnp.where(is_act, got[m ^ 1], done if m == 0 else got[m]) for m in (0, 3, 4, 7)]
    tiles = [
        jnp.einsum("at,bt->ab", acts, slot, preferred_element_type=F32) / math.sqrt(token_count)
        for slot in slots
    ]
    base = jnp.where(is_act, z ^ 1, z)
    low_bit = base % 4 == 3
    high_bit = base >= 4
    t0, t3, t4, t7 = tiles
    t0, t3, t4, t7 = (jnp.where(low_bit, b, a) for a, b in ((t0, t3), (t3, t0), (t4, t7), (t7, t4)))
    t0, t3, t4, t7 = (jnp.where(high_bit, b, a) for a, b in ((t0, t4), (t3, t7), (t4, t0), (t7, t3)))
    update = jnp.stack(
        [jnp.concatenate([t3, t4], axis=1), jnp.concatenate([t7, t0], axis=1)], axis=1
    ).astype(BF16)

    late_grads, _ = lax.optimization_barrier((out_grads, pieces[4]))
    grads_whole = lax.all_gather(late_grads, ("yl", "x", "c"), axis=2, tiled=True)
    input_grad = jnp.einsum(
        "tjq,bcjq->tbc",
        grads_whole,
        weight.reshape(blocks, width, blocks, block),
        preferred_element_type=F32,
    ).astype(BF16)
    return update, input_grad


def solution(mesh):
    split = Mesh(
        mesh.devices.reshape(mesh.shape["tok"], 2, 4, 2, mesh.shape["grp"]),
        ("z", "yl", "x", "c", "yh"),
    )
    out = ("yl", "x", "c")
    in_specs = (P(("z", "yh"), None, out), P(("z", "yh"), None, out), P(None, out, None))
    out_specs = (P(("z", "yh"), None, out), P(("z", "yh"), None, out))
    return jax.shard_map(local, mesh=split, in_specs=in_specs, out_specs=out_specs, check_vma=False)
```

time: 251 us -> 194 us (0.77)
  the two profiles are of different devices: /device:TPU:64 before, /device:TPU:24 now
where the time goes in v2:
time: 194 us; the launch traced here: 193 us
  waiting for transfers between devices  70.7 us (36%)
  starting transfers between devices  45 us (23%)
  Pallas kernels  26.8 us (14%)
  blocking collectives  20.1 us (10%)
  between operations  14.6 us (8%)
  local copies, waits for them, and re-layouts  8.02 us (4%)
  matrix products  7.08 us (4%)
    ppermute x20, waiting for transfers between devices, xor_swap(): lax.ppermute(array, axes, [(i, back(order(i) ^ mask)) for i in range(coun...  50.4 us
    pallas_call x1, Pallas kernels, whitened_columns(): pl.pallas_call(chain_kernel, name='whiten', out_shape=jax.ShapeDtypeStruc...  26.8 us
    ppermute x7, starting transfers between devices, local(): lax.ppermute(done, 'z', [(s, s ^ m) for s in (0, 3, 4, 7)])  24.3 us
    all_to_all x1, blocking collectives, local(): lax.all_to_all(jnp.stack([pieces[k] for k in SIDE_AT]), 'z', 0, 0, tiled=...  20.1 us
    ppermute x20, starting transfers between devices, xor_swap(): lax.ppermute(array, axes, [(i, back(order(i) ^ mask)) for i in range(coun...  19.2 us
    ppermute x7, waiting for transfers between devices, local(): lax.ppermute(done, 'z', [(s, s ^ m) for s in (0, 3, 4, 7)])  14.1 us
    ppermute x1, waiting for transfers between devices, local(): sent = lax.ppermute(done[32:], 'z', [(1, 0), (2, 3), (5, 4), (6, 7)])  6.14 us
    unnamed x21, local copies, waits for them, and re-layouts  5.27 us
  transfers between devices with their start and end apart: 30, of which 11 were waited for; matrix products, arithmetic and copies ran while one was open for 5% of the time, Pallas kernels for 14%

profile of v2, /device:TPU:24, one launch (start us, length us, event | category | flops | bytes accessed | tf_op | source)
XLA Modules:
  0.0 193.2 jit_solution(2208823867498727946)
XLA Ops:
  9.4 20.1 %all_to_all.5 = bf16[8,128,128]{2,1,0:T(8,128)(2,1)S(1)} all-to-all(bf16[8,128,128]{2,1,0:T(8,128)(2,1)S(1)} %constant_dynamic-update-slice_fusion), channel_id=1, replica_groups=mesh['z'=8,'yl'=2,'x'=4,'c'=2,'yh'=2] {'z'}, dimensions={0} | all-to-all | bytes 524288 | tf_op jit(solution)/shard_map/all_to_all | solution.py:197
  31.4 3.0 %collective-permute-start.8 = (bf16[512,128]{1,0:T(8,128)(2,1)S(1)}, bf16[512,128]{1,0:T(8,128)(2,1)S(1)}, u32[]{:S(2)}, u32[]{:S(2)}) collective-permute-start(bf16[512,128]{1,0:T(8,128)(2,1)S(1)} %bitcast.59), channel_id=1, source_target_pairs={{0,17},{1,16},{16,1},{17,0},{2,19},{3,18},{18,3},{19,2},{4,21},{5,... | collective-permute-start | bytes 393224 | tf_op jit(solution)/shard_map/ppermute | solution.py:166
  38.4 1.6 collective-permute-start.9
  39.9 2.7 %collective-permute-start.10 = (bf16[2048,128]{1,0:T(8,128)(2,1)S(1)}, bf16[2048,128]{1,0:T(8,128)(2,1)S(1)}, u32[]{:S(2)}, u32[]{:S(2)}) collective-permute-start(bf16[2048,128]{1,0:T(8,128)(2,1)S(1)} %pad_maximum_fusion.1.refs_5_), channel_id=1, source_target_pairs={{0,8},{4,12},{8,0},{12,4},{1,9},{5,13},{9,1},{13,5},{2,10},{6,14},... | collective-permute-start | bytes 1572872 | tf_op jit(solution)/shard_map/ppermute | solution.py:166
  43.1 1.8 collective-permute-start.1
  45.0 21.7 %collective-permute-done.1 = bf16[512,128]{1,0:T(8,128)(2,1)S(1)} collective-permute-done((bf16[512,128]{1,0:T(8,128)(2,1)S(1)}, bf16[512,128]{1,0:T(8,128)(2,1)S(1)}, u32[]{:S(2)}, u32[]{:S(2)}) %collective-permute-start.1) | collective-permute-done | bytes 131104 | tf_op jit(solution)/shard_map/ppermute | solution.py:166
  67.1 5.7 %collective-permute-done.2 = bf16[512,128]{1,0:T(8,128)(2,1)S(1)} collective-permute-done((bf16[512,128]{1,0:T(8,128)(2,1)S(1)}, bf16[512,128]{1,0:T(8,128)(2,1)S(1)}, u32[]{:S(2)}, u32[]{:S(2)}) %collective-permute-start.2) | collective-permute-done | bytes 131104 | tf_op jit(solution)/shard_map/ppermute | solution.py:166
  73.0 2.1 %collective-permute-start.4 = (bf16[2048,128]{1,0:T(8,128)(2,1)S(1)}, bf16[2048,128]{1,0:T(8,128)(2,1)}, u32[]{:S(2)}, u32[]{:S(2)}) collective-permute-start(bf16[2048,128]{1,0:T(8,128)(2,1)S(1)} %pad_maximum_fusion.refs_1_), channel_id=1, source_target_pairs={{0,1},{1,0},{16,17},{17,16},{2,3},{3,2},{18,19},{19,18},{4,5},{5,4... | collective-permute-start | bytes 1572872 | tf_op jit(solution)/shard_map/ppermute | solution.py:166
  75.1 2.5 %collective-permute-start.5 = (bf16[2048,128]{1,0:T(8,128)(2,1)S(1)}, bf16[2048,128]{1,0:T(8,128)(2,1)}, u32[]{:S(2)}, u32[]{:S(2)}) collective-permute-start(bf16[2048,128]{1,0:T(8,128)(2,1)S(1)} %pad_maximum_fusion.refs_1_), channel_id=1, source_target_pairs={{0,17},{1,16},{16,1},{17,0},{2,19},{3,18},{18,3},{19,2},{4,21},{5,... | collective-permute-start | bytes 1572872 | tf_op jit(solution)/shard_map/ppermute | solution.py:166
  78.2 9.7 %collective-permute-done.3.refs_2_ = bf16[2048,128]{1,0:T(8,128)(2,1)} collective-permute-done((bf16[2048,128]{1,0:T(8,128)(2,1)S(1)}, bf16[2048,128]{1,0:T(8,128)(2,1)}, u32[]{:S(2)}, u32[]{:S(2)}) %collective-permute-start.3) | collective-permute-done | bytes 524320 | tf_op jit(solution)/shard_map/ppermute | solution.py:166
  87.9 7.2 %collective-permute-done.4.refs_3_ = bf16[2048,128]{1,0:T(8,128)(2,1)} collective-permute-done((bf16[2048,128]{1,0:T(8,128)(2,1)S(1)}, bf16[2048,128]{1,0:T(8,128)(2,1)}, u32[]{:S(2)}, u32[]{:S(2)}) %collective-permute-start.4) | collective-permute-done | bytes 524320 | tf_op jit(solution)/shard_map/ppermute | solution.py:166
  95.2 2.6 %collective-permute-done.5.refs_4_ = bf16[2048,128]{1,0:T(8,128)(2,1)} collective-permute-done((bf16[2048,128]{1,0:T(8,128)(2,1)S(1)}, bf16[2048,128]{1,0:T(8,128)(2,1)}, u32[]{:S(2)}, u32[]{:S(2)}) %collective-permute-start.5) | collective-permute-done | bytes 524320 | tf_op jit(solution)/shard_map/ppermute | solution.py:166
  104.2 26.8 %whiten.1 = bf16[64,2048]{1,0:T(8,128)(2,1)S(1)} custom-call(s32[3]{0:T(128)S(1)} %pad_add_fusion.refs_0_, bf16[2048,128]{1,0:T(8,128)(2,1)S(1)} %pad_maximum_fusion.refs_1_, bf16[2048,128]{1,0:T(8,128)(2,1)} %collective-permute-done.3.refs_2_, bf16[2048,128]{1,0:T(8,128)(2,1)} %collective-permute-done.4.refs_3_, ...), custom_call_target="tpu_custom_call" | custom-call | flops 10871635968 | bytes 8388608 | tf_op jit(solution)/shard_map/whiten/pallas_call | solution.py:144
  132.3 6.1 %collective-permute-done.20 = bf16[32,2048]{1,0:T(8,128)(2,1)S(1)} collective-permute-done((bf16[32,2048]{1,0:T(8,128)(2,1)S(1)}, bf16[32,2048]{1,0:T(8,128)(2,1)S(1)}, u32[]{:S(2)}, u32[]{:S(2)}) %collective-permute-start.20) | collective-permute-done | bytes 131104 | tf_op jit(solution)/shard_map/ppermute | solution.py:215
  139.2 3.8 %collective-permute-start.26 = (bf16[64,2048]{1,0:T(8,128)(2,1)S(1)}, bf16[64,2048]{1,0:T(8,128)(2,1)S(1)}, u32[]{:S(2)}, u32[]{:S(2)}) collective-permute-start(bf16[64,2048]{1,0:T(8,128)(2,1)S(1)} %whiten.1), channel_id=1, source_target_pairs={{0,64},{96,32},{128,192},{224,160},{1,65},{97,33},{129,193},{225,1... | collective-permute-start | bytes 786440 | tf_op jit(solution)/shard_map/ppermute | solution.py:218
  143.0 3.2 %collective-permute-start.27 = (bf16[64,2048]{1,0:T(8,128)(2,1)S(1)}, bf16[64,2048]{1,0:T(8,128)(2,1)S(1)}, u32[]{:S(2)}, u32[]{:S(2)}) collective-permute-start(bf16[64,2048]{1,0:T(8,128)(2,1)S(1)} %whiten.1), channel_id=1, source_target_pairs={{0,96},{96,0},{128,224},{224,128},{1,97},{97,1},{129,225},{225,129... | collective-permute-start | bytes 786440 | tf_op jit(solution)/shard_map/ppermute | solution.py:218
  148.9 3.8 %collective-permute-start.24 = (bf16[64,2048]{1,0:T(8,128)(2,1)S(1)}, bf16[64,2048]{1,0:T(8,128)(2,1)S(1)}, u32[]{:S(2)}, u32[]{:S(2)}) collective-permute-start(bf16[64,2048]{1,0:T(8,128)(2,1)S(1)} %whiten.1), channel_id=1, source_target_pairs={{0,224},{96,128},{128,96},{224,0},{1,225},{97,129},{129,97},{225,1... | collective-permute-start | bytes 786440 | tf_op jit(solution)/shard_map/ppermute | solution.py:218
  152.7 2.8 %fusion.6 = bf16[128,2,128]{2,0,1:T(8,128)(2,1)S(1)} fusion(bf16[2,16,2,8,2048]{4,3,2,1,0:T(8,128)(2,1)} %bitcast.61, bf16[128,2,2048]{2,0,1:T(8,128)(2,1)} %all-gather.5.cloned.1.call-done), kind=kOutput, calls=%fused_computation.4 | convolution fusion | flops 268468224 | bytes 3211264 | tf_op jit(solution)/shard_map/tjq,bcjq->tbc/dot_general | solution.py:236
  156.2 8.7 %collective-permute-done.25 = bf16[64,2048]{1,0:T(8,128)(2,1)S(1)} collective-permute-done((bf16[64,2048]{1,0:T(8,128)(2,1)S(1)}, bf16[64,2048]{1,0:T(8,128)(2,1)S(1)}, u32[]{:S(2)}, u32[]{:S(2)}) %collective-permute-start.25) | collective-permute-done | bytes 262176 | tf_op jit(solution)/shard_map/ppermute | solution.py:218
  164.9 5.9 %collective-permute-start.21 = (bf16[64,2048]{1,0:T(8,128)(2,1)S(1)}, bf16[64,2048]{1,0:T(8,128)(2,1)S(1)}, u32[]{:S(2)}, u32[]{:S(2)}) collective-permute-start(bf16[64,2048]{1,0:T(8,128)(2,1)S(1)} %whiten.1), channel_id=1, source_target_pairs={{0,160},{96,192},{128,32},{224,64},{1,161},{97,193},{129,33},{225,... | collective-permute-start | bytes 786440 | tf_op jit(solution)/shard_map/ppermute | solution.py:218
  170.8 1.8 convolution_multiply_fusion.1
  172.6 4.9 %collective-permute-start.22 = (bf16[64,2048]{1,0:T(8,128)(2,1)S(1)}, bf16[64,2048]{1,0:T(8,128)(2,1)S(1)}, u32[]{:S(2)}, u32[]{:S(2)}) collective-permute-start(bf16[64,2048]{1,0:T(8,128)(2,1)S(1)} %whiten.1), channel_id=1, source_target_pairs={{0,128},{96,224},{128,0},{224,96},{1,129},{97,225},{129,1},{225,97... | collective-permute-start | bytes 786440 | tf_op jit(solution)/shard_map/ppermute | solution.py:218
  177.5 1.7 convolution_multiply_fusion
  179.6 5.5 %collective-permute-done.22 = bf16[64,2048]{1,0:T(8,128)(2,1)S(1)} collective-permute-done((bf16[64,2048]{1,0:T(8,128)(2,1)S(1)}, bf16[64,2048]{1,0:T(8,128)(2,1)S(1)}, u32[]{:S(2)}, u32[]{:S(2)}) %collective-permute-start.22) | collective-permute-done | bytes 262176 | tf_op jit(solution)/shard_map/ppermute | solution.py:218
  (78 shorter events, 22.8 us)
Async XLA Ops:
  7.2 145.6 %all-gather.5.cloned.1.call-start = ((), (), s32[]{:S(2)}) async-start(), calls=%async_computation.2 | async-start | bytes 1114112 | tf_op jit(solution)/shard_map/all_gather | solution.py:235
  30.4 6.5 %collective-permute-start.7 = (bf16[512,128]{1,0:T(8,128)(2,1)S(1)}, bf16[512,128]{1,0:T(8,128)(2,1)S(1)}, u32[]{:S(2)}, u32[]{:S(2)}) collective-permute-start(bf16[512,128]{1,0:T(8,128)(2,1)S(1)} %bitcast.58), channel_id=1, source_target_pairs={{0,1},{1,0},{16,17},{17,16},{2,3},{3,2},{18,19},{19,18},{4,5},{5,4... | collective-permute-start | bytes 393224 | tf_op jit(solution)/shard_map/ppermute | solution.py:166
  31.4 6.9 %collective-permute-start.8 = (bf16[512,128]{1,0:T(8,128)(2,1)S(1)}, bf16[512,128]{1,0:T(8,128)(2,1)S(1)}, u32[]{:S(2)}, u32[]{:S(2)}) collective-permute-start(bf16[512,128]{1,0:T(8,128)(2,1)S(1)} %bitcast.59), channel_id=1, source_target_pairs={{0,17},{1,16},{16,1},{17,0},{2,19},{3,18},{18,3},{19,2},{4,21},{5,... | collective-permute-start | bytes 393224 | tf_op jit(solution)/shard_map/ppermute | solution.py:166
  34.4 8.8 %collective-permute-start = (bf16[512,128]{1,0:T(8,128)(2,1)S(1)}, bf16[512,128]{1,0:T(8,128)(2,1)S(1)}, u32[]{:S(2)}, u32[]{:S(2)}) collective-permute-start(bf16[512,128]{1,0:T(8,128)(2,1)S(1)} %bitcast.53), channel_id=1, source_target_pairs={{0,4},{4,0},{8,12},{12,8},{1,5},{5,1},{9,13},{13,9},{2,6},{6,2},{1... | collective-permute-start | bytes 393224 | tf_op jit(solution)/shard_map/ppermute | solution.py:166
  38.4 34.6 %collective-permute-start.9 = (bf16[2048,128]{1,0:T(8,128)(2,1)S(1)}, bf16[2048,128]{1,0:T(8,128)(2,1)S(1)}, u32[]{:S(2)}, u32[]{:S(2)}) collective-permute-start(bf16[2048,128]{1,0:T(8,128)(2,1)S(1)} %pad_maximum_fusion.1.refs_5_), channel_id=1, source_target_pairs={{0,4},{4,0},{8,12},{12,8},{1,5},{5,1},{9,13},{13,9},{2,6},{6,2},{1... | collective-permute-start | bytes 1572872 | tf_op jit(solution)/shard_map/ppermute | solution.py:166
  39.9 35.2 %collective-permute-start.10 = (bf16[2048,128]{1,0:T(8,128)(2,1)S(1)}, bf16[2048,128]{1,0:T(8,128)(2,1)S(1)}, u32[]{:S(2)}, u32[]{:S(2)}) collective-permute-start(bf16[2048,128]{1,0:T(8,128)(2,1)S(1)} %pad_maximum_fusion.1.refs_5_), channel_id=1, source_target_pairs={{0,8},{4,12},{8,0},{12,4},{1,9},{5,13},{9,1},{13,5},{2,10},{6,14},... | collective-permute-start | bytes 1572872 | tf_op jit(solution)/shard_map/ppermute | solution.py:166
  42.7 35.0 %collective-permute-start.11 = (bf16[2048,128]{1,0:T(8,128)(2,1)S(1)}, bf16[2048,128]{1,0:T(8,128)(2,1)S(1)}, u32[]{:S(2)}, u32[]{:S(2)}) collective-permute-start(bf16[2048,128]{1,0:T(8,128)(2,1)S(1)} %pad_maximum_fusion.1.refs_5_), channel_id=1, source_target_pairs={{0,12},{4,8},{8,4},{12,0},{1,13},{5,9},{9,5},{13,1},{2,14},{6,10},... | collective-permute-start | bytes 1572872 | tf_op jit(solution)/shard_map/ppermute | solution.py:166
  43.1 34.5 %collective-permute-start.16 = (bf16[2048,128]{1,0:T(8,128)(2,1)S(1)}, bf16[2048,128]{1,0:T(8,128)(2,1)S(1)}, u32[]{:S(2)}, u32[]{:S(2)}) collective-permute-start(bf16[2048,128]{1,0:T(8,128)(2,1)S(1)} %pad_maximum_fusion.1.refs_5_), channel_id=1, source_target_pairs={{0,2},{2,0},{1,3},{3,1},{4,6},{6,4},{5,7},{7,5},{8,10},{10,8},{9,1... | collective-permute-start | bytes 1572872 | tf_op jit(solution)/shard_map/ppermute | solution.py:166
  43.1 23.5 %collective-permute-start.1 = (bf16[512,128]{1,0:T(8,128)(2,1)S(1)}, bf16[512,128]{1,0:T(8,128)(2,1)S(1)}, u32[]{:S(2)}, u32[]{:S(2)}) collective-permute-start(bf16[512,128]{1,0:T(8,128)(2,1)S(1)} %bitcast.54), channel_id=1, source_target_pairs={{0,8},{4,12},{8,0},{12,4},{1,9},{5,13},{9,1},{13,5},{2,10},{6,14},... | collective-permute-start | bytes 393224 | tf_op jit(solution)/shard_map/ppermute | solution.py:166
  72.9 15.1 %collective-permute-start.3 = (bf16[2048,128]{1,0:T(8,128)(2,1)S(1)}, bf16[2048,128]{1,0:T(8,128)(2,1)}, u32[]{:S(2)}, u32[]{:S(2)}) collective-permute-start(bf16[2048,128]{1,0:T(8,128)(2,1)S(1)} %pad_maximum_fusion.refs_1_), channel_id=1, source_target_pairs={{0,16},{1,17},{16,0},{17,1},{2,18},{3,19},{18,2},{19,3},{4,20},{5,... | collective-permute-start | bytes 1572872 | tf_op jit(solution)/shard_map/ppermute | solution.py:166
  73.0 22.2 %collective-permute-start.4 = (bf16[2048,128]{1,0:T(8,128)(2,1)S(1)}, bf16[2048,128]{1,0:T(8,128)(2,1)}, u32[]{:S(2)}, u32[]{:S(2)}) collective-permute-start(bf16[2048,128]{1,0:T(8,128)(2,1)S(1)} %pad_maximum_fusion.refs_1_), channel_id=1, source_target_pairs={{0,1},{1,0},{16,17},{17,16},{2,3},{3,2},{18,19},{19,18},{4,5},{5,4... | collective-permute-start | bytes 1572872 | tf_op jit(solution)/shard_map/ppermute | solution.py:166
  75.1 22.6 %collective-permute-start.5 = (bf16[2048,128]{1,0:T(8,128)(2,1)S(1)}, bf16[2048,128]{1,0:T(8,128)(2,1)}, u32[]{:S(2)}, u32[]{:S(2)}) collective-permute-start(bf16[2048,128]{1,0:T(8,128)(2,1)S(1)} %pad_maximum_fusion.refs_1_), channel_id=1, source_target_pairs={{0,17},{1,16},{16,1},{17,0},{2,19},{3,18},{18,3},{19,2},{4,21},{5,... | collective-permute-start | bytes 1572872 | tf_op jit(solution)/shard_map/ppermute | solution.py:166
  77.7 20.1 %collective-permute-start.12 = (bf16[2048,128]{1,0:T(8,128)(2,1)S(1)}, bf16[2048,128]{1,0:T(8,128)(2,1)S(1)}, u32[]{:S(2)}, u32[]{:S(2)}) collective-permute-start(bf16[2048,128]{1,0:T(8,128)(2,1)S(1)} %pad_maximum_fusion.refs_1_), channel_id=1, source_target_pairs={{0,2},{2,0},{1,3},{3,1},{4,6},{6,4},{5,7},{7,5},{8,10},{10,8},{9,1... | collective-permute-start | bytes 1572872 | tf_op jit(solution)/shard_map/ppermute | solution.py:166
  77.7 21.4 %collective-permute-start.17 = (bf16[2048,128]{1,0:T(8,128)(2,1)S(1)}, bf16[2048,128]{1,0:T(8,128)(2,1)S(1)}, u32[]{:S(2)}, u32[]{:S(2)}) collective-permute-start(bf16[2048,128]{1,0:T(8,128)(2,1)S(1)} %collective-permute-done.9.refs_6_), channel_id=1, source_target_pairs={{0,2},{2,0},{1,3},{3,1},{4,6},{6,4},{5,7},{7,5},{8,10},{10,8},{9,1... | collective-permute-start | bytes 1572872 | tf_op jit(solution)/shard_map/ppermute | solution.py:166
  87.9 13.2 %collective-permute-start.18 = (bf16[2048,128]{1,0:T(8,128)(2,1)S(1)}, bf16[2048,128]{1,0:T(8,128)(2,1)}, u32[]{:S(2)}, u32[]{:S(2)}) collective-permute-start(bf16[2048,128]{1,0:T(8,128)(2,1)S(1)} %collective-permute-done.10.refs_7_), channel_id=1, source_target_pairs={{0,2},{2,0},{1,3},{3,1},{4,6},{6,4},{5,7},{7,5},{8,10},{10,8},{9,1... | collective-permute-start | bytes 1572872 | tf_op jit(solution)/shard_map/ppermute | solution.py:166
  100.5 70.3 %all-gather.3.cloned.1.call-start = ((), (), s32[]{:S(2)}) async-start(), calls=%async_computation.1 | async-start | bytes 1179648 | tf_op jit(solution)/shard_map/all_gather | solution.py:217
  131.0 7.4 %collective-permute-start.20 = (bf16[32,2048]{1,0:T(8,128)(2,1)S(1)}, bf16[32,2048]{1,0:T(8,128)(2,1)S(1)}, u32[]{:S(2)}, u32[]{:S(2)}) collective-permute-start(bf16[32,2048]{1,0:T(8,128)(2,1)S(1)} %slice.43), channel_id=1, source_target_pairs={{32,0},{64,96},{160,128},{192,224},{33,1},{65,97},{161,129},{193,2... | collective-permute-start | bytes 393224 | tf_op jit(solution)/shard_map/ppermute | solution.py:215
  139.2 33.4 %collective-permute-start.26 = (bf16[64,2048]{1,0:T(8,128)(2,1)S(1)}, bf16[64,2048]{1,0:T(8,128)(2,1)S(1)}, u32[]{:S(2)}, u32[]{:S(2)}) collective-permute-start(bf16[64,2048]{1,0:T(8,128)(2,1)S(1)} %whiten.1), channel_id=1, source_target_pairs={{0,64},{96,32},{128,192},{224,160},{1,65},{97,33},{129,193},{225,1... | collective-permute-start | bytes 786440 | tf_op jit(solution)/shard_map/ppermute | solution.py:218
  143.0 34.5 %collective-permute-start.27 = (bf16[64,2048]{1,0:T(8,128)(2,1)S(1)}, bf16[64,2048]{1,0:T(8,128)(2,1)S(1)}, u32[]{:S(2)}, u32[]{:S(2)}) collective-permute-start(bf16[64,2048]{1,0:T(8,128)(2,1)S(1)} %whiten.1), channel_id=1, source_target_pairs={{0,96},{96,0},{128,224},{224,128},{1,97},{97,1},{129,225},{225,129... | collective-permute-start | bytes 786440 | tf_op jit(solution)/shard_map/ppermute | solution.py:218
  146.2 18.6 %collective-permute-start.25 = (bf16[64,2048]{1,0:T(8,128)(2,1)S(1)}, bf16[64,2048]{1,0:T(8,128)(2,1)S(1)}, u32[]{:S(2)}, u32[]{:S(2)}) collective-permute-start(bf16[64,2048]{1,0:T(8,128)(2,1)S(1)} %whiten.1), channel_id=1, source_target_pairs={{0,32},{96,64},{128,160},{224,192},{1,33},{97,65},{129,161},{225,1... | collective-permute-start | bytes 786440 | tf_op jit(solution)/shard_map/ppermute | solution.py:218
  147.5 31.6 %collective-permute-start.23 = (bf16[64,2048]{1,0:T(8,128)(2,1)S(1)}, bf16[64,2048]{1,0:T(8,128)(2,1)S(1)}, u32[]{:S(2)}, u32[]{:S(2)}) collective-permute-start(bf16[64,2048]{1,0:T(8,128)(2,1)S(1)} %whiten.1), channel_id=1, source_target_pairs={{0,192},{96,160},{128,64},{224,32},{1,193},{97,161},{129,65},{225,... | collective-permute-start | bytes 786440 | tf_op jit(solution)/shard_map/ppermute | solution.py:218
  148.9 30.3 %collective-permute-start.24 = (bf16[64,2048]{1,0:T(8,128)(2,1)S(1)}, bf16[64,2048]{1,0:T(8,128)(2,1)S(1)}, u32[]{:S(2)}, u32[]{:S(2)}) collective-permute-start(bf16[64,2048]{1,0:T(8,128)(2,1)S(1)} %whiten.1), channel_id=1, source_target_pairs={{0,224},{96,128},{128,96},{224,0},{1,225},{97,129},{129,97},{225,1... | collective-permute-start | bytes 786440 | tf_op jit(solution)/shard_map/ppermute | solution.py:218
  164.9 14.8 %collective-permute-start.21 = (bf16[64,2048]{1,0:T(8,128)(2,1)S(1)}, bf16[64,2048]{1,0:T(8,128)(2,1)S(1)}, u32[]{:S(2)}, u32[]{:S(2)}) collective-permute-start(bf16[64,2048]{1,0:T(8,128)(2,1)S(1)} %whiten.1), channel_id=1, source_target_pairs={{0,160},{96,192},{128,32},{224,64},{1,161},{97,193},{129,33},{225,... | collective-permute-start | bytes 786440 | tf_op jit(solution)/shard_map/ppermute | solution.py:218
  172.6 12.5 %collective-permute-start.22 = (bf16[64,2048]{1,0:T(8,128)(2,1)S(1)}, bf16[64,2048]{1,0:T(8,128)(2,1)S(1)}, u32[]{:S(2)}, u32[]{:S(2)}) collective-permute-start(bf16[64,2048]{1,0:T(8,128)(2,1)S(1)} %whiten.1), channel_id=1, source_target_pairs={{0,128},{96,224},{128,0},{224,96},{1,129},{97,225},{129,1},{225,97... | collective-permute-start | bytes 786440 | tf_op jit(solution)/shard_map/ppermute | solution.py:218
  (12 other events, 130.2 us)
Sparse Core Ops, SparseCore 0:
  100.7 34.4 all-gather.4
  139.3 24.3 all-gather.2

commit v3 on v2

--- a/solution.py
+++ b/solution.py
@@ -31,15 +31,15 @@
 
 
 def chain_kernel(*refs):
-    where, pieces = refs[0], refs[1:17]
-    out, side, turned, now, later, unit, f1, f2, a3, u1, u2, zu, sems = refs[17:]
+    where, pieces = refs[0], refs[1:9]
+    out, side, turned, now, later, unit, f1, f2, a3, u1, u2, zu, sems = refs[9:]
     block, tokens = turned.shape
     half = COLUMNS // 2
     copies = []
-    for at, (source, spot) in enumerate(placed(pieces)):
-        row, col = spot
-        to = side.at[row : row + 512, col : col + 128]
-        copies.append((pltpu.make_async_copy(source, to, sems.at[at]), row, col))
+    for source, row, col in placed(pieces, where[3] == 0):
+        row, col = pl.multiple_of(row, 512), pl.multiple_of(col, 128)
+        to = side.at[pl.ds(row, 512), pl.ds(col, 128)]
+        copies.append((pltpu.make_async_copy(source, to, sems.at[len(copies)]), row, col))
         copies[-1][0].start()
 
     row_id = lax.broadcasted_iota(jnp.int32, (COLUMNS, block), 0)
@@ -54,7 +54,7 @@
     later[...] = jnp.zeros_like(later)
     for copy, row, col in copies:
         copy.wait()
-        turned[col : col + 128, row : row + 512] = side[row : row + 512, col : col + 128].T
+        turned[pl.ds(col, 128), pl.ds(row, 512)] = side[pl.ds(row, 512), pl.ds(col, 128)].T
 
     def sweep(source, matrix, use):
         def tile(at, carry):
@@ -119,7 +119,7 @@
         keep(now, cols, rows)
 
     def result(at, cols, rows, probe):
-        spot = (at + where[2] * (tokens // TILE // 2)) % (tokens // TILE)
+        spot = at ^ where[2]
         out[:, pl.ds(pl.multiple_of(spot * TILE, TILE), TILE)] = rows.astype(BF16)
 
     sweep(later, side, third_power)
@@ -128,14 +128,20 @@
     sweep(now, turned, result)
 
 
-def placed(pieces):
+def placed(pieces, first_core):
     for core in range(2):
-        for at in range(4):
-            by_y, by_x = pieces[core * 8 + at], pieces[core * 8 + 4 + at]
+        for outer in range(4):
             for inner in range(4):
-                part = pl.ds(inner * 512, 512)
-                yield by_y.at[part], (at // 2 * 1024, ((at % 2) * 8 + inner * 2 + core) * 128)
-                yield by_x.at[part], (inner // 2 * 1024 + 512, ((inner % 2) * 8 + at * 2 + core) * 128)
+                for other in range(2):
+                    part = pieces[core * 4 + outer].at[pl.ds((inner * 2 + other) * 512, 512)]
+
+                    def spot(x, y):
+                        return y // 2 * 1024 + core * 512, (y % 2 * 8 + x * 2 + (core ^ other)) * 128
+
+                    x_first, y_first = spot(inner, outer), spot(outer, inner)
+                    if core:
+                        x_first, y_first = y_first, x_first
+                    yield part, *(jnp.where(first_core, p, q) for p, q in zip(x_first, y_first))
 
 
 def whitened_columns(pieces, where, block, tokens):
@@ -145,7 +151,7 @@
         chain_kernel,
         name="whiten",
         out_shape=jax.ShapeDtypeStruct((COLUMNS, tokens), BF16),
-        in_specs=[pl.BlockSpec(memory_space=pltpu.SMEM)] + [pl.BlockSpec(memory_space=pl.ANY)] * 16,
+        in_specs=[pl.BlockSpec(memory_space=pltpu.SMEM)] + [pl.BlockSpec(memory_space=pl.ANY)] * 8,
         out_specs=pl.BlockSpec(memory_space=pltpu.VMEM),
         scratch_shapes=[
             pltpu.VMEM((tokens, block), BF16),
@@ -161,29 +167,63 @@
     )(where, *pieces)
 
 
-def xor_swap(array, axes, mask, order=lambda i: i, back=lambda i: i):
-    count = lax.axis_size(axes)
-    return lax.ppermute(array, axes, [(i, back(order(i) ^ mask)) for i in range(count)])
-
-
-def y_of(i):
-    return i % 2 * 2 + i // 2
-
-
-def side_pieces(mine):
+def xor_swap(array, axis, mask):
+    return lax.ppermute(array, axis, [(i, i ^ mask) for i in range(lax.axis_size(axis))])
+
+
+def plane_swap(array, first_mask, second_mask):
+    def at(x, y, c):
+        return (((y % 2) * 4 + x) * 2 + c) * 2 + y // 2
+
+    pairs = []
+    for x in range(4):
+        for y in range(4):
+            pairs.append((at(x, y, 0), at(x ^ first_mask, y ^ second_mask, 0)))
+            pairs.append((at(x, y, 1), at(x ^ second_mask, y ^ first_mask, 1)))
+    return lax.ppermute(array, ("yl", "x", "c", "yh"), pairs)
+
+
+def side_pieces(mine, c):
     lower, upper = mine[:512], mine[512:]
+    keep, give = jnp.where(c == 0, lower, upper), jnp.where(c == 0, upper, lower)
+    part = jnp.concatenate([keep, xor_swap(give, "c", 1)])
     masks = (1, 3, 2)
-    lower_x, upper_y = {0: lower}, {0: upper}
-    for m in masks:
-        lower_x[m] = xor_swap(lower, "x", m)
-        upper_y[m] = xor_swap(upper, ("yl", "yh"), m, y_of, y_of)
-    by_y = {0: jnp.concatenate([lower_x[m] for m in range(4)])}
-    by_x = {0: jnp.concatenate([upper_y[m] for m in range(4)])}
-    for m in masks:
-        by_y[m] = xor_swap(by_y[0], ("yl", "yh"), m, y_of, y_of)
-        by_x[m] = xor_swap(by_x[0], "x", m)
-    own = [by_y[m] for m in range(4)] + [by_x[m] for m in range(4)]
+    step = {0: part, **{m: plane_swap(part, m, 0) for m in masks}}
+    row = jnp.concatenate([step[m] for m in range(4)])
+    wide = {0: row, **{m: plane_swap(row, 0, m) for m in masks}}
+    own = [wide[m] for m in range(4)]
     return own + [xor_swap(piece, "c", 1) for piece in own]
+
+
+def tile_kernel(where, own, other, *refs):
+    parts, out, grads = refs[:8], refs[8], refs[9]
+    tokens = grads.shape[1]
+    for slot in range(4):
+        chosen = jnp.where(where[0] == 1, parts[2 * slot + 1][...], parts[2 * slot][...])
+        grads[pl.ds(pl.multiple_of(where[2 + slot] * COLUMNS, COLUMNS), COLUMNS), :] = chosen
+    for core, acts in enumerate((own, other)):
+        product = lax.dot_general(
+            acts[...], grads[...], (((1,), (1,)), ((), ())), preferred_element_type=F32
+        )
+        product = (product / math.sqrt(tokens)).astype(BF16)
+        for at in range(4):
+            row = pl.multiple_of(((at * 2 + core) ^ where[1]) * 32, 32)
+            for side in range(2):
+                out[side, pl.ds(row, 32), :] = product[at * 32 : at * 32 + 32, side * 128 : side * 128 + 128]
+
+
+def update_tile(where, own, other, parts):
+    tokens = own.shape[1]
+    return pl.pallas_call(
+        tile_kernel,
+        name="update_tile",
+        out_shape=jax.ShapeDtypeStruct((2, 256, 128), BF16),
+        in_specs=[pl.BlockSpec(memory_space=pltpu.SMEM)] + [pl.BlockSpec(memory_space=pltpu.VMEM)] * 10,
+        out_specs=pl.BlockSpec(memory_space=pltpu.VMEM),
+        scratch_shapes=[pltpu.VMEM((4 * COLUMNS, tokens), BF16)],
+        compiler_params=pltpu.CompilerParams(vmem_limit_bytes=16 * 2**20),
+        cost_estimate=pl.CostEstimate(flops=2 * 256 * 256 * tokens, bytes_accessed=3 * 2**20, transcendentals=0),
+    )(where, own, other, *parts)
 
 
 def local(activations, out_grads, weight):
@@ -196,7 +236,7 @@
     pieces = [activations[:, 0], activations[:, 1], out_grads[:, 0], out_grads[:, 1]]
     mine = lax.all_to_all(jnp.stack([pieces[k] for k in SIDE_AT]), "z", 0, 0, tiled=True)
     mine = mine.reshape(8 * tok_dev, width)
-    pieces = side_pieces(mine)
+    pieces = side_pieces(mine, c)
 
     is_act = jnp.logical_or(z % 4 == 1, z % 4 == 2)
     sub = (x * 2 + c) * 32
@@ -210,26 +250,21 @@
 
     first = jnp.where(is_act, relative(act_first), upper * COLUMNS)
     second = jnp.where(is_act, relative(act_second), upper * COLUMNS + 32)
-    done = whitened_columns(pieces, jnp.stack([first, second, yh]), block, token_count)
+    done = whitened_columns(pieces, jnp.stack([first, second, yh * 2 + c, c]), block, token_count)
 
     sent = lax.ppermute(done[32:], "z", [(1, 0), (2, 3), (5, 4), (6, 7)])
     act_part = jnp.where(is_act, done[:32], sent)
-    acts = lax.all_gather(act_part, ("x", "c"), axis=0, tiled=True)
     got = {m: lax.ppermute(done, "z", [(s, s ^ m) for s in (0, 3, 4, 7)]) for m in range(1, 8)}
-    slots = [jnp.where(is_act, got[m ^ 1], done if m == 0 else got[m]) for m in (0, 3, 4, 7)]
-    tiles = [
-        jnp.einsum("at,bt->ab", acts, slot, preferred_element_type=F32) / math.sqrt(token_count)
-        for slot in slots
-    ]
+    acts = {0: act_part, **{m: xor_swap(act_part, "x", m) for m in (1, 3, 2)}}
+    acts = jnp.concatenate([acts[m] for m in range(4)])
     base = jnp.where(is_act, z ^ 1, z)
-    low_bit = base % 4 == 3
-    high_bit = base >= 4
-    t0, t3, t4, t7 = tiles
-    t0, t3, t4, t7 = (jnp.where(low_bit, b, a) for a, b in ((t0, t3), (t3, t0), (t4, t7), (t7, t4)))
-    t0, t3, t4, t7 = (jnp.where(high_bit, b, a) for a, b in ((t0, t4), (t3, t7), (t4, t0), (t7, t3)))
-    update = jnp.stack(
-        [jnp.concatenate([t3, t4], axis=1), jnp.concatenate([t7, t0], axis=1)], axis=1
-    ).astype(BF16)
+    spots = []
+    for m in (0, 3, 4, 7):
+        at = base ^ m
+        spots.append(jnp.where(at == 3, 0, jnp.where(at == 4, 1, jnp.where(at == 7, 2, 3))))
+    parts = [part for m in (0, 3, 4, 7) for part in (got[m] if m else done, got[m ^ 1])]
+    numbers = jnp.stack([is_act.astype(jnp.int32), x * 2 + c, *spots]).astype(jnp.int32)
+    update = update_tile(numbers, acts, xor_swap(acts, "c", 1), parts).transpose(1, 0, 2)
 
     late_grads, _ = lax.optimization_barrier((out_grads, pieces[4]))
     grads_whole = lax.all_gather(late_grads, ("yl", "x", "c"), axis=2, tiled=True)

time: 194 us -> 174 us (0.90)
  the two profiles are of different devices: /device:TPU:24 before, /device:TPU:64 now
where the time goes in v3:
time: 174 us; the launch traced here: 172 us
  waiting for transfers between devices  85.5 us (49%)
  starting transfers between devices  32 us (18%)
  Pallas kernels  27.7 us (16%)
  between operations  14.3 us (8%)
  local copies, waits for them, and re-layouts  9.29 us (5%)
  matrix products  2.75 us (2%)
    ppermute x6, waiting for transfers between devices, plane_swap(): return lax.ppermute(array, ('yl', 'x', 'c', 'yh'), pairs)  36.4 us
    ppermute x7, waiting for transfers between devices, local(): lax.ppermute(done, 'z', [(s, s ^ m) for s in (0, 3, 4, 7)])  30.8 us
    pallas_call x1, Pallas kernels, whitened_columns(): pl.pallas_call(chain_kernel, name='whiten', out_shape=jax.ShapeDtypeStruc...  26.3 us
    ppermute x6, starting transfers between devices, plane_swap(): return lax.ppermute(array, ('yl', 'x', 'c', 'yh'), pairs)  9.66 us
    all_to_all x1, waiting for transfers between devices, local(): lax.all_to_all(jnp.stack([pieces[k] for k in SIDE_AT]), 'z', 0, 0, tiled=...  8.99 us
    all_to_all x1, starting transfers between devices, local(): lax.all_to_all(jnp.stack([pieces[k] for k in SIDE_AT]), 'z', 0, 0, tiled=...  8.11 us
    ppermute x7, starting transfers between devices, local(): lax.ppermute(done, 'z', [(s, s ^ m) for s in (0, 3, 4, 7)])  7.15 us
    ppermute x9, waiting for transfers between devices, xor_swap(): lax.ppermute(array, axis, [(i, i ^ mask) for i in range(lax.axis_size(axi...  6.24 us
  transfers between devices with their start and end apart: 25, of which 14 were waited for; matrix products, arithmetic and copies ran while one was open for 1% of the time, Pallas kernels for 16%

profile of v3, /device:TPU:64, one launch (start us, length us, event | category | flops | bytes accessed | tf_op | source)
XLA Modules:
  0.0 171.8 jit_solution(8870219429020155209)
XLA Ops:
  14.1 8.1 %all-to-all-start = ((bf16[8,128,128]{2,1,0:T(8,128)(2,1)}), bf16[8,128,128]{2,1,0:T(8,128)(2,1)S(1)}, u32[]{:S(2)}, u32[]{:S(2)}) async-start(bf16[8,128,128]{2,1,0:T(8,128)(2,1)} %constant_dynamic-update-slice_fusion), calls=%async_computation | async-start | bytes 524288 | tf_op jit(solution)/shard_map/all_to_all | solution.py:237
  22.2 9.0 %all-to-all-done = bf16[8,128,128]{2,1,0:T(8,128)(2,1)S(1)} async-done(((bf16[8,128,128]{2,1,0:T(8,128)(2,1)}), bf16[8,128,128]{2,1,0:T(8,128)(2,1)S(1)}, u32[]{:S(2)}, u32[]{:S(2)}) %all-to-all-start) | async-done | bytes 262176 | tf_op jit(solution)/shard_map/all_to_all | solution.py:237
  31.3 1.3 collective-permute-done
  32.7 1.6 collective-permute-start.1
  34.3 2.7 %collective-permute-start.2 = (bf16[1024,128]{1,0:T(8,128)(2,1)S(1)}, bf16[1024,128]{1,0:T(8,128)(2,1)S(1)}, u32[]{:S(2)}, u32[]{:S(2)}) collective-permute-start(bf16[1024,128]{1,0:T(8,128)(2,1)S(1)} %pad_maximum_fusion.1), channel_id=1, source_target_pairs={{0,8},{2,3},{16,24},{18,19},{1,9},{3,2},{17,25},{19,18},{4,12},{6,... | collective-permute-start | bytes 786440 | tf_op jit(solution)/shard_map/ppermute | solution.py:183
  37.6 1.6 collective-permute-done.1
  39.2 5.1 %collective-permute-done.2 = bf16[1024,128]{1,0:T(8,128)(2,1)S(1)} collective-permute-done((bf16[1024,128]{1,0:T(8,128)(2,1)S(1)}, bf16[1024,128]{1,0:T(8,128)(2,1)S(1)}, u32[]{:S(2)}, u32[]{:S(2)}) %collective-permute-start.2) | collective-permute-done | bytes 262176 | tf_op jit(solution)/shard_map/ppermute | solution.py:183
  44.3 2.7 %collective-permute-done.3 = bf16[1024,128]{1,0:T(8,128)(2,1)S(1)} collective-permute-done((bf16[1024,128]{1,0:T(8,128)(2,1)S(1)}, bf16[1024,128]{1,0:T(8,128)(2,1)S(1)}, u32[]{:S(2)}, u32[]{:S(2)}) %collective-permute-start.3) | collective-permute-done | bytes 262176 | tf_op jit(solution)/shard_map/ppermute | solution.py:183
  47.0 1.7 collective-permute-start.4
  48.7 2.9 %collective-permute-start.5 = (bf16[4096,128]{1,0:T(8,128)(2,1)S(1)}, bf16[4096,128]{1,0:T(8,128)(2,1)}, u32[]{:S(2)}, u32[]{:S(2)}) collective-permute-start(bf16[4096,128]{1,0:T(8,128)(2,1)S(1)} %constant_dynamic-update-slice_fusion.8.refs_1_), channel_id=1, source_target_pairs={{0,1},{2,10},{16,17},{18,26},{1,0},{3,11},{17,16},{19,27},{4,5},{6... | collective-permute-start | bytes 3145736 | tf_op jit(solution)/shard_map/ppermute | solution.py:183
  51.8 10.1 %collective-permute-done.4.refs_2_ = bf16[4096,128]{1,0:T(8,128)(2,1)S(1)} collective-permute-done((bf16[4096,128]{1,0:T(8,128)(2,1)S(1)}, bf16[4096,128]{1,0:T(8,128)(2,1)S(1)}, u32[]{:S(2)}, u32[]{:S(2)}) %collective-permute-start.4) | collective-permute-done | bytes 1048608 | tf_op jit(solution)/shard_map/ppermute | solution.py:183
  61.9 13.9 %collective-permute-done.5.refs_3_ = bf16[4096,128]{1,0:T(8,128)(2,1)} collective-permute-done((bf16[4096,128]{1,0:T(8,128)(2,1)S(1)}, bf16[4096,128]{1,0:T(8,128)(2,1)}, u32[]{:S(2)}, u32[]{:S(2)}) %collective-permute-start.5) | collective-permute-done | bytes 1048608 | tf_op jit(solution)/shard_map/ppermute | solution.py:183
  75.8 3.1 %collective-permute-done.6.refs_4_ = bf16[4096,128]{1,0:T(8,128)(2,1)} collective-permute-done((bf16[4096,128]{1,0:T(8,128)(2,1)S(1)}, bf16[4096,128]{1,0:T(8,128)(2,1)}, u32[]{:S(2)}, u32[]{:S(2)}) %collective-permute-start.6) | collective-permute-done | bytes 1048608 | tf_op jit(solution)/shard_map/ppermute | solution.py:183
  79.7 2.2 %collective-permute-done.10.refs_8_ = bf16[4096,128]{1,0:T(8,128)(2,1)} collective-permute-done((bf16[4096,128]{1,0:T(8,128)(2,1)}, bf16[4096,128]{1,0:T(8,128)(2,1)}, u32[]{:S(2)}, u32[]{:S(2)}) %collective-permute-start.10) | collective-permute-done | bytes 1048608 | tf_op jit(solution)/shard_map/ppermute | solution.py:171
  81.9 26.3 %whiten.1.refs_0_ = bf16[64,2048]{1,0:T(8,128)(2,1)S(1)} custom-call(s32[4]{0:T(128)S(1)} %pad_add_fusion.refs_0_, bf16[4096,128]{1,0:T(8,128)(2,1)S(1)} %constant_dynamic-update-slice_fusion.8.refs_1_, bf16[4096,128]{1,0:T(8,128)(2,1)S(1)} %collective-permute-done.4.refs_2_, bf16[4096,128]{1,0:T(8,128)(2,1)} %collective-permute-done.5.refs_3_, ...), custom_call_target="tpu_custom_call" | custom-call | flops 10871635968 | bytes 8388608 | tf_op jit(solution)/shard_map/whiten/pallas_call | solution.py:150
  108.2 2.7 %collective-permute-start.11 = (bf16[32,2048]{1,0:T(8,128)(2,1)S(1)}, bf16[32,2048]{1,0:T(8,128)(2,1)S(1)}, u32[]{:S(2)}, u32[]{:S(2)}) collective-permute-start(bf16[32,2048]{1,0:T(8,128)(2,1)S(1)} %slice.37), channel_id=1, source_target_pairs={{32,0},{64,96},{160,128},{192,224},{33,1},{65,97},{161,129},{193,2... | collective-permute-start | bytes 393224 | tf_op jit(solution)/shard_map/ppermute | solution.py:255
  110.9 3.0 %collective-permute-done.11 = bf16[32,2048]{1,0:T(8,128)(2,1)S(1)} collective-permute-done((bf16[32,2048]{1,0:T(8,128)(2,1)S(1)}, bf16[32,2048]{1,0:T(8,128)(2,1)S(1)}, u32[]{:S(2)}, u32[]{:S(2)}) %collective-permute-start.11) | collective-permute-done | bytes 131104 | tf_op jit(solution)/shard_map/ppermute | solution.py:255
  115.7 2.5 %collective-permute-start.12 = (bf16[32,2048]{1,0:T(8,128)(2,1)S(1)}, bf16[32,2048]{1,0:T(8,128)(2,1)S(1)}, u32[]{:S(2)}, u32[]{:S(2)}) collective-permute-start(bf16[32,2048]{1,0:T(8,128)(2,1)S(1)} %slice_select_fusion), channel_id=1, source_target_pairs={{0,4},{4,0},{8,12},{12,8},{1,5},{5,1},{9,13},{13,9},{2,6},{6,2},{1... | collective-permute-start | bytes 393224 | tf_op jit(solution)/shard_map/ppermute | solution.py:171
  120.1 2.7 %collective-permute-done.14 = bf16[32,2048]{1,0:T(8,128)(2,1)S(1)} collective-permute-done((bf16[32,2048]{1,0:T(8,128)(2,1)S(1)}, bf16[32,2048]{1,0:T(8,128)(2,1)S(1)}, u32[]{:S(2)}, u32[]{:S(2)}) %collective-permute-start.14) | collective-permute-done | bytes 131104 | tf_op jit(solution)/shard_map/ppermute | solution.py:171
  124.9 2.2 %collective-permute-done.16.refs_1_ = bf16[64,2048]{1,0:T(8,128)(2,1)S(1)} collective-permute-done((bf16[64,2048]{1,0:T(8,128)(2,1)S(1)}, bf16[64,2048]{1,0:T(8,128)(2,1)S(1)}, u32[]{:S(2)}, u32[]{:S(2)}) %collective-permute-start.16) | collective-permute-done | bytes 262176 | tf_op jit(solution)/shard_map/ppermute | solution.py:257
  129.1 19.1 %collective-permute-done.18.refs_3_ = bf16[64,2048]{1,0:T(8,128)(2,1)S(1)} collective-permute-done((bf16[64,2048]{1,0:T(8,128)(2,1)S(1)}, bf16[64,2048]{1,0:T(8,128)(2,1)S(1)}, u32[]{:S(2)}, u32[]{:S(2)}) %collective-permute-start.18) | collective-permute-done | bytes 262176 | tf_op jit(solution)/shard_map/ppermute | solution.py:257
  149.7 9.5 %collective-permute-done.22.refs_7_ = bf16[64,2048]{1,0:T(8,128)(2,1)S(1)} collective-permute-done((bf16[64,2048]{1,0:T(8,128)(2,1)S(1)}, bf16[64,2048]{1,0:T(8,128)(2,1)S(1)}, u32[]{:S(2)}, u32[]{:S(2)}) %collective-permute-start.22) | collective-permute-done | bytes 262176 | tf_op jit(solution)/shard_map/ppermute | solution.py:257
  159.2 1.5 update_tile.1
  161.4 2.8 %fusion.6 = bf16[128,2,128]{2,0,1:T(8,128)(2,1)S(1)} fusion(bf16[2,16,2,8,2048]{4,3,2,1,0:T(8,128)(2,1)} %bitcast.57, bf16[128,2,2048]{2,0,1:T(8,128)(2,1)} %all-gather.2.cloned.1.call-done), kind=kOutput, calls=%fused_computation.4 | convolution fusion | flops 268468224 | bytes 3211264 | tf_op jit(solution)/shard_map/tjq,bcjq->tbc/dot_general | solution.py:271
  (57 shorter events, 19.3 us)
Async XLA Ops:
  14.1 17.1 %all-to-all-start = ((bf16[8,128,128]{2,1,0:T(8,128)(2,1)}), bf16[8,128,128]{2,1,0:T(8,128)(2,1)S(1)}, u32[]{:S(2)}, u32[]{:S(2)}) async-start(bf16[8,128,128]{2,1,0:T(8,128)(2,1)} %constant_dynamic-update-slice_fusion), calls=%async_computation | async-start | bytes 524288 | tf_op jit(solution)/shard_map/all_to_all | solution.py:237
  22.2 139.2 %all-gather.2.cloned.1.call-start = ((), (), s32[]{:S(2)}) async-start(), calls=%async_computation.1 | async-start | bytes 1114112 | tf_op jit(solution)/shard_map/all_gather | solution.py:270
  32.7 6.5 %collective-permute-start.1 = (bf16[1024,128]{1,0:T(8,128)(2,1)S(1)}, bf16[1024,128]{1,0:T(8,128)(2,1)S(1)}, u32[]{:S(2)}, u32[]{:S(2)}) collective-permute-start(bf16[1024,128]{1,0:T(8,128)(2,1)S(1)} %pad_maximum_fusion.1), channel_id=1, source_target_pairs={{0,4},{2,18},{16,20},{18,2},{1,5},{3,19},{17,21},{19,3},{4,0},{6,2... | collective-permute-start | bytes 786440 | tf_op jit(solution)/shard_map/ppermute | solution.py:183
  34.3 10.0 %collective-permute-start.2 = (bf16[1024,128]{1,0:T(8,128)(2,1)S(1)}, bf16[1024,128]{1,0:T(8,128)(2,1)S(1)}, u32[]{:S(2)}, u32[]{:S(2)}) collective-permute-start(bf16[1024,128]{1,0:T(8,128)(2,1)S(1)} %pad_maximum_fusion.1), channel_id=1, source_target_pairs={{0,8},{2,3},{16,24},{18,19},{1,9},{3,2},{17,25},{19,18},{4,12},{6,... | collective-permute-start | bytes 786440 | tf_op jit(solution)/shard_map/ppermute | solution.py:183
  37.0 10.0 %collective-permute-start.3 = (bf16[1024,128]{1,0:T(8,128)(2,1)S(1)}, bf16[1024,128]{1,0:T(8,128)(2,1)S(1)}, u32[]{:S(2)}, u32[]{:S(2)}) collective-permute-start(bf16[1024,128]{1,0:T(8,128)(2,1)S(1)} %pad_maximum_fusion.1), channel_id=1, source_target_pairs={{0,12},{2,19},{16,28},{18,3},{1,13},{3,18},{17,29},{19,2},{4,8},{6... | collective-permute-start | bytes 786440 | tf_op jit(solution)/shard_map/ppermute | solution.py:183
  47.0 14.9 %collective-permute-start.4 = (bf16[4096,128]{1,0:T(8,128)(2,1)S(1)}, bf16[4096,128]{1,0:T(8,128)(2,1)S(1)}, u32[]{:S(2)}, u32[]{:S(2)}) collective-permute-start(bf16[4096,128]{1,0:T(8,128)(2,1)S(1)} %constant_dynamic-update-slice_fusion.8.refs_1_), channel_id=1, source_target_pairs={{0,16},{2,6},{16,0},{18,22},{1,17},{3,7},{17,1},{19,23},{4,20},{6,... | collective-permute-start | bytes 3145736 | tf_op jit(solution)/shard_map/ppermute | solution.py:183
  48.7 27.1 %collective-permute-start.5 = (bf16[4096,128]{1,0:T(8,128)(2,1)S(1)}, bf16[4096,128]{1,0:T(8,128)(2,1)}, u32[]{:S(2)}, u32[]{:S(2)}) collective-permute-start(bf16[4096,128]{1,0:T(8,128)(2,1)S(1)} %constant_dynamic-update-slice_fusion.8.refs_1_), channel_id=1, source_target_pairs={{0,1},{2,10},{16,17},{18,26},{1,0},{3,11},{17,16},{19,27},{4,5},{6... | collective-permute-start | bytes 3145736 | tf_op jit(solution)/shard_map/ppermute | solution.py:183
  51.6 27.4 %collective-permute-start.6 = (bf16[4096,128]{1,0:T(8,128)(2,1)S(1)}, bf16[4096,128]{1,0:T(8,128)(2,1)}, u32[]{:S(2)}, u32[]{:S(2)}) collective-permute-start(bf16[4096,128]{1,0:T(8,128)(2,1)S(1)} %constant_dynamic-update-slice_fusion.8.refs_1_), channel_id=1, source_target_pairs={{0,17},{2,14},{16,1},{18,30},{1,16},{3,15},{17,0},{19,31},{4,21},{... | collective-permute-start | bytes 3145736 | tf_op jit(solution)/shard_map/ppermute | solution.py:183
  51.8 27.2 %collective-permute-start.7 = (bf16[4096,128]{1,0:T(8,128)(2,1)S(1)}, bf16[4096,128]{1,0:T(8,128)(2,1)}, u32[]{:S(2)}, u32[]{:S(2)}) collective-permute-start(bf16[4096,128]{1,0:T(8,128)(2,1)S(1)} %constant_dynamic-update-slice_fusion.8.refs_1_), channel_id=1, source_target_pairs={{0,2},{2,0},{1,3},{3,1},{4,6},{6,4},{5,7},{7,5},{8,10},{10,8},{9,1... | collective-permute-start | bytes 3145736 | tf_op jit(solution)/shard_map/ppermute | solution.py:171
  61.9 17.8 %collective-permute-start.8 = (bf16[4096,128]{1,0:T(8,128)(2,1)S(1)}, bf16[4096,128]{1,0:T(8,128)(2,1)}, u32[]{:S(2)}, u32[]{:S(2)}) collective-permute-start(bf16[4096,128]{1,0:T(8,128)(2,1)S(1)} %collective-permute-done.4.refs_2_), channel_id=1, source_target_pairs={{0,2},{2,0},{1,3},{3,1},{4,6},{6,4},{5,7},{7,5},{8,10},{10,8},{9,1... | collective-permute-start | bytes 3145736 | tf_op jit(solution)/shard_map/ppermute | solution.py:171
  75.8 3.9 %collective-permute-start.9 = (bf16[4096,128]{1,0:T(8,128)(2,1)}, bf16[4096,128]{1,0:T(8,128)(2,1)}, u32[]{:S(2)}, u32[]{:S(2)}) collective-permute-start(bf16[4096,128]{1,0:T(8,128)(2,1)} %collective-permute-done.5.refs_3_), channel_id=1, source_target_pairs={{0,2},{2,0},{1,3},{3,1},{4,6},{6,4},{5,7},{7,5},{8,10},{10,8},{9,1... | collective-permute-start | bytes 3145736 | tf_op jit(solution)/shard_map/ppermute | solution.py:171
  78.9 3.0 %collective-permute-start.10 = (bf16[4096,128]{1,0:T(8,128)(2,1)}, bf16[4096,128]{1,0:T(8,128)(2,1)}, u32[]{:S(2)}, u32[]{:S(2)}) collective-permute-start(bf16[4096,128]{1,0:T(8,128)(2,1)} %collective-permute-done.6.refs_4_), channel_id=1, source_target_pairs={{0,2},{2,0},{1,3},{3,1},{4,6},{6,4},{5,7},{7,5},{8,10},{10,8},{9,1... | collective-permute-start | bytes 3145736 | tf_op jit(solution)/shard_map/ppermute | solution.py:171
  108.2 5.7 %collective-permute-start.11 = (bf16[32,2048]{1,0:T(8,128)(2,1)S(1)}, bf16[32,2048]{1,0:T(8,128)(2,1)S(1)}, u32[]{:S(2)}, u32[]{:S(2)}) collective-permute-start(bf16[32,2048]{1,0:T(8,128)(2,1)S(1)} %slice.37), channel_id=1, source_target_pairs={{32,0},{64,96},{160,128},{192,224},{33,1},{65,97},{161,129},{193,2... | collective-permute-start | bytes 393224 | tf_op jit(solution)/shard_map/ppermute | solution.py:255
  114.0 8.8 %collective-permute-start.14 = (bf16[32,2048]{1,0:T(8,128)(2,1)S(1)}, bf16[32,2048]{1,0:T(8,128)(2,1)S(1)}, u32[]{:S(2)}, u32[]{:S(2)}) collective-permute-start(bf16[32,2048]{1,0:T(8,128)(2,1)S(1)} %slice_select_fusion), channel_id=1, source_target_pairs={{0,12},{4,8},{8,4},{12,0},{1,13},{5,9},{9,5},{13,1},{2,14},{6,10},... | collective-permute-start | bytes 393224 | tf_op jit(solution)/shard_map/ppermute | solution.py:171
  114.5 9.5 %collective-permute-start.13 = (bf16[32,2048]{1,0:T(8,128)(2,1)S(1)}, bf16[32,2048]{1,0:T(8,128)(2,1)S(1)}, u32[]{:S(2)}, u32[]{:S(2)}) collective-permute-start(bf16[32,2048]{1,0:T(8,128)(2,1)S(1)} %slice_select_fusion), channel_id=1, source_target_pairs={{0,8},{4,12},{8,0},{12,4},{1,9},{5,13},{9,1},{13,5},{2,10},{6,14},... | collective-permute-start | bytes 393224 | tf_op jit(solution)/shard_map/ppermute | solution.py:171
  115.7 8.4 %collective-permute-start.12 = (bf16[32,2048]{1,0:T(8,128)(2,1)S(1)}, bf16[32,2048]{1,0:T(8,128)(2,1)S(1)}, u32[]{:S(2)}, u32[]{:S(2)}) collective-permute-start(bf16[32,2048]{1,0:T(8,128)(2,1)S(1)} %slice_select_fusion), channel_id=1, source_target_pairs={{0,4},{4,0},{8,12},{12,8},{1,5},{5,1},{9,13},{13,9},{2,6},{6,2},{1... | collective-permute-start | bytes 393224 | tf_op jit(solution)/shard_map/ppermute | solution.py:171
  118.1 9.0 %collective-permute-start.16 = (bf16[64,2048]{1,0:T(8,128)(2,1)S(1)}, bf16[64,2048]{1,0:T(8,128)(2,1)S(1)}, u32[]{:S(2)}, u32[]{:S(2)}) collective-permute-start(bf16[64,2048]{1,0:T(8,128)(2,1)S(1)} %whiten.1.refs_0_), channel_id=1, source_target_pairs={{0,32},{96,64},{128,160},{224,192},{1,33},{97,65},{129,161},{225,1... | collective-permute-start | bytes 786440 | tf_op jit(solution)/shard_map/ppermute | solution.py:257
  119.4 9.0 %collective-permute-start.17 = (bf16[64,2048]{1,0:T(8,128)(2,1)S(1)}, bf16[64,2048]{1,0:T(8,128)(2,1)S(1)}, u32[]{:S(2)}, u32[]{:S(2)}) collective-permute-start(bf16[64,2048]{1,0:T(8,128)(2,1)S(1)} %whiten.1.refs_0_), channel_id=1, source_target_pairs={{0,96},{96,0},{128,224},{224,128},{1,97},{97,1},{129,225},{225,129... | collective-permute-start | bytes 786440 | tf_op jit(solution)/shard_map/ppermute | solution.py:257
  122.8 25.4 %collective-permute-start.18 = (bf16[64,2048]{1,0:T(8,128)(2,1)S(1)}, bf16[64,2048]{1,0:T(8,128)(2,1)S(1)}, u32[]{:S(2)}, u32[]{:S(2)}) collective-permute-start(bf16[64,2048]{1,0:T(8,128)(2,1)S(1)} %whiten.1.refs_0_), channel_id=1, source_target_pairs={{0,64},{96,32},{128,192},{224,160},{1,65},{97,33},{129,193},{225,1... | collective-permute-start | bytes 786440 | tf_op jit(solution)/shard_map/ppermute | solution.py:257
  124.1 35.0 %collective-permute-start.15 = (bf16[128,2048]{1,0:T(8,128)(2,1)S(1)}, bf16[128,2048]{1,0:T(8,128)(2,1)S(1)}, u32[]{:S(2)}, u32[]{:S(2)}) collective-permute-start(bf16[128,2048]{1,0:T(8,128)(2,1)S(1)} %pad_maximum_fusion.own), channel_id=1, source_target_pairs={{0,2},{2,0},{1,3},{3,1},{4,6},{6,4},{5,7},{7,5},{8,10},{10,8},{9,1... | collective-permute-start | bytes 1572872 | tf_op jit(solution)/shard_map/ppermute | solution.py:171
  124.2 25.4 %collective-permute-start.19 = (bf16[64,2048]{1,0:T(8,128)(2,1)S(1)}, bf16[64,2048]{1,0:T(8,128)(2,1)S(1)}, u32[]{:S(2)}, u32[]{:S(2)}) collective-permute-start(bf16[64,2048]{1,0:T(8,128)(2,1)S(1)} %whiten.1.refs_0_), channel_id=1, source_target_pairs={{0,128},{96,224},{128,0},{224,96},{1,129},{97,225},{129,1},{225,97... | collective-permute-start | bytes 786440 | tf_op jit(solution)/shard_map/ppermute | solution.py:257
  127.2 22.5 %collective-permute-start.20 = (bf16[64,2048]{1,0:T(8,128)(2,1)S(1)}, bf16[64,2048]{1,0:T(8,128)(2,1)S(1)}, u32[]{:S(2)}, u32[]{:S(2)}) collective-permute-start(bf16[64,2048]{1,0:T(8,128)(2,1)S(1)} %whiten.1.refs_0_), channel_id=1, source_target_pairs={{0,160},{96,192},{128,32},{224,64},{1,161},{97,193},{129,33},{225,... | collective-permute-start | bytes 786440 | tf_op jit(solution)/shard_map/ppermute | solution.py:257
  128.5 21.2 %collective-permute-start.21 = (bf16[64,2048]{1,0:T(8,128)(2,1)S(1)}, bf16[64,2048]{1,0:T(8,128)(2,1)S(1)}, u32[]{:S(2)}, u32[]{:S(2)}) collective-permute-start(bf16[64,2048]{1,0:T(8,128)(2,1)S(1)} %whiten.1.refs_0_), channel_id=1, source_target_pairs={{0,224},{96,128},{128,96},{224,0},{1,225},{97,129},{129,97},{225,1... | collective-permute-start | bytes 786440 | tf_op jit(solution)/shard_map/ppermute | solution.py:257
  148.2 11.0 %collective-permute-start.22 = (bf16[64,2048]{1,0:T(8,128)(2,1)S(1)}, bf16[64,2048]{1,0:T(8,128)(2,1)S(1)}, u32[]{:S(2)}, u32[]{:S(2)}) collective-permute-start(bf16[64,2048]{1,0:T(8,128)(2,1)S(1)} %whiten.1.refs_0_), channel_id=1, source_target_pairs={{0,192},{96,160},{128,64},{224,32},{1,193},{97,161},{129,65},{225,... | collective-permute-start | bytes 786440 | tf_op jit(solution)/shard_map/ppermute | solution.py:257
  (2 other events, 66.9 us)
Sparse Core Ops, SparseCore 0:
  79.8 30.5 all-gather.1

commit v4 on v3

v4 whole, which is shorter than its diff:
```python
import math

import jax
import jax.numpy as jnp
from jax import lax
from jax.experimental import pallas as pl
from jax.experimental.pallas import tpu as pltpu
from jax.sharding import Mesh
from jax.sharding import PartitionSpec as P

DAMPING = 0.1
COLUMNS = 64
GRADS_AT = (0, 3, 4, 7)
F32 = jnp.float32
BF16 = jnp.bfloat16


def split2(value):
    high = value.astype(BF16)
    low = (value - high.astype(F32)).astype(BF16)
    return high, low


def split3(value):
    high = value.astype(BF16)
    rest = value - high.astype(F32)
    middle = rest.astype(BF16)
    low = (rest - middle.astype(F32)).astype(BF16)
    return high, middle, low


def chain_kernel(where, *refs):
    pieces = refs[:8]
    out, side, turned, now, later, f1, f2, f3, u1, u2, sems = refs[8:]
    block, tokens = turned.shape
    half = COLUMNS // 2
    copies = []
    for source, row, col in placed(pieces, where[3] == 0, where[4]):
        row, col = pl.multiple_of(row, 512), pl.multiple_of(col, 128)
        to = side.at[pl.ds(row, 512), pl.ds(col, 128)]
        copies.append((pltpu.make_async_copy(source, to, sems.at[len(copies)]), row, col))
        copies[-1][0].start()
    now[...] = jnp.zeros_like(now)
    later[...] = jnp.zeros_like(later)
    for copy, row, col in copies:
        copy.wait()
        turned[pl.ds(col, 128), pl.ds(row, 512)] = side[pl.ds(row, 512), pl.ds(col, 128)].T

    probe_at = pl.ds(2 * COLUMNS, 16)
    probe_row = lax.broadcasted_iota(jnp.int32, (16, block), 0)

    def times(rows, matrix):
        product = jnp.dot(rows[...], matrix[...], preferred_element_type=F32)
        probe = jnp.sum(product[2 * COLUMNS :], axis=0, keepdims=True)
        return product[:COLUMNS] + product[COLUMNS : 2 * COLUMNS], probe

    def keep(target, rows, probe=None):
        target[:COLUMNS], target[COLUMNS : 2 * COLUMNS] = split2(rows)
        if probe is not None:
            high, middle, low = (part.astype(F32) for part in split3(probe))
            stacked = jnp.where(probe_row == 0, high, jnp.where(probe_row == 1, middle, low))
            target[probe_at] = jnp.where(probe_row < 3, stacked, 0.0).astype(BF16)

    def unit():
        row = lax.broadcasted_iota(jnp.int32, (COLUMNS, block), 0)
        wanted = jnp.where(row < half, where[0] + row, where[1] + row - half)
        col = lax.broadcasted_iota(jnp.int32, (COLUMNS, block), 1)
        return jnp.where(col == wanted, 1.0, 0.0)

    later[:half] = turned[pl.ds(pl.multiple_of(where[0], half), half), :]
    later[half:COLUMNS] = turned[pl.ds(pl.multiple_of(where[1], half), half), :]
    rows, _ = times(later, side)
    rows = rows / tokens + DAMPING * unit()
    f1[...] = rows
    keep(now, rows, jnp.ones((1, block), F32))
    keep(later, *times(now, turned))
    rows, probe = times(later, side)
    rows, probe = rows / tokens + DAMPING * f1[...], probe / tokens + DAMPING
    f2[...], u1[...] = rows, probe
    keep(now, rows, probe)
    keep(later, *times(now, turned))
    rows, probe = times(later, side)
    rows, probe = rows / tokens + DAMPING * f2[...], probe / tokens + DAMPING * u1[...]
    f3[...], u2[...] = rows, probe
    keep(now, rows, probe)
    rows, probe = times(now, turned)
    keep(later, rows)
    norm = jnp.sum(u2[...] * u2[...], axis=1, keepdims=True)
    scale = (jnp.sum(probe * probe, axis=1, keepdims=True) / tokens + DAMPING * norm) / norm
    inverse = 1.0 / scale
    inverse2 = inverse * inverse
    rows, _ = times(later, side)
    a3 = f3[...] * (inverse2 * inverse)
    a4 = (rows / tokens) * (inverse2 * inverse2) + DAMPING * (a3 * inverse)
    total = 36.0 * unit() - 39.0 * (f1[...] * inverse) + 27.0 * (f2[...] * inverse2)
    keep(now, (total - 9.0 * a3 + a4) * (1.0 / (16.0 * jnp.sqrt(scale))))
    rows, _ = times(now, turned)
    for at in range(tokens // 128):
        to = pl.ds(pl.multiple_of((at ^ where[2]) * 128, 128), 128)
        out[:, to] = rows[:, at * 128 : at * 128 + 128].astype(BF16)


def placed(pieces, first_core, upper_z):
    for core in range(2):
        for outer in range(4):
            for inner in range(4):
                for other in range(2):
                    part = pieces[core * 4 + outer].at[pl.ds((inner * 2 + other) * 512, 512)]

                    def spot(x, y):
                        return y // 2 * 1024 + core * 512, (y % 2 * 8 + x * 2) * 128

                    x_first, y_first = spot(inner, outer), spot(outer, inner)
                    if core:
                        x_first, y_first = y_first, x_first
                    row, col = (jnp.where(first_core, p, q) for p, q in zip(x_first, y_first))
                    yield part, row, col + ((core ^ other) ^ upper_z) * 128


def whitened_columns(pieces, where, block, tokens):
    rows = 2 * COLUMNS + 16
    passes = 8 * 2 * rows * block * tokens
    return pl.pallas_call(
        chain_kernel,
        name="whiten",
        out_shape=jax.ShapeDtypeStruct((COLUMNS, tokens), BF16),
        in_specs=[pl.BlockSpec(memory_space=pltpu.SMEM)] + [pl.BlockSpec(memory_space=pl.ANY)] * 8,
        out_specs=pl.BlockSpec(memory_space=pltpu.VMEM),
        scratch_shapes=[
            pltpu.VMEM((tokens, block), BF16),
            pltpu.VMEM((block, tokens), BF16),
            pltpu.VMEM((rows, block), BF16),
            pltpu.VMEM((rows, tokens), BF16),
            *[pltpu.VMEM((COLUMNS, block), F32)] * 3,
            *[pltpu.VMEM((1, block), F32)] * 2,
            pltpu.SemaphoreType.DMA((64,)),
        ],
        compiler_params=pltpu.CompilerParams(vmem_limit_bytes=32 * 2**20),
        cost_estimate=pl.CostEstimate(flops=passes, bytes_accessed=2 * block * tokens, transcendentals=0),
    )(where, *pieces)


def xor_swap(array, axis, mask):
    return lax.ppermute(array, axis, [(i, i ^ mask) for i in range(lax.axis_size(axis))])


def z_and_x_swap(array, mask, q):
    pairs = []
    for z in range(8):
        for x in range(4):
            if z not in GRADS_AT:
                pairs.append((z * 4 + x, (z if mask else z ^ 1) * 4 + (x ^ q)))
            elif mask:
                pairs.append((z * 4 + x, (z ^ mask) * 4 + x))
    return lax.ppermute(array, ("z", "x"), pairs)


def plane_swap(array, first_mask, second_mask):
    def at(x, y, c):
        return (((y % 2) * 4 + x) * 2 + c) * 2 + y // 2

    pairs = []
    for x in range(4):
        for y in range(4):
            pairs.append((at(x, y, 0), at(x ^ first_mask, y ^ second_mask, 0)))
            pairs.append((at(x, y, 1), at(x ^ second_mask, y ^ first_mask, 1)))
    return lax.ppermute(array, ("yl", "x", "c", "yh"), pairs)


def side_parts(activations, out_grads, z, c):
    acts_here = (z ^ z // 2) % 2 == 1
    same = jnp.where(acts_here, activations, out_grads)
    other = jnp.where(acts_here, out_grads, activations)
    swap = (z // 4) ^ c == 1
    pieces = [jnp.where(swap, kind[:, 1 - j], kind[:, j]) for kind in (same, other) for j in range(2)]
    parts = []
    for m in range(8):
        pairs = [(i * 2 + j, (i ^ m ^ (4 * j)) * 2 + i // 4) for i in range(8) for j in range(2)]
        parts.append(lax.ppermute(pieces[(m ^ m // 2) % 2 * 2 + m // 4], ("z", "c"), pairs))
    return parts


def side_pieces(parts):
    part = jnp.concatenate(parts)
    masks = (1, 3, 2)
    step = {0: part, **{m: plane_swap(part, m, 0) for m in masks}}
    row = jnp.concatenate([step[m] for m in range(4)])
    wide = {0: row, **{m: plane_swap(row, 0, m) for m in masks}}
    own = [wide[m] for m in range(4)]
    return own + [xor_swap(piece, "c", 1) for piece in own]


def tile_kernel(where, own, other, *refs):
    parts, out, grads = refs[:8], refs[8], refs[9]
    tokens = grads.shape[1]
    for slot in range(4):
        chosen = jnp.where(where[0] == 1, parts[2 * slot + 1][...], parts[2 * slot][...])
        grads[pl.ds(pl.multiple_of(where[2 + slot] * COLUMNS, COLUMNS), COLUMNS), :] = chosen
    for core, acts in enumerate((own, other)):
        product = lax.dot_general(
            acts[...], grads[...], (((1,), (1,)), ((), ())), preferred_element_type=F32
        )
        product = (product / math.sqrt(tokens)).astype(BF16)
        for at in range(4):
            row = pl.multiple_of(((at * 2 + core) ^ where[1]) * 32, 32)
            for side in range(2):
                out[side, pl.ds(row, 32), :] = product[at * 32 : at * 32 + 32, side * 128 : side * 128 + 128]


def update_tile(where, own, other, parts):
    tokens = own.shape[1]
    return pl.pallas_call(
        tile_kernel,
        name="update_tile",
        out_shape=jax.ShapeDtypeStruct((2, 256, 128), BF16),
        in_specs=[pl.BlockSpec(memory_space=pltpu.SMEM)] + [pl.BlockSpec(memory_space=pltpu.VMEM)] * 10,
        out_specs=pl.BlockSpec(memory_space=pltpu.VMEM),
        scratch_shapes=[pltpu.VMEM((4 * COLUMNS, tokens), BF16)],
        compiler_params=pltpu.CompilerParams(vmem_limit_bytes=16 * 2**20),
        cost_estimate=pl.CostEstimate(flops=2 * 256 * 256 * tokens, bytes_accessed=3 * 2**20, transcendentals=0),
    )(where, own, other, *parts)


def local(activations, out_grads, weight):
    tok_dev, blocks, width = activations.shape
    outs = lax.axis_size(("yl", "x", "c"))
    block = width * outs
    z, yl, x, c, yh = (lax.axis_index(a) for a in ("z", "yl", "x", "c", "yh"))
    token_count = tok_dev * lax.axis_size("z") * lax.axis_size("yh")

    pieces = side_pieces(side_parts(activations, out_grads, z, c))

    is_act = jnp.logical_or(z % 4 == 1, z % 4 == 2)
    sub = (x * 2 + c) * 32
    act_first = ((z % 4) * 2 + yh) * 256 + sub
    act_second = (((z ^ 1) % 4) * 2 + yh) * 256 + sub
    upper = z % 2

    def relative(column):
        place = column // width
        return (((place // 8) ^ yl) * 8 + ((place // 2 % 4) ^ x) * 2 + ((place % 2) ^ c)) * width + column % width

    first = jnp.where(is_act, relative(act_first), upper * COLUMNS)
    second = jnp.where(is_act, relative(act_second), upper * COLUMNS + 32)
    done = whitened_columns(pieces, jnp.stack([first, second, yh * 8 + c * 4 + z % 4, c, z // 4]), block, token_count)

    late_grads, _ = lax.optimization_barrier((out_grads, pieces[1]))
    grads_whole = lax.all_gather(late_grads, ("yl", "x", "c"), axis=2, tiled=True)
    input_grad = jnp.einsum(
        "tjq,bcjq->tbc",
        grads_whole,
        weight.reshape(blocks, width, blocks, block),
        preferred_element_type=F32,
    ).astype(BF16)

    near = {m: z_and_x_swap(done, m, q) for q, m in ((1, 3), (2, 7), (3, 4))}
    far = {q: z_and_x_swap(done[32:], None, q) for q in range(4)}
    got = {m: lax.ppermute(done, "z", [(s, s ^ m) for s in GRADS_AT]) for m in (1, 2, 5, 6)}
    acts = [jnp.where(is_act, done[:32], far[0])]
    acts += [jnp.where(is_act, near[m][:32], far[q]) for q, m in ((1, 3), (2, 7), (3, 4))]
    acts, input_grad = lax.optimization_barrier((jnp.concatenate(acts), input_grad))
    base = jnp.where(is_act, z ^ 1, z)
    spots = [(base ^ m) // 4 * 2 + (base ^ m) % 2 for m in GRADS_AT]
    parts = [part for m in GRADS_AT for part in (near[m] if m else done, got[m ^ 1])]
    numbers = jnp.stack([is_act.astype(jnp.int32), x * 2 + c, *spots]).astype(jnp.int32)
    update = update_tile(numbers, acts, xor_swap(acts, "c", 1), parts).transpose(1, 0, 2)
    return update, input_grad


def solution(mesh):
    split = Mesh(
        mesh.devices.reshape(mesh.shape["tok"], 2, 4, 2, mesh.shape["grp"]),
        ("z", "yl", "x", "c", "yh"),
    )
    out = ("yl", "x", "c")
    in_specs = (P(("z", "yh"), None, out), P(("z", "yh"), None, out), P(None, out, None))
    out_specs = (P(("z", "yh"), None, out), P(("z", "yh"), None, out))
    return jax.shard_map(local, mesh=split, in_specs=in_specs, out_specs=out_specs, check_vma=False)
```

time: 174 us -> 184 us (1.057)
  the two profiles are of different devices: /device:TPU:64 before, /device:TPU:32 now
where the time goes in v4:
time: 184 us
  waiting for transfers between devices  85.9 us (47%)
  starting transfers between devices  57.5 us (31%)
  Pallas kernels  19.5 us (11%)
  between operations  14.5 us (8%)
  matrix products  2.75 us (1%)
  local copies, waits for them, and re-layouts  2.53 us (1%)
    ppermute x6, waiting for transfers between devices, plane_swap(): return lax.ppermute(array, ('yl', 'x', 'c', 'yh'), pairs)  33.9 us
    ppermute x4, waiting for transfers between devices, local(): lax.ppermute(done, 'z', [(s, s ^ m) for s in GRADS_AT])  24.1 us
    ppermute x8, starting transfers between devices, side_parts(): lax.ppermute(pieces[(m ^ m // 2) % 2 * 2 + m // 4], ('z', 'c'), pairs)  22.9 us
    pallas_call x1, Pallas kernels, whitened_columns(): pl.pallas_call(chain_kernel, name='whiten', out_shape=jax.ShapeDtypeStruc...  18 us
    ppermute x7, starting transfers between devices, z_and_x_swap(): return lax.ppermute(array, ('z', 'x'), pairs)  16.8 us
    ppermute x7, waiting for transfers between devices, z_and_x_swap(): return lax.ppermute(array, ('z', 'x'), pairs)  11.9 us
    all_gather x1, waiting for transfers between devices, local(): lax.all_gather(late_grads, ('yl', 'x', 'c'), axis=2, tiled=True)  11.6 us
    ppermute x6, starting transfers between devices, plane_swap(): return lax.ppermute(array, ('yl', 'x', 'c', 'yh'), pairs)  9.57 us
  transfers between devices with their start and end apart: 31, of which 16 were waited for; matrix products, arithmetic and copies ran while one was open for 1% of the time, Pallas kernels for 0%

profile of v4, /device:TPU:32, one launch (start us, length us, event | category | flops | bytes accessed | tf_op | source)
XLA Modules:
  0.0 183.7 jit_solution(10835999965776545886)
XLA Ops:
  8.9 1.9 %collective-permute-start.1 = (bf16[128,128]{1,0:T(8,128)(2,1)S(1)}, bf16[128,128]{1,0:T(8,128)(2,1)S(1)}, u32[]{:S(2)}, u32[]{:S(2)}) collective-permute-start(bf16[128,128]{1,0:T(8,128)(2,1)S(1)} %get-tuple-element.13), channel_id=1, source_target_pairs={{0,32},{2,160},{32,0},{34,128},{64,96},{66,224},{96,64},{98,192},{... | collective-permute-start | bytes 98312 | tf_op jit(solution)/shard_map/ppermute | solution.py:179
  12.8 10.1 %collective-permute-start.5 = (bf16[128,128]{1,0:T(8,128)(2,1)S(1)}, bf16[128,128]{1,0:T(8,128)(2,1)S(1)}, u32[]{:S(2)}, u32[]{:S(2)}) collective-permute-start(bf16[128,128]{1,0:T(8,128)(2,1)S(1)} %get-tuple-element.12), channel_id=1, source_target_pairs={{0,160},{2,32},{32,128},{34,0},{64,224},{66,96},{96,192},{98,64},{... | collective-permute-start | bytes 98312 | tf_op jit(solution)/shard_map/ppermute | solution.py:179
  22.9 3.9 %collective-permute-start.6 = (bf16[128,128]{1,0:T(8,128)(2,1)S(1)}, bf16[128,128]{1,0:T(8,128)(2,1)S(1)}, u32[]{:S(2)}, u32[]{:S(2)}) collective-permute-start(bf16[128,128]{1,0:T(8,128)(2,1)S(1)} %get-tuple-element.12), channel_id=1, source_target_pairs={{0,192},{2,64},{32,224},{34,96},{64,128},{66,0},{96,160},{98,32},{... | collective-permute-start | bytes 98312 | tf_op jit(solution)/shard_map/ppermute | solution.py:179
  28.7 2.4 %collective-permute-start.7 = (bf16[128,128]{1,0:T(8,128)(2,1)S(1)}, bf16[128,128]{1,0:T(8,128)(2,1)S(1)}, u32[]{:S(2)}, u32[]{:S(2)}) collective-permute-start(bf16[128,128]{1,0:T(8,128)(2,1)S(1)} %get-tuple-element.14), channel_id=1, source_target_pairs={{0,224},{2,96},{32,192},{34,64},{64,160},{66,32},{96,128},{98,0},{... | collective-permute-start | bytes 98312 | tf_op jit(solution)/shard_map/ppermute | solution.py:179
  34.3 2.7 %collective-permute-start.9 = (bf16[1024,128]{1,0:T(8,128)(2,1)S(1)}, bf16[1024,128]{1,0:T(8,128)(2,1)S(1)}, u32[]{:S(2)}, u32[]{:S(2)}) collective-permute-start(bf16[1024,128]{1,0:T(8,128)(2,1)S(1)} %get-tuple-element.16), channel_id=1, source_target_pairs={{0,8},{2,3},{16,24},{18,19},{1,9},{3,2},{17,25},{19,18},{4,12},{6,... | collective-permute-start | bytes 786440 | tf_op jit(solution)/shard_map/ppermute | solution.py:167
  39.2 5.1 %collective-permute-done.9 = bf16[1024,128]{1,0:T(8,128)(2,1)S(1)} collective-permute-done((bf16[1024,128]{1,0:T(8,128)(2,1)S(1)}, bf16[1024,128]{1,0:T(8,128)(2,1)S(1)}, u32[]{:S(2)}, u32[]{:S(2)}) %collective-permute-start.9) | collective-permute-done | bytes 262176 | tf_op jit(solution)/shard_map/ppermute | solution.py:167
  44.3 2.7 %collective-permute-done.10 = bf16[1024,128]{1,0:T(8,128)(2,1)S(1)} collective-permute-done((bf16[1024,128]{1,0:T(8,128)(2,1)S(1)}, bf16[1024,128]{1,0:T(8,128)(2,1)S(1)}, u32[]{:S(2)}, u32[]{:S(2)}) %collective-permute-start.10) | collective-permute-done | bytes 262176 | tf_op jit(solution)/shard_map/ppermute | solution.py:167
  48.7 2.9 %collective-permute-start.12 = (bf16[4096,128]{1,0:T(8,128)(2,1)S(1)}, bf16[4096,128]{1,0:T(8,128)(2,1)}, u32[]{:S(2)}, u32[]{:S(2)}) collective-permute-start(bf16[4096,128]{1,0:T(8,128)(2,1)S(1)} %constant_dynamic-update-slice_fusion.8.refs_0_), channel_id=1, source_target_pairs={{0,1},{2,10},{16,17},{18,26},{1,0},{3,11},{17,16},{19,27},{4,5},{6... | collective-permute-start | bytes 3145736 | tf_op jit(solution)/shard_map/ppermute | solution.py:167
  52.9 9.1 %collective-permute-done.11.refs_1_ = bf16[4096,128]{1,0:T(8,128)(2,1)S(1)} collective-permute-done((bf16[4096,128]{1,0:T(8,128)(2,1)S(1)}, bf16[4096,128]{1,0:T(8,128)(2,1)S(1)}, u32[]{:S(2)}, u32[]{:S(2)}) %collective-permute-start.11) | collective-permute-done | bytes 1048608 | tf_op jit(solution)/shard_map/ppermute | solution.py:167
  63.1 12.8 %collective-permute-done.12.refs_2_ = bf16[4096,128]{1,0:T(8,128)(2,1)} collective-permute-done((bf16[4096,128]{1,0:T(8,128)(2,1)S(1)}, bf16[4096,128]{1,0:T(8,128)(2,1)}, u32[]{:S(2)}, u32[]{:S(2)}) %collective-permute-start.12) | collective-permute-done | bytes 1048608 | tf_op jit(solution)/shard_map/ppermute | solution.py:167
  76.3 2.7 %collective-permute-done.13.refs_3_ = bf16[4096,128]{1,0:T(8,128)(2,1)} collective-permute-done((bf16[4096,128]{1,0:T(8,128)(2,1)S(1)}, bf16[4096,128]{1,0:T(8,128)(2,1)}, u32[]{:S(2)}, u32[]{:S(2)}) %collective-permute-start.13) | collective-permute-done | bytes 1048608 | tf_op jit(solution)/shard_map/ppermute | solution.py:167
  79.2 2.8 %collective-permute-done.17.refs_7_ = bf16[4096,128]{1,0:T(8,128)(2,1)} collective-permute-done((bf16[4096,128]{1,0:T(8,128)(2,1)}, bf16[4096,128]{1,0:T(8,128)(2,1)}, u32[]{:S(2)}, u32[]{:S(2)}) %collective-permute-start.17) | collective-permute-done | bytes 1048608 | tf_op jit(solution)/shard_map/ppermute | solution.py:144
  82.0 18.0 %whiten.1.refs_0_ = bf16[64,2048]{1,0:T(8,128)(2,1)S(1)} custom-call(s32[5]{0:T(128)S(1)} %stack.55.where, bf16[4096,128]{1,0:T(8,128)(2,1)S(1)} %constant_dynamic-update-slice_fusion.8.refs_0_, bf16[4096,128]{1,0:T(8,128)(2,1)S(1)} %collective-permute-done.11.refs_1_, bf16[4096,128]{1,0:T(8,128)(2,1)} %collective-permute-done.12.refs_2_, ...), custom_call_target="tpu_custom_call" | custom-call | flops 9663676416 | bytes 8388608 | tf_op jit(solution)/shard_map/whiten/pallas_call | solution.py:123
  100.0 5.0 %collective-permute-start.18 = (bf16[32,2048]{1,0:T(8,128)(2,1)S(1)}, bf16[32,2048]{1,0:T(8,128)(2,1)S(1)}, u32[]{:S(2)}, u32[]{:S(2)}) collective-permute-start(bf16[32,2048]{1,0:T(8,128)(2,1)S(1)} %slice.48), channel_id=1, source_target_pairs={{32,0},{36,4},{40,8},{44,12},{64,96},{68,100},{72,104},{76,108},{1... | collective-permute-start | bytes 393224 | tf_op jit(solution)/shard_map/ppermute | solution.py:155
  107.0 2.8 %collective-permute-start.23 = (bf16[64,2048]{1,0:T(8,128)(2,1)S(1)}, bf16[64,2048]{1,0:T(8,128)(2,1)S(1)}, u32[]{:S(2)}, u32[]{:S(2)}) collective-permute-start(bf16[64,2048]{1,0:T(8,128)(2,1)S(1)} %whiten.1.refs_0_), channel_id=1, source_target_pairs={{0,128},{4,132},{8,136},{12,140},{32,44},{36,40},{40,36},{44,32},{... | collective-permute-start | bytes 786440 | tf_op jit(solution)/shard_map/ppermute | solution.py:155
  109.8 2.1 %collective-permute-start.22 = (bf16[32,2048]{1,0:T(8,128)(2,1)S(1)}, bf16[32,2048]{1,0:T(8,128)(2,1)S(1)}, u32[]{:S(2)}, u32[]{:S(2)}) collective-permute-start(bf16[32,2048]{1,0:T(8,128)(2,1)S(1)} %slice.48), channel_id=1, source_target_pairs={{32,8},{36,12},{40,0},{44,4},{64,104},{68,108},{72,96},{76,100},{1... | collective-permute-start | bytes 393224 | tf_op jit(solution)/shard_map/ppermute | solution.py:155
  111.9 4.3 %collective-permute-start.21 = (bf16[64,2048]{1,0:T(8,128)(2,1)S(1)}, bf16[64,2048]{1,0:T(8,128)(2,1)S(1)}, u32[]{:S(2)}, u32[]{:S(2)}) collective-permute-start(bf16[64,2048]{1,0:T(8,128)(2,1)S(1)} %whiten.1.refs_0_), channel_id=1, source_target_pairs={{0,224},{4,228},{8,232},{12,236},{32,40},{36,44},{40,32},{44,36},{... | collective-permute-start | bytes 786440 | tf_op jit(solution)/shard_map/ppermute | solution.py:155
  119.4 3.3 %collective-permute-done.22 = bf16[32,2048]{1,0:T(8,128)(2,1)S(1)} collective-permute-done((bf16[32,2048]{1,0:T(8,128)(2,1)S(1)}, bf16[32,2048]{1,0:T(8,128)(2,1)S(1)}, u32[]{:S(2)}, u32[]{:S(2)}) %collective-permute-start.22) | collective-permute-done | bytes 131104 | tf_op jit(solution)/shard_map/ppermute | solution.py:155
  122.7 1.9 %collective-permute-done.21.refs_6_ = bf16[64,2048]{1,0:T(8,128)(2,1)S(1)} collective-permute-done((bf16[64,2048]{1,0:T(8,128)(2,1)S(1)}, bf16[64,2048]{1,0:T(8,128)(2,1)S(1)}, u32[]{:S(2)}, u32[]{:S(2)}) %collective-permute-start.21) | collective-permute-done | bytes 262176 | tf_op jit(solution)/shard_map/ppermute | solution.py:155
  125.4 4.1 %collective-permute-done.19.refs_2_ = bf16[64,2048]{1,0:T(8,128)(2,1)S(1)} collective-permute-done((bf16[64,2048]{1,0:T(8,128)(2,1)S(1)}, bf16[64,2048]{1,0:T(8,128)(2,1)S(1)}, u32[]{:S(2)}, u32[]{:S(2)}) %collective-permute-start.19) | collective-permute-done | bytes 262176 | tf_op jit(solution)/shard_map/ppermute | solution.py:155
  129.6 11.6 %all-gather.2.cloned.1.call-done = bf16[128,2,2048]{2,0,1:T(8,128)(2,1)} async-done(((bf16[128,2,128]{2,0,1:T(8,128)(2,1)}), bf16[128,2,2048]{2,0,1:T(8,128)(2,1)}) %all-gather.2.cloned.1.call-update) | async-done | bytes 1048592 | tf_op jit(solution)/shard_map/all_gather | solution.py:248
  141.2 2.8 %fusion.6 = bf16[128,2,128]{2,0,1:T(8,128)(2,1)S(1)} fusion(bf16[2,16,2,8,2048]{4,3,2,1,0:T(8,128)(2,1)} %bitcast.37, bf16[128,2,2048]{2,0,1:T(8,128)(2,1)} %all-gather.2.cloned.1.call-done), kind=kOutput, calls=%fused_computation.4 | convolution fusion | flops 268468224 | bytes 3211264 | tf_op jit(solution)/shard_map/tjq,bcjq->tbc/dot_general | solution.py:249
  150.4 16.1 %collective-permute-done.26.refs_1_ = bf16[64,2048]{1,0:T(8,128)(2,1)S(1)} collective-permute-done((bf16[64,2048]{1,0:T(8,128)(2,1)S(1)}, bf16[64,2048]{1,0:T(8,128)(2,1)S(1)}, u32[]{:S(2)}, u32[]{:S(2)}) %collective-permute-start.26) | collective-permute-done | bytes 262176 | tf_op jit(solution)/shard_map/ppermute | solution.py:258
  166.6 8.0 %collective-permute-done.27.refs_3_ = bf16[64,2048]{1,0:T(8,128)(2,1)S(1)} collective-permute-done((bf16[64,2048]{1,0:T(8,128)(2,1)S(1)}, bf16[64,2048]{1,0:T(8,128)(2,1)S(1)}, u32[]{:S(2)}, u32[]{:S(2)}) %collective-permute-start.27) | collective-permute-done | bytes 262176 | tf_op jit(solution)/shard_map/ppermute | solution.py:258
  (69 shorter events, 30.3 us)
Async XLA Ops:
  7.2 134.1 %all-gather.2.cloned.1.call-start = ((), (), s32[]{:S(2)}) async-start(), calls=%async_computation | async-start | bytes 1114112 | tf_op jit(solution)/shard_map/all_gather | solution.py:248
  8.2 14.7 %collective-permute-start = (bf16[128,128]{1,0:T(8,128)(2,1)S(1)}, bf16[128,128]{1,0:T(8,128)(2,1)S(1)}, u32[]{:S(2)}, u32[]{:S(2)}) collective-permute-start(bf16[128,128]{1,0:T(8,128)(2,1)S(1)} %get-tuple-element.15), channel_id=1, source_target_pairs={{0,0},{2,128},{32,32},{34,160},{64,64},{66,192},{96,96},{98,224},{... | collective-permute-start | bytes 98312 | tf_op jit(solution)/shard_map/ppermute | solution.py:179
  8.9 17.9 %collective-permute-start.1 = (bf16[128,128]{1,0:T(8,128)(2,1)S(1)}, bf16[128,128]{1,0:T(8,128)(2,1)S(1)}, u32[]{:S(2)}, u32[]{:S(2)}) collective-permute-start(bf16[128,128]{1,0:T(8,128)(2,1)S(1)} %get-tuple-element.13), channel_id=1, source_target_pairs={{0,32},{2,160},{32,0},{34,128},{64,96},{66,224},{96,64},{98,192},{... | collective-permute-start | bytes 98312 | tf_op jit(solution)/shard_map/ppermute | solution.py:179
  10.8 17.9 %collective-permute-start.2 = (bf16[128,128]{1,0:T(8,128)(2,1)S(1)}, bf16[128,128]{1,0:T(8,128)(2,1)S(1)}, u32[]{:S(2)}, u32[]{:S(2)}) collective-permute-start(bf16[128,128]{1,0:T(8,128)(2,1)S(1)} %get-tuple-element.13), channel_id=1, source_target_pairs={{0,64},{2,192},{32,96},{34,224},{64,0},{66,128},{96,32},{98,160},{... | collective-permute-start | bytes 98312 | tf_op jit(solution)/shard_map/ppermute | solution.py:179
  12.3 18.8 %collective-permute-start.3 = (bf16[128,128]{1,0:T(8,128)(2,1)S(1)}, bf16[128,128]{1,0:T(8,128)(2,1)S(1)}, u32[]{:S(2)}, u32[]{:S(2)}) collective-permute-start(bf16[128,128]{1,0:T(8,128)(2,1)S(1)} %get-tuple-element.15), channel_id=1, source_target_pairs={{0,96},{2,224},{32,64},{34,192},{64,32},{66,160},{96,0},{98,128},{... | collective-permute-start | bytes 98312 | tf_op jit(solution)/shard_map/ppermute | solution.py:179
  12.8 18.4 %collective-permute-start.5 = (bf16[128,128]{1,0:T(8,128)(2,1)S(1)}, bf16[128,128]{1,0:T(8,128)(2,1)S(1)}, u32[]{:S(2)}, u32[]{:S(2)}) collective-permute-start(bf16[128,128]{1,0:T(8,128)(2,1)S(1)} %get-tuple-element.12), channel_id=1, source_target_pairs={{0,160},{2,32},{32,128},{34,0},{64,224},{66,96},{96,192},{98,64},{... | collective-permute-start | bytes 98312 | tf_op jit(solution)/shard_map/ppermute | solution.py:179
  34.3 10.0 %collective-permute-start.9 = (bf16[1024,128]{1,0:T(8,128)(2,1)S(1)}, bf16[1024,128]{1,0:T(8,128)(2,1)S(1)}, u32[]{:S(2)}, u32[]{:S(2)}) collective-permute-start(bf16[1024,128]{1,0:T(8,128)(2,1)S(1)} %get-tuple-element.16), channel_id=1, source_target_pairs={{0,8},{2,3},{16,24},{18,19},{1,9},{3,2},{17,25},{19,18},{4,12},{6,... | collective-permute-start | bytes 786440 | tf_op jit(solution)/shard_map/ppermute | solution.py:167
  37.0 10.0 %collective-permute-start.10 = (bf16[1024,128]{1,0:T(8,128)(2,1)S(1)}, bf16[1024,128]{1,0:T(8,128)(2,1)S(1)}, u32[]{:S(2)}, u32[]{:S(2)}) collective-permute-start(bf16[1024,128]{1,0:T(8,128)(2,1)S(1)} %get-tuple-element.16), channel_id=1, source_target_pairs={{0,12},{2,19},{16,28},{18,3},{1,13},{3,18},{17,29},{19,2},{4,8},{6... | collective-permute-start | bytes 786440 | tf_op jit(solution)/shard_map/ppermute | solution.py:167
  47.1 14.9 %collective-permute-start.11 = (bf16[4096,128]{1,0:T(8,128)(2,1)S(1)}, bf16[4096,128]{1,0:T(8,128)(2,1)S(1)}, u32[]{:S(2)}, u32[]{:S(2)}) collective-permute-start(bf16[4096,128]{1,0:T(8,128)(2,1)S(1)} %constant_dynamic-update-slice_fusion.8.refs_0_), channel_id=1, source_target_pairs={{0,16},{2,6},{16,0},{18,22},{1,17},{3,7},{17,1},{19,23},{4,20},{6,... | collective-permute-start | bytes 3145736 | tf_op jit(solution)/shard_map/ppermute | solution.py:167
  48.7 27.1 %collective-permute-start.12 = (bf16[4096,128]{1,0:T(8,128)(2,1)S(1)}, bf16[4096,128]{1,0:T(8,128)(2,1)}, u32[]{:S(2)}, u32[]{:S(2)}) collective-permute-start(bf16[4096,128]{1,0:T(8,128)(2,1)S(1)} %constant_dynamic-update-slice_fusion.8.refs_0_), channel_id=1, source_target_pairs={{0,1},{2,10},{16,17},{18,26},{1,0},{3,11},{17,16},{19,27},{4,5},{6... | collective-permute-start | bytes 3145736 | tf_op jit(solution)/shard_map/ppermute | solution.py:167
  51.6 27.4 %collective-permute-start.13 = (bf16[4096,128]{1,0:T(8,128)(2,1)S(1)}, bf16[4096,128]{1,0:T(8,128)(2,1)}, u32[]{:S(2)}, u32[]{:S(2)}) collective-permute-start(bf16[4096,128]{1,0:T(8,128)(2,1)S(1)} %constant_dynamic-update-slice_fusion.8.refs_0_), channel_id=1, source_target_pairs={{0,17},{2,14},{16,1},{18,30},{1,16},{3,15},{17,0},{19,31},{4,21},{... | collective-permute-start | bytes 3145736 | tf_op jit(solution)/shard_map/ppermute | solution.py:167
  51.8 27.3 %collective-permute-start.14 = (bf16[4096,128]{1,0:T(8,128)(2,1)S(1)}, bf16[4096,128]{1,0:T(8,128)(2,1)}, u32[]{:S(2)}, u32[]{:S(2)}) collective-permute-start(bf16[4096,128]{1,0:T(8,128)(2,1)S(1)} %constant_dynamic-update-slice_fusion.8.refs_0_), channel_id=1, source_target_pairs={{0,2},{2,0},{1,3},{3,1},{4,6},{6,4},{5,7},{7,5},{8,10},{10,8},{9,1... | collective-permute-start | bytes 3145736 | tf_op jit(solution)/shard_map/ppermute | solution.py:144
  61.9 17.2 %collective-permute-start.15 = (bf16[4096,128]{1,0:T(8,128)(2,1)S(1)}, bf16[4096,128]{1,0:T(8,128)(2,1)}, u32[]{:S(2)}, u32[]{:S(2)}) collective-permute-start(bf16[4096,128]{1,0:T(8,128)(2,1)S(1)} %collective-permute-done.11.refs_1_), channel_id=1, source_target_pairs={{0,2},{2,0},{1,3},{3,1},{4,6},{6,4},{5,7},{7,5},{8,10},{10,8},{9,1... | collective-permute-start | bytes 3145736 | tf_op jit(solution)/shard_map/ppermute | solution.py:144
  100.0 16.1 %collective-permute-start.18 = (bf16[32,2048]{1,0:T(8,128)(2,1)S(1)}, bf16[32,2048]{1,0:T(8,128)(2,1)S(1)}, u32[]{:S(2)}, u32[]{:S(2)}) collective-permute-start(bf16[32,2048]{1,0:T(8,128)(2,1)S(1)} %slice.48), channel_id=1, source_target_pairs={{32,0},{36,4},{40,8},{44,12},{64,96},{68,100},{72,104},{76,108},{1... | collective-permute-start | bytes 393224 | tf_op jit(solution)/shard_map/ppermute | solution.py:155
  105.7 11.7 %collective-permute-start.24 = (bf16[32,2048]{1,0:T(8,128)(2,1)S(1)}, bf16[32,2048]{1,0:T(8,128)(2,1)S(1)}, u32[]{:S(2)}, u32[]{:S(2)}) collective-permute-start(bf16[32,2048]{1,0:T(8,128)(2,1)S(1)} %slice.48), channel_id=1, source_target_pairs={{32,12},{36,8},{40,4},{44,0},{64,108},{68,104},{72,100},{76,96},{1... | collective-permute-start | bytes 393224 | tf_op jit(solution)/shard_map/ppermute | solution.py:155
  107.0 12.4 %collective-permute-start.23 = (bf16[64,2048]{1,0:T(8,128)(2,1)S(1)}, bf16[64,2048]{1,0:T(8,128)(2,1)S(1)}, u32[]{:S(2)}, u32[]{:S(2)}) collective-permute-start(bf16[64,2048]{1,0:T(8,128)(2,1)S(1)} %whiten.1.refs_0_), channel_id=1, source_target_pairs={{0,128},{4,132},{8,136},{12,140},{32,44},{36,40},{40,36},{44,32},{... | collective-permute-start | bytes 786440 | tf_op jit(solution)/shard_map/ppermute | solution.py:155
  109.8 12.9 %collective-permute-start.22 = (bf16[32,2048]{1,0:T(8,128)(2,1)S(1)}, bf16[32,2048]{1,0:T(8,128)(2,1)S(1)}, u32[]{:S(2)}, u32[]{:S(2)}) collective-permute-start(bf16[32,2048]{1,0:T(8,128)(2,1)S(1)} %slice.48), channel_id=1, source_target_pairs={{32,8},{36,12},{40,0},{44,4},{64,104},{68,108},{72,96},{76,100},{1... | collective-permute-start | bytes 393224 | tf_op jit(solution)/shard_map/ppermute | solution.py:155
  111.9 12.8 %collective-permute-start.21 = (bf16[64,2048]{1,0:T(8,128)(2,1)S(1)}, bf16[64,2048]{1,0:T(8,128)(2,1)S(1)}, u32[]{:S(2)}, u32[]{:S(2)}) collective-permute-start(bf16[64,2048]{1,0:T(8,128)(2,1)S(1)} %whiten.1.refs_0_), channel_id=1, source_target_pairs={{0,224},{4,228},{8,232},{12,236},{32,40},{36,44},{40,32},{44,36},{... | collective-permute-start | bytes 786440 | tf_op jit(solution)/shard_map/ppermute | solution.py:155
  117.5 12.1 %collective-permute-start.19 = (bf16[64,2048]{1,0:T(8,128)(2,1)S(1)}, bf16[64,2048]{1,0:T(8,128)(2,1)S(1)}, u32[]{:S(2)}, u32[]{:S(2)}) collective-permute-start(bf16[64,2048]{1,0:T(8,128)(2,1)S(1)} %whiten.1.refs_0_), channel_id=1, source_target_pairs={{0,96},{4,100},{8,104},{12,108},{32,36},{36,32},{40,44},{44,40},{6... | collective-permute-start | bytes 786440 | tf_op jit(solution)/shard_map/ppermute | solution.py:155
  144.0 30.6 %collective-permute-start.25 = (bf16[128,2048]{1,0:T(8,128)(2,1)S(1)}, bf16[128,2048]{1,0:T(8,128)(2,1)S(1)}, u32[]{:S(2)}, u32[]{:S(2)}) collective-permute-start(bf16[128,2048]{1,0:T(8,128)(2,1)S(1)} %pad_maximum_fusion.own), channel_id=1, source_target_pairs={{0,2},{2,0},{1,3},{3,1},{4,6},{6,4},{5,7},{7,5},{8,10},{10,8},{9,1... | collective-permute-start | bytes 1572872 | tf_op jit(solution)/shard_map/ppermute | solution.py:144
  144.3 22.2 %collective-permute-start.26 = (bf16[64,2048]{1,0:T(8,128)(2,1)S(1)}, bf16[64,2048]{1,0:T(8,128)(2,1)S(1)}, u32[]{:S(2)}, u32[]{:S(2)}) collective-permute-start(bf16[64,2048]{1,0:T(8,128)(2,1)S(1)} %whiten.1.refs_0_), channel_id=1, source_target_pairs={{0,32},{96,64},{128,160},{224,192},{1,33},{97,65},{129,161},{225,1... | collective-permute-start | bytes 786440 | tf_op jit(solution)/shard_map/ppermute | solution.py:258
  145.6 28.9 %collective-permute-start.27 = (bf16[64,2048]{1,0:T(8,128)(2,1)S(1)}, bf16[64,2048]{1,0:T(8,128)(2,1)S(1)}, u32[]{:S(2)}, u32[]{:S(2)}) collective-permute-start(bf16[64,2048]{1,0:T(8,128)(2,1)S(1)} %whiten.1.refs_0_), channel_id=1, source_target_pairs={{0,64},{96,32},{128,192},{224,160},{1,65},{97,33},{129,193},{225,1... | collective-permute-start | bytes 786440 | tf_op jit(solution)/shard_map/ppermute | solution.py:258
  146.9 27.6 %collective-permute-start.28 = (bf16[64,2048]{1,0:T(8,128)(2,1)S(1)}, bf16[64,2048]{1,0:T(8,128)(2,1)S(1)}, u32[]{:S(2)}, u32[]{:S(2)}) collective-permute-start(bf16[64,2048]{1,0:T(8,128)(2,1)S(1)} %whiten.1.refs_0_), channel_id=1, source_target_pairs={{0,160},{96,192},{128,32},{224,64},{1,161},{97,193},{129,33},{225,... | collective-permute-start | bytes 786440 | tf_op jit(solution)/shard_map/ppermute | solution.py:258
  148.2 26.4 %collective-permute-start.29 = (bf16[64,2048]{1,0:T(8,128)(2,1)S(1)}, bf16[64,2048]{1,0:T(8,128)(2,1)S(1)}, u32[]{:S(2)}, u32[]{:S(2)}) collective-permute-start(bf16[64,2048]{1,0:T(8,128)(2,1)S(1)} %whiten.1.refs_0_), channel_id=1, source_target_pairs={{0,192},{96,160},{128,64},{224,32},{1,193},{97,161},{129,65},{225,... | collective-permute-start | bytes 786440 | tf_op jit(solution)/shard_map/ppermute | solution.py:258
  (8 other events, 64.8 us)
Sparse Core Ops, SparseCore 0:
  105.8 35.3 all-gather.1

commit v5 on v4

--- a/solution.py
+++ b/solution.py
@@ -10,7 +10,6 @@
 
 DAMPING = 0.1
 COLUMNS = 64
-GRADS_AT = (0, 3, 4, 7)
 F32 = jnp.float32
 BF16 = jnp.bfloat16
 
@@ -35,7 +34,7 @@
     block, tokens = turned.shape
     half = COLUMNS // 2
     copies = []
-    for source, row, col in placed(pieces, where[3] == 0, where[4]):
+    for source, row, col in placed(pieces, where[3] == 0):
         row, col = pl.multiple_of(row, 512), pl.multiple_of(col, 128)
         to = side.at[pl.ds(row, 512), pl.ds(col, 128)]
         copies.append((pltpu.make_async_copy(source, to, sems.at[len(copies)]), row, col))
@@ -95,12 +94,13 @@
     total = 36.0 * unit() - 39.0 * (f1[...] * inverse) + 27.0 * (f2[...] * inverse2)
     keep(now, (total - 9.0 * a3 + a4) * (1.0 / (16.0 * jnp.sqrt(scale))))
     rows, _ = times(now, turned)
-    for at in range(tokens // 128):
-        to = pl.ds(pl.multiple_of((at ^ where[2]) * 128, 128), 128)
+    for at in range(16):
+        z = (where[4 + at // 4 % 2] - 2 * (at % 4)) % 8
+        to = pl.ds(pl.multiple_of(((at // 8) ^ where[2]) * 1024 + z * 128, 128), 128)
         out[:, to] = rows[:, at * 128 : at * 128 + 128].astype(BF16)
 
 
-def placed(pieces, first_core, upper_z):
+def placed(pieces, first_core):
     for core in range(2):
         for outer in range(4):
             for inner in range(4):
@@ -114,7 +114,7 @@
                     if core:
                         x_first, y_first = y_first, x_first
                     row, col = (jnp.where(first_core, p, q) for p, q in zip(x_first, y_first))
-                    yield part, row, col + ((core ^ other) ^ upper_z) * 128
+                    yield part, row, col + (core ^ other) * 128
 
 
 def whitened_columns(pieces, where, block, tokens):
@@ -144,15 +144,9 @@
     return lax.ppermute(array, axis, [(i, i ^ mask) for i in range(lax.axis_size(axis))])
 
 
-def z_and_x_swap(array, mask, q):
-    pairs = []
-    for z in range(8):
-        for x in range(4):
-            if z not in GRADS_AT:
-                pairs.append((z * 4 + x, (z if mask else z ^ 1) * 4 + (x ^ q)))
-            elif mask:
-                pairs.append((z * 4 + x, (z ^ mask) * 4 + x))
-    return lax.ppermute(array, ("z", "x"), pairs)
+def y_swap(array, mask):
+    pairs = [(y % 2 * 2 + y // 2, (y ^ mask) % 2 * 2 + (y ^ mask) // 2) for y in range(4)]
+    return lax.ppermute(array, ("yl", "yh"), pairs)
 
 
 def plane_swap(array, first_mask, second_mask):
@@ -167,58 +161,79 @@
     return lax.ppermute(array, ("yl", "x", "c", "yh"), pairs)
 
 
-def side_parts(activations, out_grads, z, c):
-    acts_here = (z ^ z // 2) % 2 == 1
-    same = jnp.where(acts_here, activations, out_grads)
-    other = jnp.where(acts_here, out_grads, activations)
-    swap = (z // 4) ^ c == 1
-    pieces = [jnp.where(swap, kind[:, 1 - j], kind[:, j]) for kind in (same, other) for j in range(2)]
-    parts = []
-    for m in range(8):
-        pairs = [(i * 2 + j, (i ^ m ^ (4 * j)) * 2 + i // 4) for i in range(8) for j in range(2)]
-        parts.append(lax.ppermute(pieces[(m ^ m // 2) % 2 * 2 + m // 4], ("z", "c"), pairs))
-    return parts
-
-
-def side_pieces(parts):
-    part = jnp.concatenate(parts)
+def twin(z):
+    return (z + 1 if z % 2 else z - 1) % 8
+
+
+def shared_part(activations, out_grads, z, c):
+    turn = (z + 1) // 2 % 4
+    pieces = (activations[:, 0], out_grads[:, 0], activations[:, 1], out_grads[:, 1])
+    odd, far = turn % 2 == 1, turn >= 2
+    pieces = [jnp.where(odd, pieces[(j + 1) % 4], pieces[j]) for j in range(4)]
+    pieces = [jnp.where(far, pieces[(j + 2) % 4], pieces[j]) for j in range(4)]
+    got = [pieces[0]]
+    for shift in (1, 2, 3):
+        got.append(lax.ppermute(pieces[shift], "z", [(i, (i + 2 * shift) % 8) for i in range(8)]))
+    got = jnp.concatenate(got)
+    across, beside = [], []
+    for i in range(8):
+        for j in range(2):
+            if i % 2 == j:
+                across.append((i * 2 + j, twin(i) * 2 + j))
+            else:
+                across.append((i * 2 + j, i * 2 + 1 - j))
+                beside.append((i * 2 + j, twin(i) * 2 + 1 - j))
+    one = lax.ppermute(got, ("z", "c"), across)
+    two = lax.ppermute(got, ("z", "c"), beside)
+    stays = z % 2 == c
+    return jnp.concatenate([jnp.where(stays, got, one), jnp.where(stays, one, two)])
+
+
+def side_pieces(part):
     masks = (1, 3, 2)
     step = {0: part, **{m: plane_swap(part, m, 0) for m in masks}}
     row = jnp.concatenate([step[m] for m in range(4)])
     wide = {0: row, **{m: plane_swap(row, 0, m) for m in masks}}
-    own = [wide[m] for m in range(4)]
-    return own + [xor_swap(piece, "c", 1) for piece in own]
-
-
-def tile_kernel(where, own, other, *refs):
-    parts, out, grads = refs[:8], refs[8], refs[9]
+    return [wide[m] for m in range(4)]
+
+
+def tile_kernel(where, acts, own, other, out, grads):
     tokens = grads.shape[1]
-    for slot in range(4):
-        chosen = jnp.where(where[0] == 1, parts[2 * slot + 1][...], parts[2 * slot][...])
-        grads[pl.ds(pl.multiple_of(where[2 + slot] * COLUMNS, COLUMNS), COLUMNS), :] = chosen
-    for core, acts in enumerate((own, other)):
-        product = lax.dot_general(
-            acts[...], grads[...], (((1,), (1,)), ((), ())), preferred_element_type=F32
-        )
-        product = (product / math.sqrt(tokens)).astype(BF16)
+    for core, part in enumerate((own, other)):
         for at in range(4):
-            row = pl.multiple_of(((at * 2 + core) ^ where[1]) * 32, 32)
-            for side in range(2):
-                out[side, pl.ds(row, 32), :] = product[at * 32 : at * 32 + 32, side * 128 : side * 128 + 128]
-
-
-def update_tile(where, own, other, parts):
+            row = pl.multiple_of(((at * 2 + core) ^ where[0]) * 32, 32)
+            grads[pl.ds(row, 32), :] = part[at * 32 : at * 32 + 32, :]
+    product = lax.dot_general(acts[...], grads[...], (((1,), (1,)), ((), ())), preferred_element_type=F32)
+    product = (product / math.sqrt(tokens)).astype(BF16)
+    for at in range(4):
+        row = pl.multiple_of((at ^ where[1]) * 64, 64)
+        for core in range(2):
+            out[core ^ where[2], pl.ds(row, 64), :] = product[at * 64 : at * 64 + 64, core * 128 : core * 128 + 128]
+
+
+def update_tile(where, acts, own, other):
     tokens = own.shape[1]
     return pl.pallas_call(
         tile_kernel,
         name="update_tile",
         out_shape=jax.ShapeDtypeStruct((2, 256, 128), BF16),
-        in_specs=[pl.BlockSpec(memory_space=pltpu.SMEM)] + [pl.BlockSpec(memory_space=pltpu.VMEM)] * 10,
+        in_specs=[pl.BlockSpec(memory_space=pltpu.SMEM)] + [pl.BlockSpec(memory_space=pltpu.VMEM)] * 3,
         out_specs=pl.BlockSpec(memory_space=pltpu.VMEM),
-        scratch_shapes=[pltpu.VMEM((4 * COLUMNS, tokens), BF16)],
+        scratch_shapes=[pltpu.VMEM((256, tokens), BF16)],
         compiler_params=pltpu.CompilerParams(vmem_limit_bytes=16 * 2**20),
-        cost_estimate=pl.CostEstimate(flops=2 * 256 * 256 * tokens, bytes_accessed=3 * 2**20, transcendentals=0),
-    )(where, own, other, *parts)
+        cost_estimate=pl.CostEstimate(flops=2 * 256 * 256 * tokens, bytes_accessed=2**21, transcendentals=0),
+    )(where, acts, own, other)
+
+
+def owners(step):
+    pairs = []
+    for z in range(8):
+        act_side, grad_side = (0, 1, 1, 0)[z // 2], z // 4
+        for yl in range(2):
+            for c in range(2):
+                to = ((act_side * 4 + yl * 2 + c) * 2 + z % 2) * 2 + (step ^ grad_side)
+                pairs.append(((z * 2 + yl) * 2 + c, to))
+    return pairs
 
 
 def local(activations, out_grads, weight):
@@ -228,42 +243,48 @@
     z, yl, x, c, yh = (lax.axis_index(a) for a in ("z", "yl", "x", "c", "yh"))
     token_count = tok_dev * lax.axis_size("z") * lax.axis_size("yh")
 
-    pieces = side_pieces(side_parts(activations, out_grads, z, c))
-
-    is_act = jnp.logical_or(z % 4 == 1, z % 4 == 2)
-    sub = (x * 2 + c) * 32
-    act_first = ((z % 4) * 2 + yh) * 256 + sub
-    act_second = (((z ^ 1) % 4) * 2 + yh) * 256 + sub
-    upper = z % 2
-
-    def relative(column):
-        place = column // width
-        return (((place // 8) ^ yl) * 8 + ((place // 2 % 4) ^ x) * 2 + ((place % 2) ^ c)) * width + column % width
-
-    first = jnp.where(is_act, relative(act_first), upper * COLUMNS)
-    second = jnp.where(is_act, relative(act_second), upper * COLUMNS + 32)
-    done = whitened_columns(pieces, jnp.stack([first, second, yh * 8 + c * 4 + z % 4, c, z // 4]), block, token_count)
-
-    late_grads, _ = lax.optimization_barrier((out_grads, pieces[1]))
-    grads_whole = lax.all_gather(late_grads, ("yl", "x", "c"), axis=2, tiled=True)
+    pieces = side_pieces(shared_part(activations, out_grads, z, c))
+    grads_whole = lax.all_gather(out_grads, ("yl", "x", "c"), axis=2, tiled=True)
     input_grad = jnp.einsum(
         "tjq,bcjq->tbc",
         grads_whole,
         weight.reshape(blocks, width, blocks, block),
         preferred_element_type=F32,
     ).astype(BF16)
-
-    near = {m: z_and_x_swap(done, m, q) for q, m in ((1, 3), (2, 7), (3, 4))}
-    far = {q: z_and_x_swap(done[32:], None, q) for q in range(4)}
-    got = {m: lax.ppermute(done, "z", [(s, s ^ m) for s in GRADS_AT]) for m in (1, 2, 5, 6)}
-    acts = [jnp.where(is_act, done[:32], far[0])]
-    acts += [jnp.where(is_act, near[m][:32], far[q]) for q, m in ((1, 3), (2, 7), (3, 4))]
-    acts, input_grad = lax.optimization_barrier((jnp.concatenate(acts), input_grad))
-    base = jnp.where(is_act, z ^ 1, z)
-    spots = [(base ^ m) // 4 * 2 + (base ^ m) % 2 for m in GRADS_AT]
-    parts = [part for m in GRADS_AT for part in (near[m] if m else done, got[m ^ 1])]
-    numbers = jnp.stack([is_act.astype(jnp.int32), x * 2 + c, *spots]).astype(jnp.int32)
-    update = update_tile(numbers, acts, xor_swap(acts, "c", 1), parts).transpose(1, 0, 2)
+    pieces, input_grad = lax.optimization_barrier((pieces, input_grad))
+    pieces = pieces + [xor_swap(piece, "c", 1) for piece in pieces]
+
+    y = yh * 2 + yl
+    is_act = (z + 1) // 2 % 2 == 0
+    act_first = ((yl * 2 + c) * 2 + yh) * 256 + x * 64
+    grad_first = (z % 2 * 4 + x) * 256 + (y * 2 + c) * 32
+    grad_second = ((1 - z % 2) * 4 + x) * 256 + (y * 2 + c) * 32
+
+    def relative(column):
+        place = column // width
+        return (((place // 8) ^ yl) * 8 + ((place // 2 % 4) ^ x) * 2 + ((place % 2) ^ c)) * width + column % width
+
+    first = relative(jnp.where(is_act, act_first, grad_first))
+    second = relative(jnp.where(is_act, act_first + 32, grad_second))
+    pair = jnp.where(z % 2 == 1, z + 1, z - 1) % 8
+    done = whitened_columns(
+        pieces,
+        jnp.stack([first, second, yh, c, jnp.where(z % 2 == c, z, pair), jnp.where(z % 2 == c, pair, z)]),
+        block,
+        token_count,
+    )
+
+    swapped = xor_swap(done, "z", 1)
+    grads = jnp.where(is_act, swapped[32:], done[:32])
+    acts = jnp.where(is_act, done, swapped)
+    grads = {0: grads, **{m: y_swap(grads, m) for m in (1, 3, 2)}}
+    acts = {0: acts, **{m: xor_swap(acts, "x", m) for m in (1, 3, 2)}}
+    grads = jnp.concatenate([grads[m] for m in range(4)])
+    acts = jnp.concatenate([acts[m] for m in range(4)])
+    numbers = jnp.stack([y * 2 + c, x, z // 4]).astype(jnp.int32)
+    tile = update_tile(numbers, acts, grads, xor_swap(grads, "c", 1))
+    tile = [lax.ppermute(tile[step], ("z", "yl", "c"), owners(step)) for step in range(2)]
+    update = jnp.stack([jnp.where(c == 0, tile[0], tile[1]), jnp.where(c == 0, tile[1], tile[0])], axis=1)
     return update, input_grad
 
 

time: 184 us -> 172 us (0.935)
  the two profiles are of different devices: /device:TPU:32 before, /device:TPU:64 now
where the time goes in v5:
time: 172 us
  waiting for transfers between devices  78.2 us (45%)
  starting transfers between devices  53.5 us (31%)
  Pallas kernels  19.3 us (11%)
  between operations  14.3 us (8%)
  local copies, waits for them, and re-layouts  3.58 us (2%)
  matrix products  2.75 us (2%)
    all_gather x1, waiting for transfers between devices, local(): lax.all_gather(out_grads, ('yl', 'x', 'c'), axis=2, tiled=True)  25 us
    ppermute x9, waiting for transfers between devices, xor_swap(): lax.ppermute(array, axis, [(i, i ^ mask) for i in range(lax.axis_size(axi...  24.8 us
    ppermute x9, starting transfers between devices, xor_swap(): lax.ppermute(array, axis, [(i, i ^ mask) for i in range(lax.axis_size(axi...  21.7 us
    pallas_call x1, Pallas kernels, whitened_columns(): pl.pallas_call(chain_kernel, name='whiten', out_shape=jax.ShapeDtypeStruc...  18.2 us
    ppermute x3, starting transfers between devices, shared_part(): lax.ppermute(pieces[shift], 'z', [(i, (i + 2 * shift) % 8) for i in range...  9.6 us
    ppermute x6, waiting for transfers between devices, plane_swap(): return lax.ppermute(array, ('yl', 'x', 'c', 'yh'), pairs)  9.42 us
    ppermute x6, starting transfers between devices, plane_swap(): return lax.ppermute(array, ('yl', 'x', 'c', 'yh'), pairs)  8.97 us
    ppermute x2, waiting for transfers between devices, local(): lax.ppermute(tile[step], ('z', 'yl', 'c'), owners(step))  8.33 us
  transfers between devices with their start and end apart: 26, of which 16 were waited for; matrix products, arithmetic and copies ran while one was open for 2% of the time, Pallas kernels for 0%

profile of v5, /device:TPU:64, one launch (start us, length us, event | category | flops | bytes accessed | tf_op | source)
XLA Modules:
  0.0 172.1 jit_solution(7682167946591714931)
XLA Ops:
  10.7 5.5 %collective-permute-start.1 = (bf16[128,128]{1,0:T(8,128)(2,1)S(1)}, bf16[128,128]{1,0:T(8,128)(2,1)S(1)}, u32[]{:S(2)}, u32[]{:S(2)}) collective-permute-start(bf16[128,128]{1,0:T(8,128)(2,1)S(1)} %select_bitcast_fusion.3), channel_id=1, source_target_pairs={{0,128},{32,160},{64,192},{96,224},{128,0},{160,32},{192,64},{224,... | collective-permute-start | bytes 98312 | tf_op jit(solution)/shard_map/ppermute | solution.py:176
  16.1 2.7 %collective-permute-start = (bf16[128,128]{1,0:T(8,128)(2,1)S(1)}, bf16[128,128]{1,0:T(8,128)(2,1)S(1)}, u32[]{:S(2)}, u32[]{:S(2)}) collective-permute-start(bf16[128,128]{1,0:T(8,128)(2,1)S(1)} %get-tuple-element.24), channel_id=1, source_target_pairs={{0,64},{32,96},{64,128},{96,160},{128,192},{160,224},{192,0},{224,... | collective-permute-start | bytes 98312 | tf_op jit(solution)/shard_map/ppermute | solution.py:176
  18.8 2.1 %collective-permute-done = bf16[128,128]{1,0:T(8,128)(2,1)S(1)} collective-permute-done((bf16[128,128]{1,0:T(8,128)(2,1)S(1)}, bf16[128,128]{1,0:T(8,128)(2,1)S(1)}, u32[]{:S(2)}, u32[]{:S(2)}) %collective-permute-start) | collective-permute-done | bytes 32800 | tf_op jit(solution)/shard_map/ppermute | solution.py:176
  23.4 1.8 %collective-permute-done.3 = bf16[512,128]{1,0:T(8,128)(2,1)S(1)} collective-permute-done((bf16[512,128]{1,0:T(8,128)(2,1)S(1)}, bf16[512,128]{1,0:T(8,128)(2,1)S(1)}, u32[]{:S(2)}, u32[]{:S(2)}) %collective-permute-start.3) | collective-permute-done | bytes 131104 | tf_op jit(solution)/shard_map/ppermute | solution.py:186
  27.0 2.7 %collective-permute-start.6 = (bf16[1024,128]{1,0:T(8,128)(2,1)S(1)}, bf16[1024,128]{1,0:T(8,128)(2,1)S(1)}, u32[]{:S(2)}, u32[]{:S(2)}) collective-permute-start(bf16[1024,128]{1,0:T(8,128)(2,1)S(1)} %pad_maximum_fusion.2), channel_id=1, source_target_pairs={{0,8},{2,3},{16,24},{18,19},{1,9},{3,2},{17,25},{19,18},{4,12},{6,... | collective-permute-start | bytes 786440 | tf_op jit(solution)/shard_map/ppermute | solution.py:161
  31.9 5.1 %collective-permute-done.6 = bf16[1024,128]{1,0:T(8,128)(2,1)S(1)} collective-permute-done((bf16[1024,128]{1,0:T(8,128)(2,1)S(1)}, bf16[1024,128]{1,0:T(8,128)(2,1)S(1)}, u32[]{:S(2)}, u32[]{:S(2)}) %collective-permute-start.6) | collective-permute-done | bytes 262176 | tf_op jit(solution)/shard_map/ppermute | solution.py:161
  37.0 2.7 %collective-permute-done.7 = bf16[1024,128]{1,0:T(8,128)(2,1)S(1)} collective-permute-done((bf16[1024,128]{1,0:T(8,128)(2,1)S(1)}, bf16[1024,128]{1,0:T(8,128)(2,1)S(1)}, u32[]{:S(2)}, u32[]{:S(2)}) %collective-permute-start.7) | collective-permute-done | bytes 262176 | tf_op jit(solution)/shard_map/ppermute | solution.py:161
  39.7 3.1 %collective-permute-start.10 = (bf16[4096,128]{1,0:T(8,128)(2,1)S(1)}, bf16[4096,128]{1,0:T(8,128)(2,1)S(1)}, u32[]{:S(2)}, u32[]{:S(2)}) collective-permute-start(bf16[4096,128]{1,0:T(8,128)(2,1)S(1)} %constant_dynamic-update-slice_fusion.refs_0_), channel_id=1, source_target_pairs={{0,17},{2,14},{16,1},{18,30},{1,16},{3,15},{17,0},{19,31},{4,21},{... | collective-permute-start | bytes 3145736 | tf_op jit(solution)/shard_map/ppermute | solution.py:161
  43.9 25.0 %all-gather.2.cloned.1.call-done = bf16[128,2,2048]{2,0,1:T(8,128)(2,1)} async-done(((bf16[128,2,128]{2,0,1:T(8,128)(2,1)}), bf16[128,2,2048]{2,0,1:T(8,128)(2,1)}) %all-gather.2.cloned.1.call-update) | async-done | bytes 1048592 | tf_op jit(solution)/shard_map/all_gather | solution.py:247
  68.9 2.8 %fusion.6 = bf16[128,2,128]{2,0,1:T(8,128)(2,1)S(1)} fusion(bf16[2,16,2,8,2048]{4,3,2,1,0:T(8,128)(2,1)} %bitcast.41, bf16[128,2,2048]{2,0,1:T(8,128)(2,1)} %all-gather.2.cloned.1.call-done), kind=kOutput, calls=%fused_computation.4 | convolution fusion | flops 268468224 | bytes 3211264 | tf_op jit(solution)/shard_map/tjq,bcjq->tbc/dot_general | solution.py:248
  74.6 3.2 %collective-permute-done.12.refs_5_ = bf16[4096,128]{1,0:T(8,128)(2,1)} collective-permute-done((bf16[4096,128]{1,0:T(8,128)(2,1)}, bf16[4096,128]{1,0:T(8,128)(2,1)}, u32[]{:S(2)}, u32[]{:S(2)}) %collective-permute-start.12) | collective-permute-done | bytes 1048608 | tf_op jit(solution)/shard_map/ppermute | solution.py:144
  79.1 18.2 %whiten.1 = bf16[64,2048]{1,0:T(8,128)(2,1)S(1)} custom-call(s32[6]{0:T(128)S(1)} %stack.52.where, bf16[4096,128]{1,0:T(8,128)(2,1)S(1)} %constant_dynamic-update-slice_fusion.refs_0_, bf16[4096,128]{1,0:T(8,128)(2,1)} %collective-permute-done.8.refs_1_, bf16[4096,128]{1,0:T(8,128)(2,1)S(1)} %collective-permute-done.9.refs_2_, ...), custom_call_target="tpu_custom_call" | custom-call | flops 9663676416 | bytes 8388608 | tf_op jit(solution)/shard_map/whiten/pallas_call | solution.py:123
  97.3 16.3 %collective-permute-start.15 = (bf16[64,2048]{1,0:T(8,128)(2,1)S(1)}, bf16[64,2048]{1,0:T(8,128)(2,1)S(1)}, u32[]{:S(2)}, u32[]{:S(2)}) collective-permute-start(bf16[64,2048]{1,0:T(8,128)(2,1)S(1)} %whiten.1), channel_id=1, source_target_pairs={{0,32},{32,0},{64,96},{96,64},{128,160},{160,128},{192,224},{224,1... | collective-permute-start | bytes 786440 | tf_op jit(solution)/shard_map/ppermute | solution.py:144
  113.6 6.6 %collective-permute-done.15 = bf16[64,2048]{1,0:T(8,128)(2,1)S(1)} collective-permute-done((bf16[64,2048]{1,0:T(8,128)(2,1)S(1)}, bf16[64,2048]{1,0:T(8,128)(2,1)S(1)}, u32[]{:S(2)}, u32[]{:S(2)}) %collective-permute-start.15) | collective-permute-done | bytes 262176 | tf_op jit(solution)/shard_map/ppermute | solution.py:144
  120.2 3.6 %collective-permute-start.21 = (bf16[32,2048]{1,0:T(8,128)(2,1)S(1)}, bf16[32,2048]{1,0:T(8,128)(2,1)S(1)}, u32[]{:S(2)}, u32[]{:S(2)}) collective-permute-start(bf16[32,2048]{1,0:T(8,128)(2,1)S(1)} %slice_select_fusion), channel_id=1, source_target_pairs={{0,17},{16,1},{1,16},{17,0},{2,19},{18,3},{3,18},{19,2},{4,21},{20... | collective-permute-start | bytes 393224 | tf_op jit(solution)/shard_map/ppermute | solution.py:149
  124.8 4.4 %collective-permute-done.21 = bf16[32,2048]{1,0:T(8,128)(2,1)S(1)} collective-permute-done((bf16[32,2048]{1,0:T(8,128)(2,1)S(1)}, bf16[32,2048]{1,0:T(8,128)(2,1)S(1)}, u32[]{:S(2)}, u32[]{:S(2)}) %collective-permute-start.21) | collective-permute-done | bytes 131104 | tf_op jit(solution)/shard_map/ppermute | solution.py:149
  129.2 2.3 %collective-permute-done.20 = bf16[32,2048]{1,0:T(8,128)(2,1)S(1)} collective-permute-done((bf16[32,2048]{1,0:T(8,128)(2,1)S(1)}, bf16[32,2048]{1,0:T(8,128)(2,1)S(1)}, u32[]{:S(2)}, u32[]{:S(2)}) %collective-permute-start.20) | collective-permute-done | bytes 131104 | tf_op jit(solution)/shard_map/ppermute | solution.py:149
  131.8 1.9 %collective-permute-start.17 = (bf16[64,2048]{1,0:T(8,128)(2,1)S(1)}, bf16[64,2048]{1,0:T(8,128)(2,1)S(1)}, u32[]{:S(2)}, u32[]{:S(2)}) collective-permute-start(bf16[64,2048]{1,0:T(8,128)(2,1)S(1)} %broadcast_select_fusion), channel_id=1, source_target_pairs={{0,8},{4,12},{8,0},{12,4},{1,9},{5,13},{9,1},{13,5},{2,10},{6,14},... | collective-permute-start | bytes 786440 | tf_op jit(solution)/shard_map/ppermute | solution.py:144
  133.7 2.2 %collective-permute-start.16 = (bf16[64,2048]{1,0:T(8,128)(2,1)S(1)}, bf16[64,2048]{1,0:T(8,128)(2,1)S(1)}, u32[]{:S(2)}, u32[]{:S(2)}) collective-permute-start(bf16[64,2048]{1,0:T(8,128)(2,1)S(1)} %broadcast_select_fusion), channel_id=1, source_target_pairs={{0,4},{4,0},{8,12},{12,8},{1,5},{5,1},{9,13},{13,9},{2,6},{6,2},{1... | collective-permute-start | bytes 786440 | tf_op jit(solution)/shard_map/ppermute | solution.py:144
  135.9 11.4 %collective-permute-done.18 = bf16[64,2048]{1,0:T(8,128)(2,1)S(1)} collective-permute-done((bf16[64,2048]{1,0:T(8,128)(2,1)S(1)}, bf16[64,2048]{1,0:T(8,128)(2,1)S(1)}, u32[]{:S(2)}, u32[]{:S(2)}) %collective-permute-start.18) | collective-permute-done | bytes 262176 | tf_op jit(solution)/shard_map/ppermute | solution.py:144
  149.1 4.2 %collective-permute-start.23 = (bf16[256,128]{1,0:T(8,128)(2,1)S(1)}, bf16[256,128]{1,0:T(8,128)(2,1)S(1)}, u32[]{:S(2)}, u32[]{:S(2)}) collective-permute-start(bf16[256,128]{1,0:T(8,128)(2,1)S(1)} %get-tuple-element.29), channel_id=1, source_target_pairs={{0,0},{2,32},{16,64},{18,96},{32,16},{34,48},{48,80},{50,112},{64,... | collective-permute-start | bytes 196616 | tf_op jit(solution)/shard_map/ppermute | solution.py:286
  153.3 2.0 %collective-permute-start.24 = (bf16[256,128]{1,0:T(8,128)(2,1)S(1)}, bf16[256,128]{1,0:T(8,128)(2,1)S(1)}, u32[]{:S(2)}, u32[]{:S(2)}) collective-permute-start(bf16[256,128]{1,0:T(8,128)(2,1)S(1)} %get-tuple-element.30), channel_id=1, source_target_pairs={{0,2},{2,34},{16,66},{18,98},{32,18},{34,50},{48,82},{50,114},{64,... | collective-permute-start | bytes 196616 | tf_op jit(solution)/shard_map/ppermute | solution.py:286
  156.0 2.4 %collective-permute-done.23 = bf16[256,128]{1,0:T(8,128)(2,1)S(1)} collective-permute-done((bf16[256,128]{1,0:T(8,128)(2,1)S(1)}, bf16[256,128]{1,0:T(8,128)(2,1)S(1)}, u32[]{:S(2)}, u32[]{:S(2)}) %collective-permute-start.23) | collective-permute-done | bytes 65568 | tf_op jit(solution)/shard_map/ppermute | solution.py:286
  158.5 5.9 %collective-permute-done.24 = bf16[256,128]{1,0:T(8,128)(2,1)S(1)} collective-permute-done((bf16[256,128]{1,0:T(8,128)(2,1)S(1)}, bf16[256,128]{1,0:T(8,128)(2,1)S(1)}, u32[]{:S(2)}, u32[]{:S(2)}) %collective-permute-start.24) | collective-permute-done | bytes 65568 | tf_op jit(solution)/shard_map/ppermute | solution.py:286
  (57 shorter events, 19.7 us)
Async XLA Ops:
  7.2 61.8 %all-gather.2.cloned.1.call-start = ((), (), s32[]{:S(2)}) async-start(), calls=%async_computation | async-start | bytes 1114112 | tf_op jit(solution)/shard_map/all_gather | solution.py:247
  9.2 9.6 %collective-permute-start.2 = (bf16[128,128]{1,0:T(8,128)(2,1)S(1)}, bf16[128,128]{1,0:T(8,128)(2,1)S(1)}, u32[]{:S(2)}, u32[]{:S(2)}) collective-permute-start(bf16[128,128]{1,0:T(8,128)(2,1)S(1)} %select_bitcast_fusion.2), channel_id=1, source_target_pairs={{0,192},{32,224},{64,0},{96,32},{128,64},{160,96},{192,128},{224,1... | collective-permute-start | bytes 98312 | tf_op jit(solution)/shard_map/ppermute | solution.py:176
  10.7 8.1 %collective-permute-start.1 = (bf16[128,128]{1,0:T(8,128)(2,1)S(1)}, bf16[128,128]{1,0:T(8,128)(2,1)S(1)}, u32[]{:S(2)}, u32[]{:S(2)}) collective-permute-start(bf16[128,128]{1,0:T(8,128)(2,1)S(1)} %select_bitcast_fusion.3), channel_id=1, source_target_pairs={{0,128},{32,160},{64,192},{96,224},{128,0},{160,32},{192,64},{224,... | collective-permute-start | bytes 98312 | tf_op jit(solution)/shard_map/ppermute | solution.py:176
  16.1 4.8 %collective-permute-start = (bf16[128,128]{1,0:T(8,128)(2,1)S(1)}, bf16[128,128]{1,0:T(8,128)(2,1)S(1)}, u32[]{:S(2)}, u32[]{:S(2)}) collective-permute-start(bf16[128,128]{1,0:T(8,128)(2,1)S(1)} %get-tuple-element.24), channel_id=1, source_target_pairs={{0,64},{32,96},{64,128},{96,160},{128,192},{160,224},{192,0},{224,... | collective-permute-start | bytes 98312 | tf_op jit(solution)/shard_map/ppermute | solution.py:176
  21.0 4.3 %collective-permute-start.3 = (bf16[512,128]{1,0:T(8,128)(2,1)S(1)}, bf16[512,128]{1,0:T(8,128)(2,1)S(1)}, u32[]{:S(2)}, u32[]{:S(2)}) collective-permute-start(bf16[512,128]{1,0:T(8,128)(2,1)S(1)} %pad_maximum_fusion.3), channel_id=1, source_target_pairs={{0,224},{2,0},{32,34},{34,66},{64,32},{66,64},{96,98},{98,130},{12... | collective-permute-start | bytes 393224 | tf_op jit(solution)/shard_map/ppermute | solution.py:186
  25.4 6.5 %collective-permute-start.5 = (bf16[1024,128]{1,0:T(8,128)(2,1)S(1)}, bf16[1024,128]{1,0:T(8,128)(2,1)S(1)}, u32[]{:S(2)}, u32[]{:S(2)}) collective-permute-start(bf16[1024,128]{1,0:T(8,128)(2,1)S(1)} %pad_maximum_fusion.2), channel_id=1, source_target_pairs={{0,4},{2,18},{16,20},{18,2},{1,5},{3,19},{17,21},{19,3},{4,0},{6,2... | collective-permute-start | bytes 786440 | tf_op jit(solution)/shard_map/ppermute | solution.py:161
  27.0 10.0 %collective-permute-start.6 = (bf16[1024,128]{1,0:T(8,128)(2,1)S(1)}, bf16[1024,128]{1,0:T(8,128)(2,1)S(1)}, u32[]{:S(2)}, u32[]{:S(2)}) collective-permute-start(bf16[1024,128]{1,0:T(8,128)(2,1)S(1)} %pad_maximum_fusion.2), channel_id=1, source_target_pairs={{0,8},{2,3},{16,24},{18,19},{1,9},{3,2},{17,25},{19,18},{4,12},{6,... | collective-permute-start | bytes 786440 | tf_op jit(solution)/shard_map/ppermute | solution.py:161
  29.7 10.0 %collective-permute-start.7 = (bf16[1024,128]{1,0:T(8,128)(2,1)S(1)}, bf16[1024,128]{1,0:T(8,128)(2,1)S(1)}, u32[]{:S(2)}, u32[]{:S(2)}) collective-permute-start(bf16[1024,128]{1,0:T(8,128)(2,1)S(1)} %pad_maximum_fusion.2), channel_id=1, source_target_pairs={{0,12},{2,19},{16,28},{18,3},{1,13},{3,18},{17,29},{19,2},{4,8},{6... | collective-permute-start | bytes 786440 | tf_op jit(solution)/shard_map/ppermute | solution.py:161
  39.7 32.0 %collective-permute-start.10 = (bf16[4096,128]{1,0:T(8,128)(2,1)S(1)}, bf16[4096,128]{1,0:T(8,128)(2,1)S(1)}, u32[]{:S(2)}, u32[]{:S(2)}) collective-permute-start(bf16[4096,128]{1,0:T(8,128)(2,1)S(1)} %constant_dynamic-update-slice_fusion.refs_0_), channel_id=1, source_target_pairs={{0,17},{2,14},{16,1},{18,30},{1,16},{3,15},{17,0},{19,31},{4,21},{... | collective-permute-start | bytes 3145736 | tf_op jit(solution)/shard_map/ppermute | solution.py:161
  42.8 28.9 %collective-permute-start.9 = (bf16[4096,128]{1,0:T(8,128)(2,1)S(1)}, bf16[4096,128]{1,0:T(8,128)(2,1)S(1)}, u32[]{:S(2)}, u32[]{:S(2)}) collective-permute-start(bf16[4096,128]{1,0:T(8,128)(2,1)S(1)} %constant_dynamic-update-slice_fusion.refs_0_), channel_id=1, source_target_pairs={{0,1},{2,10},{16,17},{18,26},{1,0},{3,11},{17,16},{19,27},{4,5},{6... | collective-permute-start | bytes 3145736 | tf_op jit(solution)/shard_map/ppermute | solution.py:161
  43.4 28.3 %collective-permute-start.8 = (bf16[4096,128]{1,0:T(8,128)(2,1)S(1)}, bf16[4096,128]{1,0:T(8,128)(2,1)}, u32[]{:S(2)}, u32[]{:S(2)}) collective-permute-start(bf16[4096,128]{1,0:T(8,128)(2,1)S(1)} %constant_dynamic-update-slice_fusion.refs_0_), channel_id=1, source_target_pairs={{0,16},{2,6},{16,0},{18,22},{1,17},{3,7},{17,1},{19,23},{4,20},{6,... | collective-permute-start | bytes 3145736 | tf_op jit(solution)/shard_map/ppermute | solution.py:161
  72.0 5.8 %collective-permute-start.12 = (bf16[4096,128]{1,0:T(8,128)(2,1)}, bf16[4096,128]{1,0:T(8,128)(2,1)}, u32[]{:S(2)}, u32[]{:S(2)}) collective-permute-start(bf16[4096,128]{1,0:T(8,128)(2,1)} %collective-permute-done.8.refs_1_), channel_id=1, source_target_pairs={{0,2},{2,0},{1,3},{3,1},{4,6},{6,4},{5,7},{7,5},{8,10},{10,8},{9,1... | collective-permute-start | bytes 3145736 | tf_op jit(solution)/shard_map/ppermute | solution.py:144
  72.3 5.5 %collective-permute-start.13 = (bf16[4096,128]{1,0:T(8,128)(2,1)S(1)}, bf16[4096,128]{1,0:T(8,128)(2,1)}, u32[]{:S(2)}, u32[]{:S(2)}) collective-permute-start(bf16[4096,128]{1,0:T(8,128)(2,1)S(1)} %collective-permute-done.9.refs_2_), channel_id=1, source_target_pairs={{0,2},{2,0},{1,3},{3,1},{4,6},{6,4},{5,7},{7,5},{8,10},{10,8},{9,1... | collective-permute-start | bytes 3145736 | tf_op jit(solution)/shard_map/ppermute | solution.py:144
  72.6 6.5 %collective-permute-start.14 = (bf16[4096,128]{1,0:T(8,128)(2,1)S(1)}, bf16[4096,128]{1,0:T(8,128)(2,1)}, u32[]{:S(2)}, u32[]{:S(2)}) collective-permute-start(bf16[4096,128]{1,0:T(8,128)(2,1)S(1)} %collective-permute-done.10.refs_3_), channel_id=1, source_target_pairs={{0,2},{2,0},{1,3},{3,1},{4,6},{6,4},{5,7},{7,5},{8,10},{10,8},{9,1... | collective-permute-start | bytes 3145736 | tf_op jit(solution)/shard_map/ppermute | solution.py:144
  97.3 22.9 %collective-permute-start.15 = (bf16[64,2048]{1,0:T(8,128)(2,1)S(1)}, bf16[64,2048]{1,0:T(8,128)(2,1)S(1)}, u32[]{:S(2)}, u32[]{:S(2)}) collective-permute-start(bf16[64,2048]{1,0:T(8,128)(2,1)S(1)} %whiten.1), channel_id=1, source_target_pairs={{0,32},{32,0},{64,96},{96,64},{128,160},{160,128},{192,224},{224,1... | collective-permute-start | bytes 786440 | tf_op jit(solution)/shard_map/ppermute | solution.py:144
  120.2 9.0 %collective-permute-start.21 = (bf16[32,2048]{1,0:T(8,128)(2,1)S(1)}, bf16[32,2048]{1,0:T(8,128)(2,1)S(1)}, u32[]{:S(2)}, u32[]{:S(2)}) collective-permute-start(bf16[32,2048]{1,0:T(8,128)(2,1)S(1)} %slice_select_fusion), channel_id=1, source_target_pairs={{0,17},{16,1},{1,16},{17,0},{2,19},{18,3},{3,18},{19,2},{4,21},{20... | collective-permute-start | bytes 393224 | tf_op jit(solution)/shard_map/ppermute | solution.py:149
  123.8 7.7 %collective-permute-start.20 = (bf16[32,2048]{1,0:T(8,128)(2,1)S(1)}, bf16[32,2048]{1,0:T(8,128)(2,1)S(1)}, u32[]{:S(2)}, u32[]{:S(2)}) collective-permute-start(bf16[32,2048]{1,0:T(8,128)(2,1)S(1)} %slice_select_fusion), channel_id=1, source_target_pairs={{0,1},{16,17},{1,0},{17,16},{2,3},{18,19},{3,2},{19,18},{4,5},{20,... | collective-permute-start | bytes 393224 | tf_op jit(solution)/shard_map/ppermute | solution.py:149
  124.1 7.3 %collective-permute-start.19 = (bf16[32,2048]{1,0:T(8,128)(2,1)S(1)}, bf16[32,2048]{1,0:T(8,128)(2,1)S(1)}, u32[]{:S(2)}, u32[]{:S(2)}) collective-permute-start(bf16[32,2048]{1,0:T(8,128)(2,1)S(1)} %slice_select_fusion), channel_id=1, source_target_pairs={{0,16},{16,0},{1,17},{17,1},{2,18},{18,2},{3,19},{19,3},{4,20},{20... | collective-permute-start | bytes 393224 | tf_op jit(solution)/shard_map/ppermute | solution.py:149
  131.5 16.5 %collective-permute-start.22 = (bf16[128,2048]{1,0:T(8,128)(2,1)S(1)}, bf16[128,2048]{1,0:T(8,128)(2,1)S(1)}, u32[]{:S(2)}, u32[]{:S(2)}) collective-permute-start(bf16[128,2048]{1,0:T(8,128)(2,1)S(1)} %pad_maximum_fusion.1.own), channel_id=1, source_target_pairs={{0,2},{2,0},{1,3},{3,1},{4,6},{6,4},{5,7},{7,5},{8,10},{10,8},{9,1... | collective-permute-start | bytes 1572872 | tf_op jit(solution)/shard_map/ppermute | solution.py:144
  131.7 15.6 %collective-permute-start.18 = (bf16[64,2048]{1,0:T(8,128)(2,1)S(1)}, bf16[64,2048]{1,0:T(8,128)(2,1)S(1)}, u32[]{:S(2)}, u32[]{:S(2)}) collective-permute-start(bf16[64,2048]{1,0:T(8,128)(2,1)S(1)} %broadcast_select_fusion), channel_id=1, source_target_pairs={{0,12},{4,8},{8,4},{12,0},{1,13},{5,9},{9,5},{13,1},{2,14},{6,10},... | collective-permute-start | bytes 786440 | tf_op jit(solution)/shard_map/ppermute | solution.py:144
  131.8 15.5 %collective-permute-start.17 = (bf16[64,2048]{1,0:T(8,128)(2,1)S(1)}, bf16[64,2048]{1,0:T(8,128)(2,1)S(1)}, u32[]{:S(2)}, u32[]{:S(2)}) collective-permute-start(bf16[64,2048]{1,0:T(8,128)(2,1)S(1)} %broadcast_select_fusion), channel_id=1, source_target_pairs={{0,8},{4,12},{8,0},{12,4},{1,9},{5,13},{9,1},{13,5},{2,10},{6,14},... | collective-permute-start | bytes 786440 | tf_op jit(solution)/shard_map/ppermute | solution.py:144
  133.7 14.3 %collective-permute-start.16 = (bf16[64,2048]{1,0:T(8,128)(2,1)S(1)}, bf16[64,2048]{1,0:T(8,128)(2,1)S(1)}, u32[]{:S(2)}, u32[]{:S(2)}) collective-permute-start(bf16[64,2048]{1,0:T(8,128)(2,1)S(1)} %broadcast_select_fusion), channel_id=1, source_target_pairs={{0,4},{4,0},{8,12},{12,8},{1,5},{5,1},{9,13},{13,9},{2,6},{6,2},{1... | collective-permute-start | bytes 786440 | tf_op jit(solution)/shard_map/ppermute | solution.py:144
  149.1 9.4 %collective-permute-start.23 = (bf16[256,128]{1,0:T(8,128)(2,1)S(1)}, bf16[256,128]{1,0:T(8,128)(2,1)S(1)}, u32[]{:S(2)}, u32[]{:S(2)}) collective-permute-start(bf16[256,128]{1,0:T(8,128)(2,1)S(1)} %get-tuple-element.29), channel_id=1, source_target_pairs={{0,0},{2,32},{16,64},{18,96},{32,16},{34,48},{48,80},{50,112},{64,... | collective-permute-start | bytes 196616 | tf_op jit(solution)/shard_map/ppermute | solution.py:286
  153.3 11.1 %collective-permute-start.24 = (bf16[256,128]{1,0:T(8,128)(2,1)S(1)}, bf16[256,128]{1,0:T(8,128)(2,1)S(1)}, u32[]{:S(2)}, u32[]{:S(2)}) collective-permute-start(bf16[256,128]{1,0:T(8,128)(2,1)S(1)} %get-tuple-element.30), channel_id=1, source_target_pairs={{0,2},{2,34},{16,66},{18,98},{32,18},{34,50},{48,82},{50,114},{64,... | collective-permute-start | bytes 196616 | tf_op jit(solution)/shard_map/ppermute | solution.py:286
  (3 other events, 20.0 us)
Sparse Core Ops, SparseCore 0:
  22.9 46.0 all-gather.1

commit v6 on v5

--- a/solution.py
+++ b/solution.py
@@ -29,8 +29,8 @@
 
 
 def chain_kernel(where, *refs):
-    pieces = refs[:8]
-    out, side, turned, now, later, f1, f2, f3, u1, u2, sems = refs[8:]
+    pieces = refs[:10]
+    out, side, turned, now, later, f1, f2, f3, u1, u2, sems = refs[10:]
     block, tokens = turned.shape
     half = COLUMNS // 2
     copies = []
@@ -105,7 +105,8 @@
         for outer in range(4):
             for inner in range(4):
                 for other in range(2):
-                    part = pieces[core * 4 + outer].at[pl.ds((inner * 2 + other) * 512, 512)]
+                    piece = core * 5 + outer + (outer == 3 or outer == 2 and inner >= 2)
+                    part = pieces[piece].at[pl.ds(((inner % 2 if outer == 2 else inner) * 2 + other) * 512, 512)]
 
                     def spot(x, y):
                         return y // 2 * 1024 + core * 512, (y % 2 * 8 + x * 2) * 128
@@ -124,7 +125,7 @@
         chain_kernel,
         name="whiten",
         out_shape=jax.ShapeDtypeStruct((COLUMNS, tokens), BF16),
-        in_specs=[pl.BlockSpec(memory_space=pltpu.SMEM)] + [pl.BlockSpec(memory_space=pl.ANY)] * 8,
+        in_specs=[pl.BlockSpec(memory_space=pltpu.SMEM)] + [pl.BlockSpec(memory_space=pl.ANY)] * 10,
         out_specs=pl.BlockSpec(memory_space=pltpu.VMEM),
         scratch_shapes=[
             pltpu.VMEM((tokens, block), BF16),
@@ -193,8 +194,9 @@
     masks = (1, 3, 2)
     step = {0: part, **{m: plane_swap(part, m, 0) for m in masks}}
     row = jnp.concatenate([step[m] for m in range(4)])
-    wide = {0: row, **{m: plane_swap(row, 0, m) for m in masks}}
-    return [wide[m] for m in range(4)]
+    one, three = plane_swap(row, 0, 1), plane_swap(row, 0, 3)
+    two = [plane_swap(one[:2048], 0, 3), plane_swap(three[2048:], 0, 1)]
+    return [row, one, *two, three]
 
 
 def tile_kernel(where, acts, own, other, out, grads):
@@ -225,6 +227,38 @@
     )(where, acts, own, other)
 
 
+def input_kernel(where, *refs):
+    parts, weight, out, grads = refs[:4], refs[4], refs[5], refs[6]
+    for x in range(4):
+        for yl in range(2):
+            for core in range(2):
+                spot = (yl ^ where[0]) * 1024 + (x ^ where[1]) * 256 + (core ^ where[2]) * 128
+                for side in range(2):
+                    row = ((yl * 2 + core) * 2 + side) * 128
+                    col = pl.multiple_of(side * 2048 + spot, 128)
+                    grads[:, pl.ds(col, 128)] = parts[x][row : row + 128, :]
+    product = lax.dot_general(grads[...], weight[...], (((1,), (1,)), ((), ())), preferred_element_type=F32)
+    for side in range(2):
+        out[side] = product[:, side * 128 : side * 128 + 128].astype(BF16)
+
+
+def grads_by_weight(where, parts, weight):
+    blocks, width, features = weight.shape
+    tokens = parts[0].shape[0] // 8
+    return pl.pallas_call(
+        input_kernel,
+        name="input_grad",
+        out_shape=jax.ShapeDtypeStruct((blocks, tokens, width), BF16),
+        in_specs=[pl.BlockSpec(memory_space=pltpu.SMEM)] + [pl.BlockSpec(memory_space=pltpu.VMEM)] * 5,
+        out_specs=pl.BlockSpec(memory_space=pltpu.VMEM),
+        scratch_shapes=[pltpu.VMEM((tokens, features), BF16)],
+        compiler_params=pltpu.CompilerParams(vmem_limit_bytes=16 * 2**20),
+        cost_estimate=pl.CostEstimate(
+            flops=2 * tokens * features * blocks * width, bytes_accessed=3 * 2**20, transcendentals=0
+        ),
+    )(where, *parts, weight.reshape(blocks * width, features))
+
+
 def owners(step):
     pairs = []
     for z in range(8):
@@ -244,15 +278,12 @@
     token_count = tok_dev * lax.axis_size("z") * lax.axis_size("yh")
 
     pieces = side_pieces(shared_part(activations, out_grads, z, c))
-    grads_whole = lax.all_gather(out_grads, ("yl", "x", "c"), axis=2, tiled=True)
-    input_grad = jnp.einsum(
-        "tjq,bcjq->tbc",
-        grads_whole,
-        weight.reshape(blocks, width, blocks, block),
-        preferred_element_type=F32,
-    ).astype(BF16)
-    pieces, input_grad = lax.optimization_barrier((pieces, input_grad))
-    pieces = pieces + [xor_swap(piece, "c", 1) for piece in pieces]
+    pieces += [xor_swap(piece, "c", 1) for piece in pieces]
+    near = jnp.concatenate([out_grads[:, 0], out_grads[:, 1]])
+    near = jnp.concatenate([near, xor_swap(near, "c", 1)])
+    near = jnp.concatenate([near, xor_swap(near, "yl", 1)])
+    near, pieces = lax.optimization_barrier((near, pieces))
+    over_x = [near] + [xor_swap(near, "x", m) for m in (1, 2, 3)]
 
     y = yh * 2 + yl
     is_act = (z + 1) // 2 % 2 == 0
@@ -274,6 +305,9 @@
         token_count,
     )
 
+    done, over_x = lax.optimization_barrier((done, over_x))
+    input_grad = grads_by_weight(jnp.stack([yl, x, c]).astype(jnp.int32), over_x, weight)
+
     swapped = xor_swap(done, "z", 1)
     grads = jnp.where(is_act, swapped[32:], done[:32])
     acts = jnp.where(is_act, done, swapped)
@@ -281,11 +315,12 @@
     acts = {0: acts, **{m: xor_swap(acts, "x", m) for m in (1, 3, 2)}}
     grads = jnp.concatenate([grads[m] for m in range(4)])
     acts = jnp.concatenate([acts[m] for m in range(4)])
+    grads, acts, input_grad = lax.optimization_barrier((grads, acts, input_grad))
     numbers = jnp.stack([y * 2 + c, x, z // 4]).astype(jnp.int32)
     tile = update_tile(numbers, acts, grads, xor_swap(grads, "c", 1))
     tile = [lax.ppermute(tile[step], ("z", "yl", "c"), owners(step)) for step in range(2)]
     update = jnp.stack([jnp.where(c == 0, tile[0], tile[1]), jnp.where(c == 0, tile[1], tile[0])], axis=1)
-    return update, input_grad
+    return update, input_grad.transpose(1, 0, 2)
 
 
 def solution(mesh):

time: 172 us -> 138 us (0.80)
  waiting for transfers between devices: 78.2 us -> 63.1 us
  between operations: 14.3 us -> 0.95 us
  starting transfers between devices: 53.5 us -> 49.1 us
  matrix products: 2.75 us -> 0 us
    all_gather x1 -> x0, waiting for transfers between devices: 25 us -> none  [local(): lax.all_gather(out_grads, ('yl', 'x', 'c'), axis=2, tiled=True)]
    ppermute x6 -> x7, waiting for transfers between devices: 9.42 us -> 30.9 us  [plane_swap(): return lax.ppermute(array, ('yl', 'x', 'c', 'yh'), pairs)]
    ppermute x9 -> x15, waiting for transfers between devices: 24.8 us -> 19 us  [xor_swap(): lax.ppermute(array, axis, [(i, i ^ mask) for i in range(lax.axis_size(axi...]
    ppermute x3, waiting for transfers between devices: 6.7 us -> 1.53 us  [y_swap(): return lax.ppermute(array, ('yl', 'yh'), pairs)]
    ppermute x9 -> x15, starting transfers between devices: 21.7 us -> 17.2 us  [xor_swap(): lax.ppermute(array, axis, [(i, i ^ mask) for i in range(lax.axis_size(axi...]
    dot_general x1 -> x0, matrix products: 2.75 us -> none  [local(): jnp.einsum('tjq,bcjq->tbc', grads_whole, weight.reshape(blocks, width, bl...]
    ppermute x6 -> x7, starting transfers between devices: 8.97 us -> 8.79 us  [plane_swap(): return lax.ppermute(array, ('yl', 'x', 'c', 'yh'), pairs)]
  transfers between devices with their start and end apart: 26 -> 32, of which waited for: 16 -> 19; matrix products, arithmetic and copies ran while one was open for 2% -> 1% of each run, Pallas kernels for 0% -> 14%
where the time goes in v6:
time: 138 us
  waiting for transfers between devices  63.1 us (46%)
  starting transfers between devices  49.1 us (36%)
  Pallas kernels  20.9 us (15%)
  local copies, waits for them, and re-layouts  2.94 us (2%)
    ppermute x7, waiting for transfers between devices, plane_swap(): return lax.ppermute(array, ('yl', 'x', 'c', 'yh'), pairs)  30.9 us
    ppermute x15, waiting for transfers between devices, xor_swap(): lax.ppermute(array, axis, [(i, i ^ mask) for i in range(lax.axis_size(axi...  19 us
    pallas_call x1, Pallas kernels, whitened_columns(): pl.pallas_call(chain_kernel, name='whiten', out_shape=jax.ShapeDtypeStruc...  18.2 us
    ppermute x15, starting transfers between devices, xor_swap(): lax.ppermute(array, axis, [(i, i ^ mask) for i in range(lax.axis_size(axi...  17.2 us
    ppermute x3, starting transfers between devices, shared_part(): lax.ppermute(pieces[shift], 'z', [(i, (i + 2 * shift) % 8) for i in range...  9.6 us
    ppermute x7, starting transfers between devices, plane_swap(): return lax.ppermute(array, ('yl', 'x', 'c', 'yh'), pairs)  8.79 us
    ppermute x2, waiting for transfers between devices, local(): lax.ppermute(tile[step], ('z', 'yl', 'c'), owners(step))  7.74 us
    ppermute x2, starting transfers between devices, local(): lax.ppermute(tile[step], ('z', 'yl', 'c'), owners(step))  6.91 us
  transfers between devices with their start and end apart: 32, of which 19 were waited for; matrix products, arithmetic and copies ran while one was open for 1% of the time, Pallas kernels for 14%

profile of v6, /device:TPU:64, one launch (start us, length us, event | category | flops | bytes accessed | tf_op | source)
XLA Modules:
  0.0 137.6 jit_solution(5710186310453756671)
XLA Ops:
  3.4 5.5 %collective-permute-start.3 = (bf16[128,128]{1,0:T(8,128)(2,1)S(1)}, bf16[128,128]{1,0:T(8,128)(2,1)S(1)}, u32[]{:S(2)}, u32[]{:S(2)}) collective-permute-start(bf16[128,128]{1,0:T(8,128)(2,1)S(1)} %broadcast_select_fusion.8), channel_id=1, source_target_pairs={{0,128},{32,160},{64,192},{96,224},{128,0},{160,32},{192,64},{224,... | collective-permute-start | bytes 98312 | tf_op jit(solution)/shard_map/ppermute | solution.py:177
  8.9 2.7 %collective-permute-start.2 = (bf16[128,128]{1,0:T(8,128)(2,1)S(1)}, bf16[128,128]{1,0:T(8,128)(2,1)S(1)}, u32[]{:S(2)}, u32[]{:S(2)}) collective-permute-start(bf16[128,128]{1,0:T(8,128)(2,1)S(1)} %get-tuple-element.51), channel_id=1, source_target_pairs={{0,64},{32,96},{64,128},{96,160},{128,192},{160,224},{192,0},{224,... | collective-permute-start | bytes 98312 | tf_op jit(solution)/shard_map/ppermute | solution.py:177
  11.5 2.1 %collective-permute-done.2 = bf16[128,128]{1,0:T(8,128)(2,1)S(1)} collective-permute-done((bf16[128,128]{1,0:T(8,128)(2,1)S(1)}, bf16[128,128]{1,0:T(8,128)(2,1)S(1)}, u32[]{:S(2)}, u32[]{:S(2)}) %collective-permute-start.2) | collective-permute-done | bytes 32800 | tf_op jit(solution)/shard_map/ppermute | solution.py:177
  16.1 1.9 %collective-permute-done.5 = bf16[512,128]{1,0:T(8,128)(2,1)S(1)} collective-permute-done((bf16[512,128]{1,0:T(8,128)(2,1)S(1)}, bf16[512,128]{1,0:T(8,128)(2,1)S(1)}, u32[]{:S(2)}, u32[]{:S(2)}) %collective-permute-start.5) | collective-permute-done | bytes 131104 | tf_op jit(solution)/shard_map/ppermute | solution.py:187
  19.7 2.7 %collective-permute-start.8 = (bf16[1024,128]{1,0:T(8,128)(2,1)S(1)}, bf16[1024,128]{1,0:T(8,128)(2,1)S(1)}, u32[]{:S(2)}, u32[]{:S(2)}) collective-permute-start(bf16[1024,128]{1,0:T(8,128)(2,1)S(1)} %pad_maximum_fusion.3), channel_id=1, source_target_pairs={{0,8},{2,3},{16,24},{18,19},{1,9},{3,2},{17,25},{19,18},{4,12},{6,... | collective-permute-start | bytes 786440 | tf_op jit(solution)/shard_map/ppermute | solution.py:162
  24.6 5.1 %collective-permute-done.8 = bf16[1024,128]{1,0:T(8,128)(2,1)S(1)} collective-permute-done((bf16[1024,128]{1,0:T(8,128)(2,1)S(1)}, bf16[1024,128]{1,0:T(8,128)(2,1)S(1)}, u32[]{:S(2)}, u32[]{:S(2)}) %collective-permute-start.8) | collective-permute-done | bytes 262176 | tf_op jit(solution)/shard_map/ppermute | solution.py:162
  29.7 2.7 %collective-permute-done.9 = bf16[1024,128]{1,0:T(8,128)(2,1)S(1)} collective-permute-done((bf16[1024,128]{1,0:T(8,128)(2,1)S(1)}, bf16[1024,128]{1,0:T(8,128)(2,1)S(1)}, u32[]{:S(2)}, u32[]{:S(2)}) %collective-permute-start.9) | collective-permute-done | bytes 262176 | tf_op jit(solution)/shard_map/ppermute | solution.py:162
  32.4 3.1 %collective-permute-start.12 = (bf16[4096,128]{1,0:T(8,128)(2,1)S(1)}, bf16[4096,128]{1,0:T(8,128)(2,1)S(1)}, u32[]{:S(2)}, u32[]{:S(2)}) collective-permute-start(bf16[4096,128]{1,0:T(8,128)(2,1)S(1)} %constant_dynamic-update-slice_fusion.refs_0_), channel_id=1, source_target_pairs={{0,17},{2,14},{16,1},{18,30},{1,16},{3,15},{17,0},{19,31},{4,21},{... | collective-permute-start | bytes 3145736 | tf_op jit(solution)/shard_map/ppermute | solution.py:162
  38.9 9.6 %collective-permute-done.12.refs_4_ = bf16[4096,128]{1,0:T(8,128)(2,1)S(1)} collective-permute-done((bf16[4096,128]{1,0:T(8,128)(2,1)S(1)}, bf16[4096,128]{1,0:T(8,128)(2,1)S(1)}, u32[]{:S(2)}, u32[]{:S(2)}) %collective-permute-start.12) | collective-permute-done | bytes 1048608 | tf_op jit(solution)/shard_map/ppermute | solution.py:162
  49.0 2.7 %collective-permute-done.10.refs_1_ = bf16[4096,128]{1,0:T(8,128)(2,1)S(1)} collective-permute-done((bf16[4096,128]{1,0:T(8,128)(2,1)S(1)}, bf16[4096,128]{1,0:T(8,128)(2,1)S(1)}, u32[]{:S(2)}, u32[]{:S(2)}) %collective-permute-start.10) | collective-permute-done | bytes 1048608 | tf_op jit(solution)/shard_map/ppermute | solution.py:162
  53.2 5.7 %collective-permute-done.13.refs_3_ = bf16[2048,128]{1,0:T(8,128)(2,1)} collective-permute-done((bf16[2048,128]{1,0:T(8,128)(2,1)S(1)}, bf16[2048,128]{1,0:T(8,128)(2,1)}, u32[]{:S(2)}, u32[]{:S(2)}) %collective-permute-start.13) | collective-permute-done | bytes 524320 | tf_op jit(solution)/shard_map/ppermute | solution.py:162
  58.9 3.5 %collective-permute-done.11.refs_2_ = bf16[2048,128]{1,0:T(8,128)(2,1)} collective-permute-done((bf16[2048,128]{1,0:T(8,128)(2,1)S(1)}, bf16[2048,128]{1,0:T(8,128)(2,1)}, u32[]{:S(2)}, u32[]{:S(2)}) %collective-permute-start.11) | collective-permute-done | bytes 524320 | tf_op jit(solution)/shard_map/ppermute | solution.py:162
  62.5 2.1 %collective-permute-done.16.refs_7_ = bf16[2048,128]{1,0:T(8,128)(2,1)} collective-permute-done((bf16[2048,128]{1,0:T(8,128)(2,1)}, bf16[2048,128]{1,0:T(8,128)(2,1)}, u32[]{:S(2)}, u32[]{:S(2)}) %collective-permute-start.16) | collective-permute-done | bytes 524320 | tf_op jit(solution)/shard_map/ppermute | solution.py:145
  66.1 2.6 %collective-permute-start.19 = (bf16[1024,128]{1,0:T(8,128)(2,1)S(1)}, bf16[1024,128]{1,0:T(8,128)(2,1)S(1)}, u32[]{:S(2)}, u32[]{:S(2)}) collective-permute-start(bf16[1024,128]{1,0:T(8,128)(2,1)S(1)} %pad_maximum_fusion.2.refs_0_), channel_id=1, source_target_pairs={{0,4},{4,0},{8,12},{12,8},{1,5},{5,1},{9,13},{13,9},{2,6},{6,2},{1... | collective-permute-start | bytes 786440 | tf_op jit(solution)/shard_map/ppermute | solution.py:145
  68.7 18.2 %whiten.1 = bf16[64,2048]{1,0:T(8,128)(2,1)S(1)} custom-call(s32[6]{0:T(128)S(1)} %stack.60.where, bf16[4096,128]{1,0:T(8,128)(2,1)S(1)} %constant_dynamic-update-slice_fusion.refs_0_, bf16[4096,128]{1,0:T(8,128)(2,1)S(1)} %collective-permute-done.10.refs_1_, bf16[2048,128]{1,0:T(8,128)(2,1)} %collective-permute-done.11.refs_2_, ...), custom_call_target="tpu_custom_call" | custom-call | flops 9663676416 | bytes 8388608 | tf_op jit(solution)/shard_map/whiten/pallas_call | solution.py:124
  86.9 7.7 %collective-permute-start.22 = (bf16[64,2048]{1,0:T(8,128)(2,1)S(1)}, bf16[64,2048]{1,0:T(8,128)(2,1)S(1)}, u32[]{:S(2)}, u32[]{:S(2)}) collective-permute-start(bf16[64,2048]{1,0:T(8,128)(2,1)S(1)} %whiten.1), channel_id=1, source_target_pairs={{0,32},{32,0},{64,96},{96,64},{128,160},{160,128},{192,224},{224,1... | collective-permute-start | bytes 786440 | tf_op jit(solution)/shard_map/ppermute | solution.py:145
  94.7 5.7 %collective-permute-done.22 = bf16[64,2048]{1,0:T(8,128)(2,1)S(1)} collective-permute-done((bf16[64,2048]{1,0:T(8,128)(2,1)S(1)}, bf16[64,2048]{1,0:T(8,128)(2,1)S(1)}, u32[]{:S(2)}, u32[]{:S(2)}) %collective-permute-start.22) | collective-permute-done | bytes 262176 | tf_op jit(solution)/shard_map/ppermute | solution.py:145
  101.6 3.0 %collective-permute-start.23 = (bf16[32,2048]{1,0:T(8,128)(2,1)S(1)}, bf16[32,2048]{1,0:T(8,128)(2,1)S(1)}, u32[]{:S(2)}, u32[]{:S(2)}) collective-permute-start(bf16[32,2048]{1,0:T(8,128)(2,1)S(1)} %slice_select_fusion), channel_id=1, source_target_pairs={{0,16},{16,0},{1,17},{17,1},{2,18},{18,2},{3,19},{19,3},{4,20},{20... | collective-permute-start | bytes 393224 | tf_op jit(solution)/shard_map/ppermute | solution.py:150
  105.0 2.1 %collective-permute-start.27 = (bf16[64,2048]{1,0:T(8,128)(2,1)S(1)}, bf16[64,2048]{1,0:T(8,128)(2,1)S(1)}, u32[]{:S(2)}, u32[]{:S(2)}) collective-permute-start(bf16[64,2048]{1,0:T(8,128)(2,1)S(1)} %broadcast_select_fusion), channel_id=1, source_target_pairs={{0,8},{4,12},{8,0},{12,4},{1,9},{5,13},{9,1},{13,5},{2,10},{6,14},... | collective-permute-start | bytes 786440 | tf_op jit(solution)/shard_map/ppermute | solution.py:145
  110.9 6.8 %collective-permute-done.28 = bf16[64,2048]{1,0:T(8,128)(2,1)S(1)} collective-permute-done((bf16[64,2048]{1,0:T(8,128)(2,1)S(1)}, bf16[64,2048]{1,0:T(8,128)(2,1)S(1)}, u32[]{:S(2)}, u32[]{:S(2)}) %collective-permute-start.28) | collective-permute-done | bytes 262176 | tf_op jit(solution)/shard_map/ppermute | solution.py:145
  118.5 1.8 %collective-permute-done.29.other = bf16[128,2048]{1,0:T(8,128)(2,1)S(1)} collective-permute-done((bf16[128,2048]{1,0:T(8,128)(2,1)S(1)}, bf16[128,2048]{1,0:T(8,128)(2,1)S(1)}, u32[]{:S(2)}, u32[]{:S(2)}) %collective-permute-start.29) | collective-permute-done | bytes 524320 | tf_op jit(solution)/shard_map/ppermute | solution.py:145
  121.4 4.1 %collective-permute-start.30 = (bf16[256,128]{1,0:T(8,128)(2,1)S(1)}, bf16[256,128]{1,0:T(8,128)(2,1)S(1)}, u32[]{:S(2)}, u32[]{:S(2)}) collective-permute-start(bf16[256,128]{1,0:T(8,128)(2,1)S(1)} %get-tuple-element.56), channel_id=1, source_target_pairs={{0,0},{2,32},{16,64},{18,96},{32,16},{34,48},{48,80},{50,112},{64,... | collective-permute-start | bytes 196616 | tf_op jit(solution)/shard_map/ppermute | solution.py:321
  125.5 2.8 %collective-permute-start.31 = (bf16[256,128]{1,0:T(8,128)(2,1)S(1)}, bf16[256,128]{1,0:T(8,128)(2,1)S(1)}, u32[]{:S(2)}, u32[]{:S(2)}) collective-permute-start(bf16[256,128]{1,0:T(8,128)(2,1)S(1)} %get-tuple-element.57), channel_id=1, source_target_pairs={{0,2},{2,34},{16,66},{18,98},{32,18},{34,50},{48,82},{50,114},{64,... | collective-permute-start | bytes 196616 | tf_op jit(solution)/shard_map/ppermute | solution.py:321
  130.4 6.3 %collective-permute-done.31 = bf16[256,128]{1,0:T(8,128)(2,1)S(1)} collective-permute-done((bf16[256,128]{1,0:T(8,128)(2,1)S(1)}, bf16[256,128]{1,0:T(8,128)(2,1)S(1)}, u32[]{:S(2)}, u32[]{:S(2)}) %collective-permute-start.31) | collective-permute-done | bytes 65568 | tf_op jit(solution)/shard_map/ppermute | solution.py:321
  (74 shorter events, 26.3 us)
Async XLA Ops:
  1.9 9.6 %collective-permute-start.4 = (bf16[128,128]{1,0:T(8,128)(2,1)S(1)}, bf16[128,128]{1,0:T(8,128)(2,1)S(1)}, u32[]{:S(2)}, u32[]{:S(2)}) collective-permute-start(bf16[128,128]{1,0:T(8,128)(2,1)S(1)} %broadcast_select_fusion.7), channel_id=1, source_target_pairs={{0,192},{32,224},{64,0},{96,32},{128,64},{160,96},{192,128},{224,1... | collective-permute-start | bytes 98312 | tf_op jit(solution)/shard_map/ppermute | solution.py:177
  3.4 8.1 %collective-permute-start.3 = (bf16[128,128]{1,0:T(8,128)(2,1)S(1)}, bf16[128,128]{1,0:T(8,128)(2,1)S(1)}, u32[]{:S(2)}, u32[]{:S(2)}) collective-permute-start(bf16[128,128]{1,0:T(8,128)(2,1)S(1)} %broadcast_select_fusion.8), channel_id=1, source_target_pairs={{0,128},{32,160},{64,192},{96,224},{128,0},{160,32},{192,64},{224,... | collective-permute-start | bytes 98312 | tf_op jit(solution)/shard_map/ppermute | solution.py:177
  19.7 10.0 %collective-permute-start.8 = (bf16[1024,128]{1,0:T(8,128)(2,1)S(1)}, bf16[1024,128]{1,0:T(8,128)(2,1)S(1)}, u32[]{:S(2)}, u32[]{:S(2)}) collective-permute-start(bf16[1024,128]{1,0:T(8,128)(2,1)S(1)} %pad_maximum_fusion.3), channel_id=1, source_target_pairs={{0,8},{2,3},{16,24},{18,19},{1,9},{3,2},{17,25},{19,18},{4,12},{6,... | collective-permute-start | bytes 786440 | tf_op jit(solution)/shard_map/ppermute | solution.py:162
  22.4 10.0 %collective-permute-start.9 = (bf16[1024,128]{1,0:T(8,128)(2,1)S(1)}, bf16[1024,128]{1,0:T(8,128)(2,1)S(1)}, u32[]{:S(2)}, u32[]{:S(2)}) collective-permute-start(bf16[1024,128]{1,0:T(8,128)(2,1)S(1)} %pad_maximum_fusion.3), channel_id=1, source_target_pairs={{0,12},{2,19},{16,28},{18,3},{1,13},{3,18},{17,29},{19,2},{4,8},{6... | collective-permute-start | bytes 786440 | tf_op jit(solution)/shard_map/ppermute | solution.py:162
  32.4 16.1 %collective-permute-start.12 = (bf16[4096,128]{1,0:T(8,128)(2,1)S(1)}, bf16[4096,128]{1,0:T(8,128)(2,1)S(1)}, u32[]{:S(2)}, u32[]{:S(2)}) collective-permute-start(bf16[4096,128]{1,0:T(8,128)(2,1)S(1)} %constant_dynamic-update-slice_fusion.refs_0_), channel_id=1, source_target_pairs={{0,17},{2,14},{16,1},{18,30},{1,16},{3,15},{17,0},{19,31},{4,21},{... | collective-permute-start | bytes 3145736 | tf_op jit(solution)/shard_map/ppermute | solution.py:162
  35.5 16.2 %collective-permute-start.10 = (bf16[4096,128]{1,0:T(8,128)(2,1)S(1)}, bf16[4096,128]{1,0:T(8,128)(2,1)S(1)}, u32[]{:S(2)}, u32[]{:S(2)}) collective-permute-start(bf16[4096,128]{1,0:T(8,128)(2,1)S(1)} %constant_dynamic-update-slice_fusion.refs_0_), channel_id=1, source_target_pairs={{0,16},{2,6},{16,0},{18,22},{1,17},{3,7},{17,1},{19,23},{4,20},{6,... | collective-permute-start | bytes 3145736 | tf_op jit(solution)/shard_map/ppermute | solution.py:162
  37.5 15.6 %collective-permute-start.1 = (bf16[512,128]{1,0:T(8,128)(2,1)S(1)}, bf16[512,128]{1,0:T(8,128)(2,1)S(1)}, u32[]{:S(2)}, u32[]{:S(2)}) collective-permute-start(bf16[512,128]{1,0:T(8,128)(2,1)S(1)} %pad_maximum_fusion.4), channel_id=1, source_target_pairs={{0,16},{16,0},{1,17},{17,1},{2,18},{18,2},{3,19},{19,3},{4,20},{20... | collective-permute-start | bytes 393224 | tf_op jit(solution)/shard_map/ppermute | solution.py:145
  38.9 23.6 %collective-permute-start.14 = (bf16[4096,128]{1,0:T(8,128)(2,1)S(1)}, bf16[4096,128]{1,0:T(8,128)(2,1)}, u32[]{:S(2)}, u32[]{:S(2)}) collective-permute-start(bf16[4096,128]{1,0:T(8,128)(2,1)S(1)} %constant_dynamic-update-slice_fusion.refs_0_), channel_id=1, source_target_pairs={{0,2},{2,0},{1,3},{3,1},{4,6},{6,4},{5,7},{7,5},{8,10},{10,8},{9,1... | collective-permute-start | bytes 3145736 | tf_op jit(solution)/shard_map/ppermute | solution.py:145
  48.6 10.3 %collective-permute-start.13 = (bf16[2048,128]{1,0:T(8,128)(2,1)S(1)}, bf16[2048,128]{1,0:T(8,128)(2,1)}, u32[]{:S(2)}, u32[]{:S(2)}) collective-permute-start(bf16[2048,128]{1,0:T(8,128)(2,1)S(1)} %slice.43), channel_id=1, source_target_pairs={{0,16},{2,6},{16,0},{18,22},{1,17},{3,7},{17,1},{19,23},{4,20},{6,... | collective-permute-start | bytes 1572872 | tf_op jit(solution)/shard_map/ppermute | solution.py:162
  51.8 10.6 %collective-permute-start.11 = (bf16[2048,128]{1,0:T(8,128)(2,1)S(1)}, bf16[2048,128]{1,0:T(8,128)(2,1)}, u32[]{:S(2)}, u32[]{:S(2)}) collective-permute-start(bf16[2048,128]{1,0:T(8,128)(2,1)S(1)} %slice.42), channel_id=1, source_target_pairs={{0,17},{2,14},{16,1},{18,30},{1,16},{3,15},{17,0},{19,31},{4,21},{... | collective-permute-start | bytes 1572872 | tf_op jit(solution)/shard_map/ppermute | solution.py:162
  52.1 10.4 %collective-permute-start.18 = (bf16[4096,128]{1,0:T(8,128)(2,1)S(1)}, bf16[4096,128]{1,0:T(8,128)(2,1)}, u32[]{:S(2)}, u32[]{:S(2)}) collective-permute-start(bf16[4096,128]{1,0:T(8,128)(2,1)S(1)} %collective-permute-done.12.refs_4_), channel_id=1, source_target_pairs={{0,2},{2,0},{1,3},{3,1},{4,6},{6,4},{5,7},{7,5},{8,10},{10,8},{9,1... | collective-permute-start | bytes 3145736 | tf_op jit(solution)/shard_map/ppermute | solution.py:145
  53.1 11.5 %collective-permute-start.15 = (bf16[4096,128]{1,0:T(8,128)(2,1)S(1)}, bf16[4096,128]{1,0:T(8,128)(2,1)}, u32[]{:S(2)}, u32[]{:S(2)}) collective-permute-start(bf16[4096,128]{1,0:T(8,128)(2,1)S(1)} %collective-permute-done.10.refs_1_), channel_id=1, source_target_pairs={{0,2},{2,0},{1,3},{3,1},{4,6},{6,4},{5,7},{7,5},{8,10},{10,8},{9,1... | collective-permute-start | bytes 3145736 | tf_op jit(solution)/shard_map/ppermute | solution.py:145
  64.6 22.3 %collective-permute-start.21 = (bf16[1024,128]{1,0:T(8,128)(2,1)S(1)}, bf16[1024,128]{1,0:T(8,128)(2,1)S(1)}, u32[]{:S(2)}, u32[]{:S(2)}) collective-permute-start(bf16[1024,128]{1,0:T(8,128)(2,1)S(1)} %pad_maximum_fusion.2.refs_0_), channel_id=1, source_target_pairs={{0,12},{4,8},{8,4},{12,0},{1,13},{5,9},{9,5},{13,1},{2,14},{6,10},... | collective-permute-start | bytes 786440 | tf_op jit(solution)/shard_map/ppermute | solution.py:145
  65.1 21.8 %collective-permute-start.20 = (bf16[1024,128]{1,0:T(8,128)(2,1)S(1)}, bf16[1024,128]{1,0:T(8,128)(2,1)S(1)}, u32[]{:S(2)}, u32[]{:S(2)}) collective-permute-start(bf16[1024,128]{1,0:T(8,128)(2,1)S(1)} %pad_maximum_fusion.2.refs_0_), channel_id=1, source_target_pairs={{0,8},{4,12},{8,0},{12,4},{1,9},{5,13},{9,1},{13,5},{2,10},{6,14},... | collective-permute-start | bytes 786440 | tf_op jit(solution)/shard_map/ppermute | solution.py:145
  66.1 20.8 %collective-permute-start.19 = (bf16[1024,128]{1,0:T(8,128)(2,1)S(1)}, bf16[1024,128]{1,0:T(8,128)(2,1)S(1)}, u32[]{:S(2)}, u32[]{:S(2)}) collective-permute-start(bf16[1024,128]{1,0:T(8,128)(2,1)S(1)} %pad_maximum_fusion.2.refs_0_), channel_id=1, source_target_pairs={{0,4},{4,0},{8,12},{12,8},{1,5},{5,1},{9,13},{13,9},{2,6},{6,2},{1... | collective-permute-start | bytes 786440 | tf_op jit(solution)/shard_map/ppermute | solution.py:145
  86.9 13.5 %collective-permute-start.22 = (bf16[64,2048]{1,0:T(8,128)(2,1)S(1)}, bf16[64,2048]{1,0:T(8,128)(2,1)S(1)}, u32[]{:S(2)}, u32[]{:S(2)}) collective-permute-start(bf16[64,2048]{1,0:T(8,128)(2,1)S(1)} %whiten.1), channel_id=1, source_target_pairs={{0,32},{32,0},{64,96},{96,64},{128,160},{160,128},{192,224},{224,1... | collective-permute-start | bytes 786440 | tf_op jit(solution)/shard_map/ppermute | solution.py:145
  100.4 8.2 %collective-permute-start.25 = (bf16[32,2048]{1,0:T(8,128)(2,1)S(1)}, bf16[32,2048]{1,0:T(8,128)(2,1)S(1)}, u32[]{:S(2)}, u32[]{:S(2)}) collective-permute-start(bf16[32,2048]{1,0:T(8,128)(2,1)S(1)} %slice_select_fusion), channel_id=1, source_target_pairs={{0,17},{16,1},{1,16},{17,0},{2,19},{18,3},{3,18},{19,2},{4,21},{20... | collective-permute-start | bytes 393224 | tf_op jit(solution)/shard_map/ppermute | solution.py:150
  100.6 10.2 %collective-permute-start.24 = (bf16[32,2048]{1,0:T(8,128)(2,1)S(1)}, bf16[32,2048]{1,0:T(8,128)(2,1)S(1)}, u32[]{:S(2)}, u32[]{:S(2)}) collective-permute-start(bf16[32,2048]{1,0:T(8,128)(2,1)S(1)} %slice_select_fusion), channel_id=1, source_target_pairs={{0,1},{16,17},{1,0},{17,16},{2,3},{18,19},{3,2},{19,18},{4,5},{20,... | collective-permute-start | bytes 393224 | tf_op jit(solution)/shard_map/ppermute | solution.py:150
  101.6 9.2 %collective-permute-start.23 = (bf16[32,2048]{1,0:T(8,128)(2,1)S(1)}, bf16[32,2048]{1,0:T(8,128)(2,1)S(1)}, u32[]{:S(2)}, u32[]{:S(2)}) collective-permute-start(bf16[32,2048]{1,0:T(8,128)(2,1)S(1)} %slice_select_fusion), channel_id=1, source_target_pairs={{0,16},{16,0},{1,17},{17,1},{2,18},{18,2},{3,19},{19,3},{4,20},{20... | collective-permute-start | bytes 393224 | tf_op jit(solution)/shard_map/ppermute | solution.py:150
  104.7 13.0 %collective-permute-start.28 = (bf16[64,2048]{1,0:T(8,128)(2,1)S(1)}, bf16[64,2048]{1,0:T(8,128)(2,1)S(1)}, u32[]{:S(2)}, u32[]{:S(2)}) collective-permute-start(bf16[64,2048]{1,0:T(8,128)(2,1)S(1)} %broadcast_select_fusion), channel_id=1, source_target_pairs={{0,12},{4,8},{8,4},{12,0},{1,13},{5,9},{9,5},{13,1},{2,14},{6,10},... | collective-permute-start | bytes 786440 | tf_op jit(solution)/shard_map/ppermute | solution.py:145
  105.0 12.6 %collective-permute-start.27 = (bf16[64,2048]{1,0:T(8,128)(2,1)S(1)}, bf16[64,2048]{1,0:T(8,128)(2,1)S(1)}, u32[]{:S(2)}, u32[]{:S(2)}) collective-permute-start(bf16[64,2048]{1,0:T(8,128)(2,1)S(1)} %broadcast_select_fusion), channel_id=1, source_target_pairs={{0,8},{4,12},{8,0},{12,4},{1,9},{5,13},{9,1},{13,5},{2,10},{6,14},... | collective-permute-start | bytes 786440 | tf_op jit(solution)/shard_map/ppermute | solution.py:145
  108.6 9.6 %collective-permute-start.26 = (bf16[64,2048]{1,0:T(8,128)(2,1)S(1)}, bf16[64,2048]{1,0:T(8,128)(2,1)S(1)}, u32[]{:S(2)}, u32[]{:S(2)}) collective-permute-start(bf16[64,2048]{1,0:T(8,128)(2,1)S(1)} %broadcast_select_fusion), channel_id=1, source_target_pairs={{0,4},{4,0},{8,12},{12,8},{1,5},{5,1},{9,13},{13,9},{2,6},{6,2},{1... | collective-permute-start | bytes 786440 | tf_op jit(solution)/shard_map/ppermute | solution.py:145
  121.4 9.0 %collective-permute-start.30 = (bf16[256,128]{1,0:T(8,128)(2,1)S(1)}, bf16[256,128]{1,0:T(8,128)(2,1)S(1)}, u32[]{:S(2)}, u32[]{:S(2)}) collective-permute-start(bf16[256,128]{1,0:T(8,128)(2,1)S(1)} %get-tuple-element.56), channel_id=1, source_target_pairs={{0,0},{2,32},{16,64},{18,96},{32,16},{34,48},{48,80},{50,112},{64,... | collective-permute-start | bytes 196616 | tf_op jit(solution)/shard_map/ppermute | solution.py:321
  125.5 11.3 %collective-permute-start.31 = (bf16[256,128]{1,0:T(8,128)(2,1)S(1)}, bf16[256,128]{1,0:T(8,128)(2,1)S(1)}, u32[]{:S(2)}, u32[]{:S(2)}) collective-permute-start(bf16[256,128]{1,0:T(8,128)(2,1)S(1)} %get-tuple-element.57), channel_id=1, source_target_pairs={{0,2},{2,34},{16,66},{18,98},{32,18},{34,50},{48,82},{50,114},{64,... | collective-permute-start | bytes 196616 | tf_op jit(solution)/shard_map/ppermute | solution.py:321
  (9 other events, 68.3 us)

commit v7 on v6

--- a/solution.py
+++ b/solution.py
@@ -30,20 +30,31 @@
 
 def chain_kernel(where, *refs):
     pieces = refs[:10]
-    out, side, turned, now, later, f1, f2, f3, u1, u2, sems = refs[10:]
+    out, side, turned, now, later, powers, probes, scales, sems = refs[10:]
     block, tokens = turned.shape
     half = COLUMNS // 2
     copies = []
     for source, row, col in placed(pieces, where[3] == 0):
         row, col = pl.multiple_of(row, 512), pl.multiple_of(col, 128)
         to = side.at[pl.ds(row, 512), pl.ds(col, 128)]
-        copies.append((pltpu.make_async_copy(source, to, sems.at[len(copies)]), row, col))
-        copies[-1][0].start()
+        copies.append(pltpu.make_async_copy(source, to, sems.at[len(copies)]))
+        copies[-1].start()
     now[...] = jnp.zeros_like(now)
     later[...] = jnp.zeros_like(later)
-    for copy, row, col in copies:
-        copy.wait()
-        turned[pl.ds(col, 128), pl.ds(row, 512)] = side[pl.ds(row, 512), pl.ds(col, 128)].T
+    row = lax.broadcasted_iota(jnp.int32, (COLUMNS, block), 0)
+    wanted = jnp.where(row < half, where[0] + row, where[1] + row - half)
+    powers[0] = jnp.where(lax.broadcasted_iota(jnp.int32, (COLUMNS, block), 1) == wanted, 1.0, 0.0)
+    for core in range(2):
+        for copy in copies[core * 32 : core * 32 + 32]:
+            copy.wait()
+
+        def turn(at, carry, core=core):
+            rows = pl.ds(pl.multiple_of(at // 8 * 1024 + core * 512, 512), 512)
+            cols = pl.ds(pl.multiple_of(at % 8 * 256, 256), 256)
+            turned[cols, rows] = side[rows, cols].T
+            return carry
+
+        lax.fori_loop(0, 16, turn, 0)
 
     probe_at = pl.ds(2 * COLUMNS, 16)
     probe_row = lax.broadcasted_iota(jnp.int32, (16, block), 0)
@@ -53,51 +64,52 @@
         probe = jnp.sum(product[2 * COLUMNS :], axis=0, keepdims=True)
         return product[:COLUMNS] + product[COLUMNS : 2 * COLUMNS], probe
 
-    def keep(target, rows, probe=None):
+    def keep(target, rows, probe):
         target[:COLUMNS], target[COLUMNS : 2 * COLUMNS] = split2(rows)
-        if probe is not None:
-            high, middle, low = (part.astype(F32) for part in split3(probe))
-            stacked = jnp.where(probe_row == 0, high, jnp.where(probe_row == 1, middle, low))
-            target[probe_at] = jnp.where(probe_row < 3, stacked, 0.0).astype(BF16)
-
-    def unit():
-        row = lax.broadcasted_iota(jnp.int32, (COLUMNS, block), 0)
-        wanted = jnp.where(row < half, where[0] + row, where[1] + row - half)
-        col = lax.broadcasted_iota(jnp.int32, (COLUMNS, block), 1)
-        return jnp.where(col == wanted, 1.0, 0.0)
+        high, middle, low = (part.astype(F32) for part in split3(probe))
+        stacked = jnp.where(probe_row == 0, high, jnp.where(probe_row == 1, middle, low))
+        target[probe_at] = jnp.where(probe_row < 3, stacked, 0.0).astype(BF16)
 
     later[:half] = turned[pl.ds(pl.multiple_of(where[0], half), half), :]
     later[half:COLUMNS] = turned[pl.ds(pl.multiple_of(where[1], half), half), :]
-    rows, _ = times(later, side)
-    rows = rows / tokens + DAMPING * unit()
-    f1[...] = rows
-    keep(now, rows, jnp.ones((1, block), F32))
-    keep(later, *times(now, turned))
-    rows, probe = times(later, side)
-    rows, probe = rows / tokens + DAMPING * f1[...], probe / tokens + DAMPING
-    f2[...], u1[...] = rows, probe
-    keep(now, rows, probe)
-    keep(later, *times(now, turned))
-    rows, probe = times(later, side)
-    rows, probe = rows / tokens + DAMPING * f2[...], probe / tokens + DAMPING * u1[...]
-    f3[...], u2[...] = rows, probe
-    keep(now, rows, probe)
-    rows, probe = times(now, turned)
-    keep(later, rows)
-    norm = jnp.sum(u2[...] * u2[...], axis=1, keepdims=True)
-    scale = (jnp.sum(probe * probe, axis=1, keepdims=True) / tokens + DAMPING * norm) / norm
-    inverse = 1.0 / scale
-    inverse2 = inverse * inverse
-    rows, _ = times(later, side)
-    a3 = f3[...] * (inverse2 * inverse)
-    a4 = (rows / tokens) * (inverse2 * inverse2) + DAMPING * (a3 * inverse)
-    total = 36.0 * unit() - 39.0 * (f1[...] * inverse) + 27.0 * (f2[...] * inverse2)
-    keep(now, (total - 9.0 * a3 + a4) * (1.0 / (16.0 * jnp.sqrt(scale))))
-    rows, _ = times(now, turned)
-    for at in range(16):
-        z = (where[4 + at // 4 % 2] - 2 * (at % 4)) % 8
-        to = pl.ds(pl.multiple_of(((at // 8) ^ where[2]) * 1024 + z * 128, 128), 128)
-        out[:, to] = rows[:, at * 128 : at * 128 + 128].astype(BF16)
+
+    def step(j, carry):
+        rows, probe = times(later, side)
+        rows = rows / tokens + DAMPING * powers[j]
+        probe = jnp.where(j == 0, 1.0, probe / tokens + DAMPING * probes[...])
+
+        @pl.when(j < 3)
+        def _():
+            powers[j + 1] = rows
+            probes[...] = probe
+            keep(now, rows, probe)
+
+        @pl.when(j == 3)
+        def _():
+            inverse = 1.0 / scales[...]
+            total = rows * (inverse * inverse) - 9.0 * (powers[3] * inverse)
+            total = (total + 27.0 * powers[2]) * (inverse * inverse) - 39.0 * (powers[1] * inverse)
+            total = (total + 36.0 * powers[0]) * (1.0 / (16.0 * jnp.sqrt(scales[...])))
+            keep(now, total, probe)
+
+        rows, probe = times(now, turned)
+        norm = jnp.sum(probes[...] * probes[...], axis=1, keepdims=True)
+
+        @pl.when(j < 3)
+        def _():
+            keep(later, rows, probe)
+            scales[...] = (jnp.sum(probe * probe, axis=1, keepdims=True) / tokens + DAMPING * norm) / norm
+
+        @pl.when(j == 3)
+        def _():
+            for at in range(16):
+                z = (where[4 + at // 4 % 2] - 2 * (at % 4)) % 8
+                to = pl.ds(pl.multiple_of(((at // 8) ^ where[2]) * 1024 + z * 128, 128), 128)
+                out[:, to] = rows[:, at * 128 : at * 128 + 128].astype(BF16)
+
+        return carry
+
+    lax.fori_loop(0, 4, step, 0)
 
 
 def placed(pieces, first_core):
@@ -132,8 +144,9 @@
             pltpu.VMEM((block, tokens), BF16),
             pltpu.VMEM((rows, block), BF16),
             pltpu.VMEM((rows, tokens), BF16),
-            *[pltpu.VMEM((COLUMNS, block), F32)] * 3,
-            *[pltpu.VMEM((1, block), F32)] * 2,
+            pltpu.VMEM((4, COLUMNS, block), F32),
+            pltpu.VMEM((1, block), F32),
+            pltpu.VMEM((1, 1), F32),
             pltpu.SemaphoreType.DMA((64,)),
         ],
         compiler_params=pltpu.CompilerParams(vmem_limit_bytes=32 * 2**20),

time: 138 us -> 140 us (1.014)
  Pallas kernels: 20.9 us -> 22.9 us
    pallas_call x1, Pallas kernels: 18.2 us -> 20.2 us  [whitened_columns(): pl.pallas_call(chain_kernel, name='whiten', out_shape=jax.ShapeDtypeStruc...]
  transfers between devices with their start and end apart: 32 -> 32, of which waited for: 19 -> 19; matrix products, arithmetic and copies ran while one was open for 1% -> 1% of each run, Pallas kernels for 14% -> 16%
where the time goes in v7:
time: 140 us
  waiting for transfers between devices  63.1 us (45%)
  starting transfers between devices  49.2 us (35%)
  Pallas kernels  22.9 us (16%)
  local copies, waits for them, and re-layouts  2.94 us (2%)
    ppermute x7, waiting for transfers between devices, plane_swap(): return lax.ppermute(array, ('yl', 'x', 'c', 'yh'), pairs)  30.9 us
    pallas_call x1, Pallas kernels, whitened_columns(): pl.pallas_call(chain_kernel, name='whiten', out_shape=jax.ShapeDtypeStruc...  20.2 us
    ppermute x15, waiting for transfers between devices, xor_swap(): lax.ppermute(array, axis, [(i, i ^ mask) for i in range(lax.axis_size(axi...  18.9 us
    ppermute x15, starting transfers between devices, xor_swap(): lax.ppermute(array, axis, [(i, i ^ mask) for i in range(lax.axis_size(axi...  17.3 us
    ppermute x3, starting transfers between devices, shared_part(): lax.ppermute(pieces[shift], 'z', [(i, (i + 2 * shift) % 8) for i in range...  9.6 us
    ppermute x7, starting transfers between devices, plane_swap(): return lax.ppermute(array, ('yl', 'x', 'c', 'yh'), pairs)  8.79 us
    ppermute x2, waiting for transfers between devices, local(): lax.ppermute(tile[step], ('z', 'yl', 'c'), owners(step))  7.75 us
    ppermute x2, starting transfers between devices, local(): lax.ppermute(tile[step], ('z', 'yl', 'c'), owners(step))  6.93 us
  transfers between devices with their start and end apart: 32, of which 19 were waited for; matrix products, arithmetic and copies ran while one was open for 1% of the time, Pallas kernels for 16%

profile of v7, /device:TPU:64, one launch (start us, length us, event | category | flops | bytes accessed | tf_op | source)
XLA Modules:
  0.0 139.6 jit_solution(9548953353135455778)
XLA Ops:
  3.4 5.5 %collective-permute-start.3 = (bf16[128,128]{1,0:T(8,128)(2,1)S(1)}, bf16[128,128]{1,0:T(8,128)(2,1)S(1)}, u32[]{:S(2)}, u32[]{:S(2)}) collective-permute-start(bf16[128,128]{1,0:T(8,128)(2,1)S(1)} %broadcast_select_fusion.8), channel_id=1, source_target_pairs={{0,128},{32,160},{64,192},{96,224},{128,0},{160,32},{192,64},{224,... | collective-permute-start | bytes 98312 | tf_op jit(solution)/shard_map/ppermute | solution.py:190
  8.9 2.7 %collective-permute-start.2 = (bf16[128,128]{1,0:T(8,128)(2,1)S(1)}, bf16[128,128]{1,0:T(8,128)(2,1)S(1)}, u32[]{:S(2)}, u32[]{:S(2)}) collective-permute-start(bf16[128,128]{1,0:T(8,128)(2,1)S(1)} %get-tuple-element.51), channel_id=1, source_target_pairs={{0,64},{32,96},{64,128},{96,160},{128,192},{160,224},{192,0},{224,... | collective-permute-start | bytes 98312 | tf_op jit(solution)/shard_map/ppermute | solution.py:190
  11.5 2.1 %collective-permute-done.2 = bf16[128,128]{1,0:T(8,128)(2,1)S(1)} collective-permute-done((bf16[128,128]{1,0:T(8,128)(2,1)S(1)}, bf16[128,128]{1,0:T(8,128)(2,1)S(1)}, u32[]{:S(2)}, u32[]{:S(2)}) %collective-permute-start.2) | collective-permute-done | bytes 32800 | tf_op jit(solution)/shard_map/ppermute | solution.py:190
  16.1 1.9 %collective-permute-done.5 = bf16[512,128]{1,0:T(8,128)(2,1)S(1)} collective-permute-done((bf16[512,128]{1,0:T(8,128)(2,1)S(1)}, bf16[512,128]{1,0:T(8,128)(2,1)S(1)}, u32[]{:S(2)}, u32[]{:S(2)}) %collective-permute-start.5) | collective-permute-done | bytes 131104 | tf_op jit(solution)/shard_map/ppermute | solution.py:200
  19.7 2.7 %collective-permute-start.8 = (bf16[1024,128]{1,0:T(8,128)(2,1)S(1)}, bf16[1024,128]{1,0:T(8,128)(2,1)S(1)}, u32[]{:S(2)}, u32[]{:S(2)}) collective-permute-start(bf16[1024,128]{1,0:T(8,128)(2,1)S(1)} %pad_maximum_fusion.3), channel_id=1, source_target_pairs={{0,8},{2,3},{16,24},{18,19},{1,9},{3,2},{17,25},{19,18},{4,12},{6,... | collective-permute-start | bytes 786440 | tf_op jit(solution)/shard_map/ppermute | solution.py:175
  24.6 5.1 %collective-permute-done.8 = bf16[1024,128]{1,0:T(8,128)(2,1)S(1)} collective-permute-done((bf16[1024,128]{1,0:T(8,128)(2,1)S(1)}, bf16[1024,128]{1,0:T(8,128)(2,1)S(1)}, u32[]{:S(2)}, u32[]{:S(2)}) %collective-permute-start.8) | collective-permute-done | bytes 262176 | tf_op jit(solution)/shard_map/ppermute | solution.py:175
  29.7 2.7 %collective-permute-done.9 = bf16[1024,128]{1,0:T(8,128)(2,1)S(1)} collective-permute-done((bf16[1024,128]{1,0:T(8,128)(2,1)S(1)}, bf16[1024,128]{1,0:T(8,128)(2,1)S(1)}, u32[]{:S(2)}, u32[]{:S(2)}) %collective-permute-start.9) | collective-permute-done | bytes 262176 | tf_op jit(solution)/shard_map/ppermute | solution.py:175
  32.4 3.1 %collective-permute-start.12 = (bf16[4096,128]{1,0:T(8,128)(2,1)S(1)}, bf16[4096,128]{1,0:T(8,128)(2,1)S(1)}, u32[]{:S(2)}, u32[]{:S(2)}) collective-permute-start(bf16[4096,128]{1,0:T(8,128)(2,1)S(1)} %constant_dynamic-update-slice_fusion.refs_0_), channel_id=1, source_target_pairs={{0,17},{2,14},{16,1},{18,30},{1,16},{3,15},{17,0},{19,31},{4,21},{... | collective-permute-start | bytes 3145736 | tf_op jit(solution)/shard_map/ppermute | solution.py:175
  38.9 9.6 %collective-permute-done.12.refs_4_ = bf16[4096,128]{1,0:T(8,128)(2,1)S(1)} collective-permute-done((bf16[4096,128]{1,0:T(8,128)(2,1)S(1)}, bf16[4096,128]{1,0:T(8,128)(2,1)S(1)}, u32[]{:S(2)}, u32[]{:S(2)}) %collective-permute-start.12) | collective-permute-done | bytes 1048608 | tf_op jit(solution)/shard_map/ppermute | solution.py:175
  49.0 2.7 %collective-permute-done.10.refs_1_ = bf16[4096,128]{1,0:T(8,128)(2,1)S(1)} collective-permute-done((bf16[4096,128]{1,0:T(8,128)(2,1)S(1)}, bf16[4096,128]{1,0:T(8,128)(2,1)S(1)}, u32[]{:S(2)}, u32[]{:S(2)}) %collective-permute-start.10) | collective-permute-done | bytes 1048608 | tf_op jit(solution)/shard_map/ppermute | solution.py:175
  53.2 5.7 %collective-permute-done.13.refs_3_ = bf16[2048,128]{1,0:T(8,128)(2,1)} collective-permute-done((bf16[2048,128]{1,0:T(8,128)(2,1)S(1)}, bf16[2048,128]{1,0:T(8,128)(2,1)}, u32[]{:S(2)}, u32[]{:S(2)}) %collective-permute-start.13) | collective-permute-done | bytes 524320 | tf_op jit(solution)/shard_map/ppermute | solution.py:175
  58.9 3.5 %collective-permute-done.11.refs_2_ = bf16[2048,128]{1,0:T(8,128)(2,1)} collective-permute-done((bf16[2048,128]{1,0:T(8,128)(2,1)S(1)}, bf16[2048,128]{1,0:T(8,128)(2,1)}, u32[]{:S(2)}, u32[]{:S(2)}) %collective-permute-start.11) | collective-permute-done | bytes 524320 | tf_op jit(solution)/shard_map/ppermute | solution.py:175
  62.5 2.1 %collective-permute-done.16.refs_7_ = bf16[2048,128]{1,0:T(8,128)(2,1)} collective-permute-done((bf16[2048,128]{1,0:T(8,128)(2,1)}, bf16[2048,128]{1,0:T(8,128)(2,1)}, u32[]{:S(2)}, u32[]{:S(2)}) %collective-permute-start.16) | collective-permute-done | bytes 524320 | tf_op jit(solution)/shard_map/ppermute | solution.py:158
  66.1 2.6 %collective-permute-start.19 = (bf16[1024,128]{1,0:T(8,128)(2,1)S(1)}, bf16[1024,128]{1,0:T(8,128)(2,1)S(1)}, u32[]{:S(2)}, u32[]{:S(2)}) collective-permute-start(bf16[1024,128]{1,0:T(8,128)(2,1)S(1)} %pad_maximum_fusion.2.refs_0_), channel_id=1, source_target_pairs={{0,4},{4,0},{8,12},{12,8},{1,5},{5,1},{9,13},{13,9},{2,6},{6,2},{1... | collective-permute-start | bytes 786440 | tf_op jit(solution)/shard_map/ppermute | solution.py:158
  68.7 20.2 %whiten.1 = bf16[64,2048]{1,0:T(8,128)(2,1)S(1)} custom-call(s32[6]{0:T(128)S(1)} %stack.60.where, bf16[4096,128]{1,0:T(8,128)(2,1)S(1)} %constant_dynamic-update-slice_fusion.refs_0_, bf16[4096,128]{1,0:T(8,128)(2,1)S(1)} %collective-permute-done.10.refs_1_, bf16[2048,128]{1,0:T(8,128)(2,1)} %collective-permute-done.11.refs_2_, ...), custom_call_target="tpu_custom_call" | custom-call | flops 9663676416 | bytes 8388608 | tf_op jit(solution)/shard_map/whiten/pallas_call | solution.py:136
  88.9 7.7 %collective-permute-start.22 = (bf16[64,2048]{1,0:T(8,128)(2,1)S(1)}, bf16[64,2048]{1,0:T(8,128)(2,1)S(1)}, u32[]{:S(2)}, u32[]{:S(2)}) collective-permute-start(bf16[64,2048]{1,0:T(8,128)(2,1)S(1)} %whiten.1), channel_id=1, source_target_pairs={{0,32},{32,0},{64,96},{96,64},{128,160},{160,128},{192,224},{224,1... | collective-permute-start | bytes 786440 | tf_op jit(solution)/shard_map/ppermute | solution.py:158
  96.7 5.7 %collective-permute-done.22 = bf16[64,2048]{1,0:T(8,128)(2,1)S(1)} collective-permute-done((bf16[64,2048]{1,0:T(8,128)(2,1)S(1)}, bf16[64,2048]{1,0:T(8,128)(2,1)S(1)}, u32[]{:S(2)}, u32[]{:S(2)}) %collective-permute-start.22) | collective-permute-done | bytes 262176 | tf_op jit(solution)/shard_map/ppermute | solution.py:158
  103.6 3.0 %collective-permute-start.23 = (bf16[32,2048]{1,0:T(8,128)(2,1)S(1)}, bf16[32,2048]{1,0:T(8,128)(2,1)S(1)}, u32[]{:S(2)}, u32[]{:S(2)}) collective-permute-start(bf16[32,2048]{1,0:T(8,128)(2,1)S(1)} %slice_select_fusion), channel_id=1, source_target_pairs={{0,16},{16,0},{1,17},{17,1},{2,18},{18,2},{3,19},{19,3},{4,20},{20... | collective-permute-start | bytes 393224 | tf_op jit(solution)/shard_map/ppermute | solution.py:163
  107.0 2.1 %collective-permute-start.27 = (bf16[64,2048]{1,0:T(8,128)(2,1)S(1)}, bf16[64,2048]{1,0:T(8,128)(2,1)S(1)}, u32[]{:S(2)}, u32[]{:S(2)}) collective-permute-start(bf16[64,2048]{1,0:T(8,128)(2,1)S(1)} %broadcast_select_fusion), channel_id=1, source_target_pairs={{0,8},{4,12},{8,0},{12,4},{1,9},{5,13},{9,1},{13,5},{2,10},{6,14},... | collective-permute-start | bytes 786440 | tf_op jit(solution)/shard_map/ppermute | solution.py:158
  112.9 6.7 %collective-permute-done.28 = bf16[64,2048]{1,0:T(8,128)(2,1)S(1)} collective-permute-done((bf16[64,2048]{1,0:T(8,128)(2,1)S(1)}, bf16[64,2048]{1,0:T(8,128)(2,1)S(1)}, u32[]{:S(2)}, u32[]{:S(2)}) %collective-permute-start.28) | collective-permute-done | bytes 262176 | tf_op jit(solution)/shard_map/ppermute | solution.py:158
  120.5 1.8 %collective-permute-done.29.other = bf16[128,2048]{1,0:T(8,128)(2,1)S(1)} collective-permute-done((bf16[128,2048]{1,0:T(8,128)(2,1)S(1)}, bf16[128,2048]{1,0:T(8,128)(2,1)S(1)}, u32[]{:S(2)}, u32[]{:S(2)}) %collective-permute-start.29) | collective-permute-done | bytes 524320 | tf_op jit(solution)/shard_map/ppermute | solution.py:158
  123.4 4.1 %collective-permute-start.30 = (bf16[256,128]{1,0:T(8,128)(2,1)S(1)}, bf16[256,128]{1,0:T(8,128)(2,1)S(1)}, u32[]{:S(2)}, u32[]{:S(2)}) collective-permute-start(bf16[256,128]{1,0:T(8,128)(2,1)S(1)} %get-tuple-element.56), channel_id=1, source_target_pairs={{0,0},{2,32},{16,64},{18,96},{32,16},{34,48},{48,80},{50,112},{64,... | collective-permute-start | bytes 196616 | tf_op jit(solution)/shard_map/ppermute | solution.py:334
  127.5 2.8 %collective-permute-start.31 = (bf16[256,128]{1,0:T(8,128)(2,1)S(1)}, bf16[256,128]{1,0:T(8,128)(2,1)S(1)}, u32[]{:S(2)}, u32[]{:S(2)}) collective-permute-start(bf16[256,128]{1,0:T(8,128)(2,1)S(1)} %get-tuple-element.57), channel_id=1, source_target_pairs={{0,2},{2,34},{16,66},{18,98},{32,18},{34,50},{48,82},{50,114},{64,... | collective-permute-start | bytes 196616 | tf_op jit(solution)/shard_map/ppermute | solution.py:334
  132.5 6.3 %collective-permute-done.31 = bf16[256,128]{1,0:T(8,128)(2,1)S(1)} collective-permute-done((bf16[256,128]{1,0:T(8,128)(2,1)S(1)}, bf16[256,128]{1,0:T(8,128)(2,1)S(1)}, u32[]{:S(2)}, u32[]{:S(2)}) %collective-permute-start.31) | collective-permute-done | bytes 65568 | tf_op jit(solution)/shard_map/ppermute | solution.py:334
  (74 shorter events, 26.3 us)
Async XLA Ops:
  1.9 9.6 %collective-permute-start.4 = (bf16[128,128]{1,0:T(8,128)(2,1)S(1)}, bf16[128,128]{1,0:T(8,128)(2,1)S(1)}, u32[]{:S(2)}, u32[]{:S(2)}) collective-permute-start(bf16[128,128]{1,0:T(8,128)(2,1)S(1)} %broadcast_select_fusion.7), channel_id=1, source_target_pairs={{0,192},{32,224},{64,0},{96,32},{128,64},{160,96},{192,128},{224,1... | collective-permute-start | bytes 98312 | tf_op jit(solution)/shard_map/ppermute | solution.py:190
  3.4 8.1 %collective-permute-start.3 = (bf16[128,128]{1,0:T(8,128)(2,1)S(1)}, bf16[128,128]{1,0:T(8,128)(2,1)S(1)}, u32[]{:S(2)}, u32[]{:S(2)}) collective-permute-start(bf16[128,128]{1,0:T(8,128)(2,1)S(1)} %broadcast_select_fusion.8), channel_id=1, source_target_pairs={{0,128},{32,160},{64,192},{96,224},{128,0},{160,32},{192,64},{224,... | collective-permute-start | bytes 98312 | tf_op jit(solution)/shard_map/ppermute | solution.py:190
  19.7 10.0 %collective-permute-start.8 = (bf16[1024,128]{1,0:T(8,128)(2,1)S(1)}, bf16[1024,128]{1,0:T(8,128)(2,1)S(1)}, u32[]{:S(2)}, u32[]{:S(2)}) collective-permute-start(bf16[1024,128]{1,0:T(8,128)(2,1)S(1)} %pad_maximum_fusion.3), channel_id=1, source_target_pairs={{0,8},{2,3},{16,24},{18,19},{1,9},{3,2},{17,25},{19,18},{4,12},{6,... | collective-permute-start | bytes 786440 | tf_op jit(solution)/shard_map/ppermute | solution.py:175
  22.4 10.0 %collective-permute-start.9 = (bf16[1024,128]{1,0:T(8,128)(2,1)S(1)}, bf16[1024,128]{1,0:T(8,128)(2,1)S(1)}, u32[]{:S(2)}, u32[]{:S(2)}) collective-permute-start(bf16[1024,128]{1,0:T(8,128)(2,1)S(1)} %pad_maximum_fusion.3), channel_id=1, source_target_pairs={{0,12},{2,19},{16,28},{18,3},{1,13},{3,18},{17,29},{19,2},{4,8},{6... | collective-permute-start | bytes 786440 | tf_op jit(solution)/shard_map/ppermute | solution.py:175
  32.4 16.1 %collective-permute-start.12 = (bf16[4096,128]{1,0:T(8,128)(2,1)S(1)}, bf16[4096,128]{1,0:T(8,128)(2,1)S(1)}, u32[]{:S(2)}, u32[]{:S(2)}) collective-permute-start(bf16[4096,128]{1,0:T(8,128)(2,1)S(1)} %constant_dynamic-update-slice_fusion.refs_0_), channel_id=1, source_target_pairs={{0,17},{2,14},{16,1},{18,30},{1,16},{3,15},{17,0},{19,31},{4,21},{... | collective-permute-start | bytes 3145736 | tf_op jit(solution)/shard_map/ppermute | solution.py:175
  35.5 16.2 %collective-permute-start.10 = (bf16[4096,128]{1,0:T(8,128)(2,1)S(1)}, bf16[4096,128]{1,0:T(8,128)(2,1)S(1)}, u32[]{:S(2)}, u32[]{:S(2)}) collective-permute-start(bf16[4096,128]{1,0:T(8,128)(2,1)S(1)} %constant_dynamic-update-slice_fusion.refs_0_), channel_id=1, source_target_pairs={{0,16},{2,6},{16,0},{18,22},{1,17},{3,7},{17,1},{19,23},{4,20},{6,... | collective-permute-start | bytes 3145736 | tf_op jit(solution)/shard_map/ppermute | solution.py:175
  37.5 15.6 %collective-permute-start.1 = (bf16[512,128]{1,0:T(8,128)(2,1)S(1)}, bf16[512,128]{1,0:T(8,128)(2,1)S(1)}, u32[]{:S(2)}, u32[]{:S(2)}) collective-permute-start(bf16[512,128]{1,0:T(8,128)(2,1)S(1)} %pad_maximum_fusion.4), channel_id=1, source_target_pairs={{0,16},{16,0},{1,17},{17,1},{2,18},{18,2},{3,19},{19,3},{4,20},{20... | collective-permute-start | bytes 393224 | tf_op jit(solution)/shard_map/ppermute | solution.py:158
  38.9 23.6 %collective-permute-start.14 = (bf16[4096,128]{1,0:T(8,128)(2,1)S(1)}, bf16[4096,128]{1,0:T(8,128)(2,1)}, u32[]{:S(2)}, u32[]{:S(2)}) collective-permute-start(bf16[4096,128]{1,0:T(8,128)(2,1)S(1)} %constant_dynamic-update-slice_fusion.refs_0_), channel_id=1, source_target_pairs={{0,2},{2,0},{1,3},{3,1},{4,6},{6,4},{5,7},{7,5},{8,10},{10,8},{9,1... | collective-permute-start | bytes 3145736 | tf_op jit(solution)/shard_map/ppermute | solution.py:158
  48.6 10.3 %collective-permute-start.13 = (bf16[2048,128]{1,0:T(8,128)(2,1)S(1)}, bf16[2048,128]{1,0:T(8,128)(2,1)}, u32[]{:S(2)}, u32[]{:S(2)}) collective-permute-start(bf16[2048,128]{1,0:T(8,128)(2,1)S(1)} %slice.43), channel_id=1, source_target_pairs={{0,16},{2,6},{16,0},{18,22},{1,17},{3,7},{17,1},{19,23},{4,20},{6,... | collective-permute-start | bytes 1572872 | tf_op jit(solution)/shard_map/ppermute | solution.py:175
  51.8 10.6 %collective-permute-start.11 = (bf16[2048,128]{1,0:T(8,128)(2,1)S(1)}, bf16[2048,128]{1,0:T(8,128)(2,1)}, u32[]{:S(2)}, u32[]{:S(2)}) collective-permute-start(bf16[2048,128]{1,0:T(8,128)(2,1)S(1)} %slice.42), channel_id=1, source_target_pairs={{0,17},{2,14},{16,1},{18,30},{1,16},{3,15},{17,0},{19,31},{4,21},{... | collective-permute-start | bytes 1572872 | tf_op jit(solution)/shard_map/ppermute | solution.py:175
  52.1 10.4 %collective-permute-start.18 = (bf16[4096,128]{1,0:T(8,128)(2,1)S(1)}, bf16[4096,128]{1,0:T(8,128)(2,1)}, u32[]{:S(2)}, u32[]{:S(2)}) collective-permute-start(bf16[4096,128]{1,0:T(8,128)(2,1)S(1)} %collective-permute-done.12.refs_4_), channel_id=1, source_target_pairs={{0,2},{2,0},{1,3},{3,1},{4,6},{6,4},{5,7},{7,5},{8,10},{10,8},{9,1... | collective-permute-start | bytes 3145736 | tf_op jit(solution)/shard_map/ppermute | solution.py:158
  53.1 11.5 %collective-permute-start.15 = (bf16[4096,128]{1,0:T(8,128)(2,1)S(1)}, bf16[4096,128]{1,0:T(8,128)(2,1)}, u32[]{:S(2)}, u32[]{:S(2)}) collective-permute-start(bf16[4096,128]{1,0:T(8,128)(2,1)S(1)} %collective-permute-done.10.refs_1_), channel_id=1, source_target_pairs={{0,2},{2,0},{1,3},{3,1},{4,6},{6,4},{5,7},{7,5},{8,10},{10,8},{9,1... | collective-permute-start | bytes 3145736 | tf_op jit(solution)/shard_map/ppermute | solution.py:158
  64.6 24.3 %collective-permute-start.21 = (bf16[1024,128]{1,0:T(8,128)(2,1)S(1)}, bf16[1024,128]{1,0:T(8,128)(2,1)S(1)}, u32[]{:S(2)}, u32[]{:S(2)}) collective-permute-start(bf16[1024,128]{1,0:T(8,128)(2,1)S(1)} %pad_maximum_fusion.2.refs_0_), channel_id=1, source_target_pairs={{0,12},{4,8},{8,4},{12,0},{1,13},{5,9},{9,5},{13,1},{2,14},{6,10},... | collective-permute-start | bytes 786440 | tf_op jit(solution)/shard_map/ppermute | solution.py:158
  65.1 23.8 %collective-permute-start.20 = (bf16[1024,128]{1,0:T(8,128)(2,1)S(1)}, bf16[1024,128]{1,0:T(8,128)(2,1)S(1)}, u32[]{:S(2)}, u32[]{:S(2)}) collective-permute-start(bf16[1024,128]{1,0:T(8,128)(2,1)S(1)} %pad_maximum_fusion.2.refs_0_), channel_id=1, source_target_pairs={{0,8},{4,12},{8,0},{12,4},{1,9},{5,13},{9,1},{13,5},{2,10},{6,14},... | collective-permute-start | bytes 786440 | tf_op jit(solution)/shard_map/ppermute | solution.py:158
  66.1 22.8 %collective-permute-start.19 = (bf16[1024,128]{1,0:T(8,128)(2,1)S(1)}, bf16[1024,128]{1,0:T(8,128)(2,1)S(1)}, u32[]{:S(2)}, u32[]{:S(2)}) collective-permute-start(bf16[1024,128]{1,0:T(8,128)(2,1)S(1)} %pad_maximum_fusion.2.refs_0_), channel_id=1, source_target_pairs={{0,4},{4,0},{8,12},{12,8},{1,5},{5,1},{9,13},{13,9},{2,6},{6,2},{1... | collective-permute-start | bytes 786440 | tf_op jit(solution)/shard_map/ppermute | solution.py:158
  88.9 13.5 %collective-permute-start.22 = (bf16[64,2048]{1,0:T(8,128)(2,1)S(1)}, bf16[64,2048]{1,0:T(8,128)(2,1)S(1)}, u32[]{:S(2)}, u32[]{:S(2)}) collective-permute-start(bf16[64,2048]{1,0:T(8,128)(2,1)S(1)} %whiten.1), channel_id=1, source_target_pairs={{0,32},{32,0},{64,96},{96,64},{128,160},{160,128},{192,224},{224,1... | collective-permute-start | bytes 786440 | tf_op jit(solution)/shard_map/ppermute | solution.py:158
  102.4 8.2 %collective-permute-start.25 = (bf16[32,2048]{1,0:T(8,128)(2,1)S(1)}, bf16[32,2048]{1,0:T(8,128)(2,1)S(1)}, u32[]{:S(2)}, u32[]{:S(2)}) collective-permute-start(bf16[32,2048]{1,0:T(8,128)(2,1)S(1)} %slice_select_fusion), channel_id=1, source_target_pairs={{0,17},{16,1},{1,16},{17,0},{2,19},{18,3},{3,18},{19,2},{4,21},{20... | collective-permute-start | bytes 393224 | tf_op jit(solution)/shard_map/ppermute | solution.py:163
  102.6 10.2 %collective-permute-start.24 = (bf16[32,2048]{1,0:T(8,128)(2,1)S(1)}, bf16[32,2048]{1,0:T(8,128)(2,1)S(1)}, u32[]{:S(2)}, u32[]{:S(2)}) collective-permute-start(bf16[32,2048]{1,0:T(8,128)(2,1)S(1)} %slice_select_fusion), channel_id=1, source_target_pairs={{0,1},{16,17},{1,0},{17,16},{2,3},{18,19},{3,2},{19,18},{4,5},{20,... | collective-permute-start | bytes 393224 | tf_op jit(solution)/shard_map/ppermute | solution.py:163
  103.6 9.3 %collective-permute-start.23 = (bf16[32,2048]{1,0:T(8,128)(2,1)S(1)}, bf16[32,2048]{1,0:T(8,128)(2,1)S(1)}, u32[]{:S(2)}, u32[]{:S(2)}) collective-permute-start(bf16[32,2048]{1,0:T(8,128)(2,1)S(1)} %slice_select_fusion), channel_id=1, source_target_pairs={{0,16},{16,0},{1,17},{17,1},{2,18},{18,2},{3,19},{19,3},{4,20},{20... | collective-permute-start | bytes 393224 | tf_op jit(solution)/shard_map/ppermute | solution.py:163
  106.7 12.9 %collective-permute-start.28 = (bf16[64,2048]{1,0:T(8,128)(2,1)S(1)}, bf16[64,2048]{1,0:T(8,128)(2,1)S(1)}, u32[]{:S(2)}, u32[]{:S(2)}) collective-permute-start(bf16[64,2048]{1,0:T(8,128)(2,1)S(1)} %broadcast_select_fusion), channel_id=1, source_target_pairs={{0,12},{4,8},{8,4},{12,0},{1,13},{5,9},{9,5},{13,1},{2,14},{6,10},... | collective-permute-start | bytes 786440 | tf_op jit(solution)/shard_map/ppermute | solution.py:158
  107.0 12.6 %collective-permute-start.27 = (bf16[64,2048]{1,0:T(8,128)(2,1)S(1)}, bf16[64,2048]{1,0:T(8,128)(2,1)S(1)}, u32[]{:S(2)}, u32[]{:S(2)}) collective-permute-start(bf16[64,2048]{1,0:T(8,128)(2,1)S(1)} %broadcast_select_fusion), channel_id=1, source_target_pairs={{0,8},{4,12},{8,0},{12,4},{1,9},{5,13},{9,1},{13,5},{2,10},{6,14},... | collective-permute-start | bytes 786440 | tf_op jit(solution)/shard_map/ppermute | solution.py:158
  110.6 9.6 %collective-permute-start.26 = (bf16[64,2048]{1,0:T(8,128)(2,1)S(1)}, bf16[64,2048]{1,0:T(8,128)(2,1)S(1)}, u32[]{:S(2)}, u32[]{:S(2)}) collective-permute-start(bf16[64,2048]{1,0:T(8,128)(2,1)S(1)} %broadcast_select_fusion), channel_id=1, source_target_pairs={{0,4},{4,0},{8,12},{12,8},{1,5},{5,1},{9,13},{13,9},{2,6},{6,2},{1... | collective-permute-start | bytes 786440 | tf_op jit(solution)/shard_map/ppermute | solution.py:158
  123.4 9.1 %collective-permute-start.30 = (bf16[256,128]{1,0:T(8,128)(2,1)S(1)}, bf16[256,128]{1,0:T(8,128)(2,1)S(1)}, u32[]{:S(2)}, u32[]{:S(2)}) collective-permute-start(bf16[256,128]{1,0:T(8,128)(2,1)S(1)} %get-tuple-element.56), channel_id=1, source_target_pairs={{0,0},{2,32},{16,64},{18,96},{32,16},{34,48},{48,80},{50,112},{64,... | collective-permute-start | bytes 196616 | tf_op jit(solution)/shard_map/ppermute | solution.py:334
  127.5 11.3 %collective-permute-start.31 = (bf16[256,128]{1,0:T(8,128)(2,1)S(1)}, bf16[256,128]{1,0:T(8,128)(2,1)S(1)}, u32[]{:S(2)}, u32[]{:S(2)}) collective-permute-start(bf16[256,128]{1,0:T(8,128)(2,1)S(1)} %get-tuple-element.57), channel_id=1, source_target_pairs={{0,2},{2,34},{16,66},{18,98},{32,18},{34,50},{48,82},{50,114},{64,... | collective-permute-start | bytes 196616 | tf_op jit(solution)/shard_map/ppermute | solution.py:334
  (9 other events, 70.3 us)

commit v8 on v6

--- a/solution.py
+++ b/solution.py
@@ -178,16 +178,11 @@
     got = jnp.concatenate(got)
     across, beside = [], []
     for i in range(8):
-        for j in range(2):
-            if i % 2 == j:
-                across.append((i * 2 + j, twin(i) * 2 + j))
-            else:
-                across.append((i * 2 + j, i * 2 + 1 - j))
-                beside.append((i * 2 + j, twin(i) * 2 + 1 - j))
+        across += [(i * 2, twin(i) * 2 + 1), (i * 2 + 1, i * 2)]
+        beside.append((i * 2 + 1, twin(i) * 2 + 1))
     one = lax.ppermute(got, ("z", "c"), across)
     two = lax.ppermute(got, ("z", "c"), beside)
-    stays = z % 2 == c
-    return jnp.concatenate([jnp.where(stays, got, one), jnp.where(stays, one, two)])
+    return jnp.concatenate([jnp.where(c == 0, got, two), one])
 
 
 def side_pieces(part):
@@ -300,7 +295,7 @@
     pair = jnp.where(z % 2 == 1, z + 1, z - 1) % 8
     done = whitened_columns(
         pieces,
-        jnp.stack([first, second, yh, c, jnp.where(z % 2 == c, z, pair), jnp.where(z % 2 == c, pair, z)]),
+        jnp.stack([first, second, yh, c, jnp.where(c == 0, z, pair), jnp.where(c == 0, pair, z)]),
         block,
         token_count,
     )

time: 138 us -> 134 us (0.971)
  starting transfers between devices: 49.1 us -> 43 us
  waiting for transfers between devices: 63.1 us -> 65.4 us
    ppermute x15, starting transfers between devices: 17.2 us -> 11.8 us  [xor_swap(): lax.ppermute(array, axis, [(i, i ^ mask) for i in range(lax.axis_size(axi...]
  transfers between devices with their start and end apart: 32 -> 32, of which waited for: 19 -> 19; matrix products, arithmetic and copies ran while one was open for 1% -> 1% of each run, Pallas kernels for 14% -> 15%
where the time goes in v8:
time: 134 us
  waiting for transfers between devices  65.4 us (49%)
  starting transfers between devices  43 us (32%)
  Pallas kernels  20.9 us (16%)
  local copies, waits for them, and re-layouts  2.96 us (2%)
    ppermute x7, waiting for transfers between devices, plane_swap(): return lax.ppermute(array, ('yl', 'x', 'c', 'yh'), pairs)  30.9 us
    ppermute x15, waiting for transfers between devices, xor_swap(): lax.ppermute(array, axis, [(i, i ^ mask) for i in range(lax.axis_size(axi...  19.3 us
    pallas_call x1, Pallas kernels, whitened_columns(): pl.pallas_call(chain_kernel, name='whiten', out_shape=jax.ShapeDtypeStruc...  18.2 us
    ppermute x15, starting transfers between devices, xor_swap(): lax.ppermute(array, axis, [(i, i ^ mask) for i in range(lax.axis_size(axi...  11.8 us
    ppermute x3, starting transfers between devices, shared_part(): lax.ppermute(pieces[shift], 'z', [(i, (i + 2 * shift) % 8) for i in range...  9.6 us
    ppermute x7, starting transfers between devices, plane_swap(): return lax.ppermute(array, ('yl', 'x', 'c', 'yh'), pairs)  8.79 us
    ppermute x2, waiting for transfers between devices, local(): lax.ppermute(tile[step], ('z', 'yl', 'c'), owners(step))  8.4 us
    ppermute x2, starting transfers between devices, local(): lax.ppermute(tile[step], ('z', 'yl', 'c'), owners(step))  6.96 us
  transfers between devices with their start and end apart: 32, of which 19 were waited for; matrix products, arithmetic and copies ran while one was open for 1% of the time, Pallas kernels for 15%

profile of v8, /device:TPU:64, one launch (start us, length us, event | category | flops | bytes accessed | tf_op | source)
XLA Modules:
  0.0 133.7 jit_solution(5081756724275008671)
XLA Ops:
  3.4 5.5 %collective-permute-start.3 = (bf16[128,128]{1,0:T(8,128)(2,1)S(1)}, bf16[128,128]{1,0:T(8,128)(2,1)S(1)}, u32[]{:S(2)}, u32[]{:S(2)}) collective-permute-start(bf16[128,128]{1,0:T(8,128)(2,1)S(1)} %broadcast_select_fusion.7), channel_id=1, source_target_pairs={{0,128},{32,160},{64,192},{96,224},{128,0},{160,32},{192,64},{224,... | collective-permute-start | bytes 98312 | tf_op jit(solution)/shard_map/ppermute | solution.py:177
  8.9 2.7 %collective-permute-start.2 = (bf16[128,128]{1,0:T(8,128)(2,1)S(1)}, bf16[128,128]{1,0:T(8,128)(2,1)S(1)}, u32[]{:S(2)}, u32[]{:S(2)}) collective-permute-start(bf16[128,128]{1,0:T(8,128)(2,1)S(1)} %get-tuple-element.49), channel_id=1, source_target_pairs={{0,64},{32,96},{64,128},{96,160},{128,192},{160,224},{192,0},{224,... | collective-permute-start | bytes 98312 | tf_op jit(solution)/shard_map/ppermute | solution.py:177
  11.5 2.1 %collective-permute-done.2 = bf16[128,128]{1,0:T(8,128)(2,1)S(1)} collective-permute-done((bf16[128,128]{1,0:T(8,128)(2,1)S(1)}, bf16[128,128]{1,0:T(8,128)(2,1)S(1)}, u32[]{:S(2)}, u32[]{:S(2)}) %collective-permute-start.2) | collective-permute-done | bytes 32800 | tf_op jit(solution)/shard_map/ppermute | solution.py:177
  15.4 3.2 %collective-permute-done.6 = bf16[512,128]{1,0:T(8,128)(2,1)S(1)} collective-permute-done((bf16[512,128]{1,0:T(8,128)(2,1)S(1)}, bf16[512,128]{1,0:T(8,128)(2,1)S(1)}, u32[]{:S(2)}, u32[]{:S(2)}) %collective-permute-start.6) | collective-permute-done | bytes 131104 | tf_op jit(solution)/shard_map/ppermute | solution.py:183
  20.2 2.7 %collective-permute-start.8 = (bf16[1024,128]{1,0:T(8,128)(2,1)S(1)}, bf16[1024,128]{1,0:T(8,128)(2,1)S(1)}, u32[]{:S(2)}, u32[]{:S(2)}) collective-permute-start(bf16[1024,128]{1,0:T(8,128)(2,1)S(1)} %pad_maximum_fusion.3), channel_id=1, source_target_pairs={{0,8},{2,3},{16,24},{18,19},{1,9},{3,2},{17,25},{19,18},{4,12},{6,... | collective-permute-start | bytes 786440 | tf_op jit(solution)/shard_map/ppermute | solution.py:162
  25.1 5.1 %collective-permute-done.8 = bf16[1024,128]{1,0:T(8,128)(2,1)S(1)} collective-permute-done((bf16[1024,128]{1,0:T(8,128)(2,1)S(1)}, bf16[1024,128]{1,0:T(8,128)(2,1)S(1)}, u32[]{:S(2)}, u32[]{:S(2)}) %collective-permute-start.8) | collective-permute-done | bytes 262176 | tf_op jit(solution)/shard_map/ppermute | solution.py:162
  30.2 2.7 %collective-permute-done.9 = bf16[1024,128]{1,0:T(8,128)(2,1)S(1)} collective-permute-done((bf16[1024,128]{1,0:T(8,128)(2,1)S(1)}, bf16[1024,128]{1,0:T(8,128)(2,1)S(1)}, u32[]{:S(2)}, u32[]{:S(2)}) %collective-permute-start.9) | collective-permute-done | bytes 262176 | tf_op jit(solution)/shard_map/ppermute | solution.py:162
  32.9 3.1 %collective-permute-start.12 = (bf16[4096,128]{1,0:T(8,128)(2,1)S(1)}, bf16[4096,128]{1,0:T(8,128)(2,1)S(1)}, u32[]{:S(2)}, u32[]{:S(2)}) collective-permute-start(bf16[4096,128]{1,0:T(8,128)(2,1)S(1)} %constant_dynamic-update-slice_fusion.refs_0_), channel_id=1, source_target_pairs={{0,17},{2,14},{16,1},{18,30},{1,16},{3,15},{17,0},{19,31},{4,21},{... | collective-permute-start | bytes 3145736 | tf_op jit(solution)/shard_map/ppermute | solution.py:162
  37.4 2.0 %collective-permute-start.1 = (bf16[512,128]{1,0:T(8,128)(2,1)S(1)}, bf16[512,128]{1,0:T(8,128)(2,1)S(1)}, u32[]{:S(2)}, u32[]{:S(2)}) collective-permute-start(bf16[512,128]{1,0:T(8,128)(2,1)S(1)} %pad_maximum_fusion.4), channel_id=1, source_target_pairs={{0,16},{16,0},{1,17},{17,1},{2,18},{18,2},{3,19},{19,3},{4,20},{20... | collective-permute-start | bytes 393224 | tf_op jit(solution)/shard_map/ppermute | solution.py:145
  39.4 9.6 %collective-permute-done.12.refs_4_ = bf16[4096,128]{1,0:T(8,128)(2,1)S(1)} collective-permute-done((bf16[4096,128]{1,0:T(8,128)(2,1)S(1)}, bf16[4096,128]{1,0:T(8,128)(2,1)S(1)}, u32[]{:S(2)}, u32[]{:S(2)}) %collective-permute-start.12) | collective-permute-done | bytes 1048608 | tf_op jit(solution)/shard_map/ppermute | solution.py:162
  49.5 2.7 %collective-permute-done.10.refs_1_ = bf16[4096,128]{1,0:T(8,128)(2,1)S(1)} collective-permute-done((bf16[4096,128]{1,0:T(8,128)(2,1)S(1)}, bf16[4096,128]{1,0:T(8,128)(2,1)S(1)}, u32[]{:S(2)}, u32[]{:S(2)}) %collective-permute-start.10) | collective-permute-done | bytes 1048608 | tf_op jit(solution)/shard_map/ppermute | solution.py:162
  53.6 5.7 %collective-permute-done.13.refs_3_ = bf16[2048,128]{1,0:T(8,128)(2,1)} collective-permute-done((bf16[2048,128]{1,0:T(8,128)(2,1)S(1)}, bf16[2048,128]{1,0:T(8,128)(2,1)}, u32[]{:S(2)}, u32[]{:S(2)}) %collective-permute-start.13) | collective-permute-done | bytes 524320 | tf_op jit(solution)/shard_map/ppermute | solution.py:162
  59.4 3.5 %collective-permute-done.11.refs_2_ = bf16[2048,128]{1,0:T(8,128)(2,1)} collective-permute-done((bf16[2048,128]{1,0:T(8,128)(2,1)S(1)}, bf16[2048,128]{1,0:T(8,128)(2,1)}, u32[]{:S(2)}, u32[]{:S(2)}) %collective-permute-start.11) | collective-permute-done | bytes 524320 | tf_op jit(solution)/shard_map/ppermute | solution.py:162
  63.0 2.1 %collective-permute-done.16.refs_7_ = bf16[2048,128]{1,0:T(8,128)(2,1)} collective-permute-done((bf16[2048,128]{1,0:T(8,128)(2,1)}, bf16[2048,128]{1,0:T(8,128)(2,1)}, u32[]{:S(2)}, u32[]{:S(2)}) %collective-permute-start.16) | collective-permute-done | bytes 524320 | tf_op jit(solution)/shard_map/ppermute | solution.py:145
  66.6 2.6 %collective-permute-start.19 = (bf16[1024,128]{1,0:T(8,128)(2,1)S(1)}, bf16[1024,128]{1,0:T(8,128)(2,1)S(1)}, u32[]{:S(2)}, u32[]{:S(2)}) collective-permute-start(bf16[1024,128]{1,0:T(8,128)(2,1)S(1)} %pad_maximum_fusion.2.refs_0_), channel_id=1, source_target_pairs={{0,4},{4,0},{8,12},{12,8},{1,5},{5,1},{9,13},{13,9},{2,6},{6,2},{1... | collective-permute-start | bytes 786440 | tf_op jit(solution)/shard_map/ppermute | solution.py:145
  69.2 18.2 %whiten.1 = bf16[64,2048]{1,0:T(8,128)(2,1)S(1)} custom-call(s32[6]{0:T(128)S(1)} %stack.60.where, bf16[4096,128]{1,0:T(8,128)(2,1)S(1)} %constant_dynamic-update-slice_fusion.refs_0_, bf16[4096,128]{1,0:T(8,128)(2,1)S(1)} %collective-permute-done.10.refs_1_, bf16[2048,128]{1,0:T(8,128)(2,1)} %collective-permute-done.11.refs_2_, ...), custom_call_target="tpu_custom_call" | custom-call | flops 9663676416 | bytes 8388608 | tf_op jit(solution)/shard_map/whiten/pallas_call | solution.py:124
  87.4 2.6 %collective-permute-start.22 = (bf16[64,2048]{1,0:T(8,128)(2,1)S(1)}, bf16[64,2048]{1,0:T(8,128)(2,1)S(1)}, u32[]{:S(2)}, u32[]{:S(2)}) collective-permute-start(bf16[64,2048]{1,0:T(8,128)(2,1)S(1)} %whiten.1), channel_id=1, source_target_pairs={{0,32},{32,0},{64,96},{96,64},{128,160},{160,128},{192,224},{224,1... | collective-permute-start | bytes 786440 | tf_op jit(solution)/shard_map/ppermute | solution.py:145
  90.1 5.7 %collective-permute-done.22 = bf16[64,2048]{1,0:T(8,128)(2,1)S(1)} collective-permute-done((bf16[64,2048]{1,0:T(8,128)(2,1)S(1)}, bf16[64,2048]{1,0:T(8,128)(2,1)S(1)}, u32[]{:S(2)}, u32[]{:S(2)}) %collective-permute-start.22) | collective-permute-done | bytes 262176 | tf_op jit(solution)/shard_map/ppermute | solution.py:145
  96.9 3.1 %collective-permute-start.23 = (bf16[32,2048]{1,0:T(8,128)(2,1)S(1)}, bf16[32,2048]{1,0:T(8,128)(2,1)S(1)}, u32[]{:S(2)}, u32[]{:S(2)}) collective-permute-start(bf16[32,2048]{1,0:T(8,128)(2,1)S(1)} %slice_select_fusion), channel_id=1, source_target_pairs={{0,16},{16,0},{1,17},{17,1},{2,18},{18,2},{3,19},{19,3},{4,20},{20... | collective-permute-start | bytes 393224 | tf_op jit(solution)/shard_map/ppermute | solution.py:150
  100.6 1.9 %collective-permute-start.27 = (bf16[64,2048]{1,0:T(8,128)(2,1)S(1)}, bf16[64,2048]{1,0:T(8,128)(2,1)S(1)}, u32[]{:S(2)}, u32[]{:S(2)}) collective-permute-start(bf16[64,2048]{1,0:T(8,128)(2,1)S(1)} %broadcast_select_fusion), channel_id=1, source_target_pairs={{0,8},{4,12},{8,0},{12,4},{1,9},{5,13},{9,1},{13,5},{2,10},{6,14},... | collective-permute-start | bytes 786440 | tf_op jit(solution)/shard_map/ppermute | solution.py:145
  106.2 6.7 %collective-permute-done.28 = bf16[64,2048]{1,0:T(8,128)(2,1)S(1)} collective-permute-done((bf16[64,2048]{1,0:T(8,128)(2,1)S(1)}, bf16[64,2048]{1,0:T(8,128)(2,1)S(1)}, u32[]{:S(2)}, u32[]{:S(2)}) %collective-permute-start.28) | collective-permute-done | bytes 262176 | tf_op jit(solution)/shard_map/ppermute | solution.py:145
  116.8 5.0 %collective-permute-start.30 = (bf16[256,128]{1,0:T(8,128)(2,1)S(1)}, bf16[256,128]{1,0:T(8,128)(2,1)S(1)}, u32[]{:S(2)}, u32[]{:S(2)}) collective-permute-start(bf16[256,128]{1,0:T(8,128)(2,1)S(1)} %get-tuple-element.54), channel_id=1, source_target_pairs={{0,0},{2,32},{16,64},{18,96},{32,16},{34,48},{48,80},{50,112},{64,... | collective-permute-start | bytes 196616 | tf_op jit(solution)/shard_map/ppermute | solution.py:316
  121.8 1.9 %collective-permute-start.31 = (bf16[256,128]{1,0:T(8,128)(2,1)S(1)}, bf16[256,128]{1,0:T(8,128)(2,1)S(1)}, u32[]{:S(2)}, u32[]{:S(2)}) collective-permute-start(bf16[256,128]{1,0:T(8,128)(2,1)S(1)} %get-tuple-element.55), channel_id=1, source_target_pairs={{0,2},{2,34},{16,66},{18,98},{32,18},{34,50},{48,82},{50,114},{64,... | collective-permute-start | bytes 196616 | tf_op jit(solution)/shard_map/ppermute | solution.py:316
  125.8 7.0 %collective-permute-done.31 = bf16[256,128]{1,0:T(8,128)(2,1)S(1)} collective-permute-done((bf16[256,128]{1,0:T(8,128)(2,1)S(1)}, bf16[256,128]{1,0:T(8,128)(2,1)S(1)}, u32[]{:S(2)}, u32[]{:S(2)}) %collective-permute-start.31) | collective-permute-done | bytes 65568 | tf_op jit(solution)/shard_map/ppermute | solution.py:316
  (74 shorter events, 25.4 us)
Async XLA Ops:
  1.9 9.6 %collective-permute-start.4 = (bf16[128,128]{1,0:T(8,128)(2,1)S(1)}, bf16[128,128]{1,0:T(8,128)(2,1)S(1)}, u32[]{:S(2)}, u32[]{:S(2)}) collective-permute-start(bf16[128,128]{1,0:T(8,128)(2,1)S(1)} %broadcast_select_fusion.6), channel_id=1, source_target_pairs={{0,192},{32,224},{64,0},{96,32},{128,64},{160,96},{192,128},{224,1... | collective-permute-start | bytes 98312 | tf_op jit(solution)/shard_map/ppermute | solution.py:177
  3.4 8.1 %collective-permute-start.3 = (bf16[128,128]{1,0:T(8,128)(2,1)S(1)}, bf16[128,128]{1,0:T(8,128)(2,1)S(1)}, u32[]{:S(2)}, u32[]{:S(2)}) collective-permute-start(bf16[128,128]{1,0:T(8,128)(2,1)S(1)} %broadcast_select_fusion.7), channel_id=1, source_target_pairs={{0,128},{32,160},{64,192},{96,224},{128,0},{160,32},{192,64},{224,... | collective-permute-start | bytes 98312 | tf_op jit(solution)/shard_map/ppermute | solution.py:177
  20.2 10.0 %collective-permute-start.8 = (bf16[1024,128]{1,0:T(8,128)(2,1)S(1)}, bf16[1024,128]{1,0:T(8,128)(2,1)S(1)}, u32[]{:S(2)}, u32[]{:S(2)}) collective-permute-start(bf16[1024,128]{1,0:T(8,128)(2,1)S(1)} %pad_maximum_fusion.3), channel_id=1, source_target_pairs={{0,8},{2,3},{16,24},{18,19},{1,9},{3,2},{17,25},{19,18},{4,12},{6,... | collective-permute-start | bytes 786440 | tf_op jit(solution)/shard_map/ppermute | solution.py:162
  22.9 10.0 %collective-permute-start.9 = (bf16[1024,128]{1,0:T(8,128)(2,1)S(1)}, bf16[1024,128]{1,0:T(8,128)(2,1)S(1)}, u32[]{:S(2)}, u32[]{:S(2)}) collective-permute-start(bf16[1024,128]{1,0:T(8,128)(2,1)S(1)} %pad_maximum_fusion.3), channel_id=1, source_target_pairs={{0,12},{2,19},{16,28},{18,3},{1,13},{3,18},{17,29},{19,2},{4,8},{6... | collective-permute-start | bytes 786440 | tf_op jit(solution)/shard_map/ppermute | solution.py:162
  32.9 16.1 %collective-permute-start.12 = (bf16[4096,128]{1,0:T(8,128)(2,1)S(1)}, bf16[4096,128]{1,0:T(8,128)(2,1)S(1)}, u32[]{:S(2)}, u32[]{:S(2)}) collective-permute-start(bf16[4096,128]{1,0:T(8,128)(2,1)S(1)} %constant_dynamic-update-slice_fusion.refs_0_), channel_id=1, source_target_pairs={{0,17},{2,14},{16,1},{18,30},{1,16},{3,15},{17,0},{19,31},{4,21},{... | collective-permute-start | bytes 3145736 | tf_op jit(solution)/shard_map/ppermute | solution.py:162
  36.0 16.2 %collective-permute-start.10 = (bf16[4096,128]{1,0:T(8,128)(2,1)S(1)}, bf16[4096,128]{1,0:T(8,128)(2,1)S(1)}, u32[]{:S(2)}, u32[]{:S(2)}) collective-permute-start(bf16[4096,128]{1,0:T(8,128)(2,1)S(1)} %constant_dynamic-update-slice_fusion.refs_0_), channel_id=1, source_target_pairs={{0,16},{2,6},{16,0},{18,22},{1,17},{3,7},{17,1},{19,23},{4,20},{6,... | collective-permute-start | bytes 3145736 | tf_op jit(solution)/shard_map/ppermute | solution.py:162
  37.4 16.2 %collective-permute-start.1 = (bf16[512,128]{1,0:T(8,128)(2,1)S(1)}, bf16[512,128]{1,0:T(8,128)(2,1)S(1)}, u32[]{:S(2)}, u32[]{:S(2)}) collective-permute-start(bf16[512,128]{1,0:T(8,128)(2,1)S(1)} %pad_maximum_fusion.4), channel_id=1, source_target_pairs={{0,16},{16,0},{1,17},{17,1},{2,18},{18,2},{3,19},{19,3},{4,20},{20... | collective-permute-start | bytes 393224 | tf_op jit(solution)/shard_map/ppermute | solution.py:145
  39.4 23.6 %collective-permute-start.14 = (bf16[4096,128]{1,0:T(8,128)(2,1)S(1)}, bf16[4096,128]{1,0:T(8,128)(2,1)}, u32[]{:S(2)}, u32[]{:S(2)}) collective-permute-start(bf16[4096,128]{1,0:T(8,128)(2,1)S(1)} %constant_dynamic-update-slice_fusion.refs_0_), channel_id=1, source_target_pairs={{0,2},{2,0},{1,3},{3,1},{4,6},{6,4},{5,7},{7,5},{8,10},{10,8},{9,1... | collective-permute-start | bytes 3145736 | tf_op jit(solution)/shard_map/ppermute | solution.py:145
  49.1 10.3 %collective-permute-start.13 = (bf16[2048,128]{1,0:T(8,128)(2,1)S(1)}, bf16[2048,128]{1,0:T(8,128)(2,1)}, u32[]{:S(2)}, u32[]{:S(2)}) collective-permute-start(bf16[2048,128]{1,0:T(8,128)(2,1)S(1)} %slice.43), channel_id=1, source_target_pairs={{0,16},{2,6},{16,0},{18,22},{1,17},{3,7},{17,1},{19,23},{4,20},{6,... | collective-permute-start | bytes 1572872 | tf_op jit(solution)/shard_map/ppermute | solution.py:162
  52.3 10.6 %collective-permute-start.11 = (bf16[2048,128]{1,0:T(8,128)(2,1)S(1)}, bf16[2048,128]{1,0:T(8,128)(2,1)}, u32[]{:S(2)}, u32[]{:S(2)}) collective-permute-start(bf16[2048,128]{1,0:T(8,128)(2,1)S(1)} %slice.42), channel_id=1, source_target_pairs={{0,17},{2,14},{16,1},{18,30},{1,16},{3,15},{17,0},{19,31},{4,21},{... | collective-permute-start | bytes 1572872 | tf_op jit(solution)/shard_map/ppermute | solution.py:162
  52.6 10.4 %collective-permute-start.18 = (bf16[4096,128]{1,0:T(8,128)(2,1)S(1)}, bf16[4096,128]{1,0:T(8,128)(2,1)}, u32[]{:S(2)}, u32[]{:S(2)}) collective-permute-start(bf16[4096,128]{1,0:T(8,128)(2,1)S(1)} %collective-permute-done.12.refs_4_), channel_id=1, source_target_pairs={{0,2},{2,0},{1,3},{3,1},{4,6},{6,4},{5,7},{7,5},{8,10},{10,8},{9,1... | collective-permute-start | bytes 3145736 | tf_op jit(solution)/shard_map/ppermute | solution.py:145
  53.6 11.5 %collective-permute-start.15 = (bf16[4096,128]{1,0:T(8,128)(2,1)S(1)}, bf16[4096,128]{1,0:T(8,128)(2,1)}, u32[]{:S(2)}, u32[]{:S(2)}) collective-permute-start(bf16[4096,128]{1,0:T(8,128)(2,1)S(1)} %collective-permute-done.10.refs_1_), channel_id=1, source_target_pairs={{0,2},{2,0},{1,3},{3,1},{4,6},{6,4},{5,7},{7,5},{8,10},{10,8},{9,1... | collective-permute-start | bytes 3145736 | tf_op jit(solution)/shard_map/ppermute | solution.py:145
  65.1 22.3 %collective-permute-start.21 = (bf16[1024,128]{1,0:T(8,128)(2,1)S(1)}, bf16[1024,128]{1,0:T(8,128)(2,1)S(1)}, u32[]{:S(2)}, u32[]{:S(2)}) collective-permute-start(bf16[1024,128]{1,0:T(8,128)(2,1)S(1)} %pad_maximum_fusion.2.refs_0_), channel_id=1, source_target_pairs={{0,12},{4,8},{8,4},{12,0},{1,13},{5,9},{9,5},{13,1},{2,14},{6,10},... | collective-permute-start | bytes 786440 | tf_op jit(solution)/shard_map/ppermute | solution.py:145
  65.6 21.8 %collective-permute-start.20 = (bf16[1024,128]{1,0:T(8,128)(2,1)S(1)}, bf16[1024,128]{1,0:T(8,128)(2,1)S(1)}, u32[]{:S(2)}, u32[]{:S(2)}) collective-permute-start(bf16[1024,128]{1,0:T(8,128)(2,1)S(1)} %pad_maximum_fusion.2.refs_0_), channel_id=1, source_target_pairs={{0,8},{4,12},{8,0},{12,4},{1,9},{5,13},{9,1},{13,5},{2,10},{6,14},... | collective-permute-start | bytes 786440 | tf_op jit(solution)/shard_map/ppermute | solution.py:145
  66.6 20.8 %collective-permute-start.19 = (bf16[1024,128]{1,0:T(8,128)(2,1)S(1)}, bf16[1024,128]{1,0:T(8,128)(2,1)S(1)}, u32[]{:S(2)}, u32[]{:S(2)}) collective-permute-start(bf16[1024,128]{1,0:T(8,128)(2,1)S(1)} %pad_maximum_fusion.2.refs_0_), channel_id=1, source_target_pairs={{0,4},{4,0},{8,12},{12,8},{1,5},{5,1},{9,13},{13,9},{2,6},{6,2},{1... | collective-permute-start | bytes 786440 | tf_op jit(solution)/shard_map/ppermute | solution.py:145
  87.4 8.4 %collective-permute-start.22 = (bf16[64,2048]{1,0:T(8,128)(2,1)S(1)}, bf16[64,2048]{1,0:T(8,128)(2,1)S(1)}, u32[]{:S(2)}, u32[]{:S(2)}) collective-permute-start(bf16[64,2048]{1,0:T(8,128)(2,1)S(1)} %whiten.1), channel_id=1, source_target_pairs={{0,32},{32,0},{64,96},{96,64},{128,160},{160,128},{192,224},{224,1... | collective-permute-start | bytes 786440 | tf_op jit(solution)/shard_map/ppermute | solution.py:145
  95.8 8.2 %collective-permute-start.25 = (bf16[32,2048]{1,0:T(8,128)(2,1)S(1)}, bf16[32,2048]{1,0:T(8,128)(2,1)S(1)}, u32[]{:S(2)}, u32[]{:S(2)}) collective-permute-start(bf16[32,2048]{1,0:T(8,128)(2,1)S(1)} %slice_select_fusion), channel_id=1, source_target_pairs={{0,17},{16,1},{1,16},{17,0},{2,19},{18,3},{3,18},{19,2},{4,21},{20... | collective-permute-start | bytes 393224 | tf_op jit(solution)/shard_map/ppermute | solution.py:150
  96.1 10.1 %collective-permute-start.24 = (bf16[32,2048]{1,0:T(8,128)(2,1)S(1)}, bf16[32,2048]{1,0:T(8,128)(2,1)S(1)}, u32[]{:S(2)}, u32[]{:S(2)}) collective-permute-start(bf16[32,2048]{1,0:T(8,128)(2,1)S(1)} %slice_select_fusion), channel_id=1, source_target_pairs={{0,1},{16,17},{1,0},{17,16},{2,3},{18,19},{3,2},{19,18},{4,5},{20,... | collective-permute-start | bytes 393224 | tf_op jit(solution)/shard_map/ppermute | solution.py:150
  96.9 9.3 %collective-permute-start.23 = (bf16[32,2048]{1,0:T(8,128)(2,1)S(1)}, bf16[32,2048]{1,0:T(8,128)(2,1)S(1)}, u32[]{:S(2)}, u32[]{:S(2)}) collective-permute-start(bf16[32,2048]{1,0:T(8,128)(2,1)S(1)} %slice_select_fusion), channel_id=1, source_target_pairs={{0,16},{16,0},{1,17},{17,1},{2,18},{18,2},{3,19},{19,3},{4,20},{20... | collective-permute-start | bytes 393224 | tf_op jit(solution)/shard_map/ppermute | solution.py:150
  100.0 13.0 %collective-permute-start.28 = (bf16[64,2048]{1,0:T(8,128)(2,1)S(1)}, bf16[64,2048]{1,0:T(8,128)(2,1)S(1)}, u32[]{:S(2)}, u32[]{:S(2)}) collective-permute-start(bf16[64,2048]{1,0:T(8,128)(2,1)S(1)} %broadcast_select_fusion), channel_id=1, source_target_pairs={{0,12},{4,8},{8,4},{12,0},{1,13},{5,9},{9,5},{13,1},{2,14},{6,10},... | collective-permute-start | bytes 786440 | tf_op jit(solution)/shard_map/ppermute | solution.py:145
  100.6 12.4 %collective-permute-start.27 = (bf16[64,2048]{1,0:T(8,128)(2,1)S(1)}, bf16[64,2048]{1,0:T(8,128)(2,1)S(1)}, u32[]{:S(2)}, u32[]{:S(2)}) collective-permute-start(bf16[64,2048]{1,0:T(8,128)(2,1)S(1)} %broadcast_select_fusion), channel_id=1, source_target_pairs={{0,8},{4,12},{8,0},{12,4},{1,9},{5,13},{9,1},{13,5},{2,10},{6,14},... | collective-permute-start | bytes 786440 | tf_op jit(solution)/shard_map/ppermute | solution.py:145
  104.0 9.6 %collective-permute-start.26 = (bf16[64,2048]{1,0:T(8,128)(2,1)S(1)}, bf16[64,2048]{1,0:T(8,128)(2,1)S(1)}, u32[]{:S(2)}, u32[]{:S(2)}) collective-permute-start(bf16[64,2048]{1,0:T(8,128)(2,1)S(1)} %broadcast_select_fusion), channel_id=1, source_target_pairs={{0,4},{4,0},{8,12},{12,8},{1,5},{5,1},{9,13},{13,9},{2,6},{6,2},{1... | collective-permute-start | bytes 786440 | tf_op jit(solution)/shard_map/ppermute | solution.py:145
  116.8 9.0 %collective-permute-start.30 = (bf16[256,128]{1,0:T(8,128)(2,1)S(1)}, bf16[256,128]{1,0:T(8,128)(2,1)S(1)}, u32[]{:S(2)}, u32[]{:S(2)}) collective-permute-start(bf16[256,128]{1,0:T(8,128)(2,1)S(1)} %get-tuple-element.54), channel_id=1, source_target_pairs={{0,0},{2,32},{16,64},{18,96},{32,16},{34,48},{48,80},{50,112},{64,... | collective-permute-start | bytes 196616 | tf_op jit(solution)/shard_map/ppermute | solution.py:316
  121.8 11.0 %collective-permute-start.31 = (bf16[256,128]{1,0:T(8,128)(2,1)S(1)}, bf16[256,128]{1,0:T(8,128)(2,1)S(1)}, u32[]{:S(2)}, u32[]{:S(2)}) collective-permute-start(bf16[256,128]{1,0:T(8,128)(2,1)S(1)} %get-tuple-element.55), channel_id=1, source_target_pairs={{0,2},{2,34},{16,66},{18,98},{32,18},{34,50},{48,82},{50,114},{64,... | collective-permute-start | bytes 196616 | tf_op jit(solution)/shard_map/ppermute | solution.py:316
  (9 other events, 61.7 us)

commit v9 on v8

--- a/solution.py
+++ b/solution.py
@@ -205,7 +205,7 @@
     for at in range(4):
         row = pl.multiple_of((at ^ where[1]) * 64, 64)
         for core in range(2):
-            out[core ^ where[2], pl.ds(row, 64), :] = product[at * 64 : at * 64 + 64, core * 128 : core * 128 + 128]
+            out[core, pl.ds(row, 64), :] = product[at * 64 : at * 64 + 64, core * 128 : core * 128 + 128]
 
 
 def update_tile(where, acts, own, other):
@@ -254,13 +254,13 @@
     )(where, *parts, weight.reshape(blocks * width, features))
 
 
-def owners(step):
+def owners():
     pairs = []
     for z in range(8):
         act_side, grad_side = (0, 1, 1, 0)[z // 2], z // 4
         for yl in range(2):
             for c in range(2):
-                to = ((act_side * 4 + yl * 2 + c) * 2 + z % 2) * 2 + (step ^ grad_side)
+                to = ((act_side * 4 + yl * 2 + c) * 2 + z % 2) * 2 + grad_side
                 pairs.append(((z * 2 + yl) * 2 + c, to))
     return pairs
 
@@ -311,10 +311,12 @@
     grads = jnp.concatenate([grads[m] for m in range(4)])
     acts = jnp.concatenate([acts[m] for m in range(4)])
     grads, acts, input_grad = lax.optimization_barrier((grads, acts, input_grad))
-    numbers = jnp.stack([y * 2 + c, x, z // 4]).astype(jnp.int32)
+    numbers = jnp.stack([y * 2 + c, x]).astype(jnp.int32)
     tile = update_tile(numbers, acts, grads, xor_swap(grads, "c", 1))
-    tile = [lax.ppermute(tile[step], ("z", "yl", "c"), owners(step)) for step in range(2)]
-    update = jnp.stack([jnp.where(c == 0, tile[0], tile[1]), jnp.where(c == 0, tile[1], tile[0])], axis=1)
+    tile = lax.ppermute(tile, ("z", "yl", "c"), owners())
+    own, give = jnp.where(c == 0, tile[0], tile[1]), jnp.where(c == 0, tile[1], tile[0])
+    other = xor_swap(give, "c", 1)
+    update = jnp.stack([jnp.where(c == 0, own, other), jnp.where(c == 0, other, own)], axis=1)
     return update, input_grad.transpose(1, 0, 2)
 
 

time: 134 us -> 132 us (0.985)
  starting transfers between devices: 43 us -> 41.2 us
    ppermute x2 -> x1, starting transfers between devices: 6.96 us -> 5.04 us  [local(): tile = lax.ppermute(tile, ('z', 'yl', 'c'), owners())]
    ppermute x2 -> x1, waiting for transfers between devices: 8.4 us -> 7.62 us  [local(): tile = lax.ppermute(tile, ('z', 'yl', 'c'), owners())]
    ppermute x15 -> x16, waiting for transfers between devices: 19.3 us -> 19.8 us  [xor_swap(): lax.ppermute(array, axis, [(i, i ^ mask) for i in range(lax.axis_size(axi...]
    ppermute x15 -> x16, starting transfers between devices: 11.8 us -> 11.9 us  [xor_swap(): lax.ppermute(array, axis, [(i, i ^ mask) for i in range(lax.axis_size(axi...]
where the time goes in v9:
time: 132 us
  waiting for transfers between devices  65.2 us (49%)
  starting transfers between devices  41.2 us (31%)
  Pallas kernels  20.9 us (16%)
  local copies, waits for them, and re-layouts  2.94 us (2%)
    ppermute x7, waiting for transfers between devices, plane_swap(): return lax.ppermute(array, ('yl', 'x', 'c', 'yh'), pairs)  30.9 us
    ppermute x16, waiting for transfers between devices, xor_swap(): lax.ppermute(array, axis, [(i, i ^ mask) for i in range(lax.axis_size(axi...  19.8 us
    pallas_call x1, Pallas kernels, whitened_columns(): pl.pallas_call(chain_kernel, name='whiten', out_shape=jax.ShapeDtypeStruc...  18.2 us
    ppermute x16, starting transfers between devices, xor_swap(): lax.ppermute(array, axis, [(i, i ^ mask) for i in range(lax.axis_size(axi...  11.9 us
    ppermute x3, starting transfers between devices, shared_part(): lax.ppermute(pieces[shift], 'z', [(i, (i + 2 * shift) % 8) for i in range...  9.6 us
    ppermute x7, starting transfers between devices, plane_swap(): return lax.ppermute(array, ('yl', 'x', 'c', 'yh'), pairs)  8.79 us
    ppermute x1, waiting for transfers between devices, local(): tile = lax.ppermute(tile, ('z', 'yl', 'c'), owners())  7.62 us
    ppermute x1, starting transfers between devices, local(): tile = lax.ppermute(tile, ('z', 'yl', 'c'), owners())  5.04 us
  transfers between devices with their start and end apart: 32, of which 19 were waited for; matrix products, arithmetic and copies ran while one was open for 1% of the time, Pallas kernels for 15%

profile of v9, /device:TPU:64, one launch (start us, length us, event | category | flops | bytes accessed | tf_op | source)
XLA Modules:
  0.0 131.6 jit_solution(11193814546106958130)
XLA Ops:
  3.4 5.5 %collective-permute-start.3 = (bf16[128,128]{1,0:T(8,128)(2,1)S(1)}, bf16[128,128]{1,0:T(8,128)(2,1)S(1)}, u32[]{:S(2)}, u32[]{:S(2)}) collective-permute-start(bf16[128,128]{1,0:T(8,128)(2,1)S(1)} %broadcast_select_fusion.8), channel_id=1, source_target_pairs={{0,128},{32,160},{64,192},{96,224},{128,0},{160,32},{192,64},{224,... | collective-permute-start | bytes 98312 | tf_op jit(solution)/shard_map/ppermute | solution.py:177
  8.9 2.7 %collective-permute-start.2 = (bf16[128,128]{1,0:T(8,128)(2,1)S(1)}, bf16[128,128]{1,0:T(8,128)(2,1)S(1)}, u32[]{:S(2)}, u32[]{:S(2)}) collective-permute-start(bf16[128,128]{1,0:T(8,128)(2,1)S(1)} %get-tuple-element.49), channel_id=1, source_target_pairs={{0,64},{32,96},{64,128},{96,160},{128,192},{160,224},{192,0},{224,... | collective-permute-start | bytes 98312 | tf_op jit(solution)/shard_map/ppermute | solution.py:177
  11.5 2.1 %collective-permute-done.2 = bf16[128,128]{1,0:T(8,128)(2,1)S(1)} collective-permute-done((bf16[128,128]{1,0:T(8,128)(2,1)S(1)}, bf16[128,128]{1,0:T(8,128)(2,1)S(1)}, u32[]{:S(2)}, u32[]{:S(2)}) %collective-permute-start.2) | collective-permute-done | bytes 32800 | tf_op jit(solution)/shard_map/ppermute | solution.py:177
  15.4 3.2 %collective-permute-done.6 = bf16[512,128]{1,0:T(8,128)(2,1)S(1)} collective-permute-done((bf16[512,128]{1,0:T(8,128)(2,1)S(1)}, bf16[512,128]{1,0:T(8,128)(2,1)S(1)}, u32[]{:S(2)}, u32[]{:S(2)}) %collective-permute-start.6) | collective-permute-done | bytes 131104 | tf_op jit(solution)/shard_map/ppermute | solution.py:183
  20.2 2.7 %collective-permute-start.8 = (bf16[1024,128]{1,0:T(8,128)(2,1)S(1)}, bf16[1024,128]{1,0:T(8,128)(2,1)S(1)}, u32[]{:S(2)}, u32[]{:S(2)}) collective-permute-start(bf16[1024,128]{1,0:T(8,128)(2,1)S(1)} %pad_maximum_fusion.3), channel_id=1, source_target_pairs={{0,8},{2,3},{16,24},{18,19},{1,9},{3,2},{17,25},{19,18},{4,12},{6,... | collective-permute-start | bytes 786440 | tf_op jit(solution)/shard_map/ppermute | solution.py:162
  25.1 5.1 %collective-permute-done.8 = bf16[1024,128]{1,0:T(8,128)(2,1)S(1)} collective-permute-done((bf16[1024,128]{1,0:T(8,128)(2,1)S(1)}, bf16[1024,128]{1,0:T(8,128)(2,1)S(1)}, u32[]{:S(2)}, u32[]{:S(2)}) %collective-permute-start.8) | collective-permute-done | bytes 262176 | tf_op jit(solution)/shard_map/ppermute | solution.py:162
  30.2 2.7 %collective-permute-done.9 = bf16[1024,128]{1,0:T(8,128)(2,1)S(1)} collective-permute-done((bf16[1024,128]{1,0:T(8,128)(2,1)S(1)}, bf16[1024,128]{1,0:T(8,128)(2,1)S(1)}, u32[]{:S(2)}, u32[]{:S(2)}) %collective-permute-start.9) | collective-permute-done | bytes 262176 | tf_op jit(solution)/shard_map/ppermute | solution.py:162
  32.9 3.1 %collective-permute-start.12 = (bf16[4096,128]{1,0:T(8,128)(2,1)S(1)}, bf16[4096,128]{1,0:T(8,128)(2,1)S(1)}, u32[]{:S(2)}, u32[]{:S(2)}) collective-permute-start(bf16[4096,128]{1,0:T(8,128)(2,1)S(1)} %constant_dynamic-update-slice_fusion.refs_0_), channel_id=1, source_target_pairs={{0,17},{2,14},{16,1},{18,30},{1,16},{3,15},{17,0},{19,31},{4,21},{... | collective-permute-start | bytes 3145736 | tf_op jit(solution)/shard_map/ppermute | solution.py:162
  37.4 2.0 %collective-permute-start.1 = (bf16[512,128]{1,0:T(8,128)(2,1)S(1)}, bf16[512,128]{1,0:T(8,128)(2,1)S(1)}, u32[]{:S(2)}, u32[]{:S(2)}) collective-permute-start(bf16[512,128]{1,0:T(8,128)(2,1)S(1)} %pad_maximum_fusion.4), channel_id=1, source_target_pairs={{0,16},{16,0},{1,17},{17,1},{2,18},{18,2},{3,19},{19,3},{4,20},{20... | collective-permute-start | bytes 393224 | tf_op jit(solution)/shard_map/ppermute | solution.py:145
  39.4 9.6 %collective-permute-done.12.refs_4_ = bf16[4096,128]{1,0:T(8,128)(2,1)S(1)} collective-permute-done((bf16[4096,128]{1,0:T(8,128)(2,1)S(1)}, bf16[4096,128]{1,0:T(8,128)(2,1)S(1)}, u32[]{:S(2)}, u32[]{:S(2)}) %collective-permute-start.12) | collective-permute-done | bytes 1048608 | tf_op jit(solution)/shard_map/ppermute | solution.py:162
  49.5 2.7 %collective-permute-done.10.refs_1_ = bf16[4096,128]{1,0:T(8,128)(2,1)S(1)} collective-permute-done((bf16[4096,128]{1,0:T(8,128)(2,1)S(1)}, bf16[4096,128]{1,0:T(8,128)(2,1)S(1)}, u32[]{:S(2)}, u32[]{:S(2)}) %collective-permute-start.10) | collective-permute-done | bytes 1048608 | tf_op jit(solution)/shard_map/ppermute | solution.py:162
  53.6 5.7 %collective-permute-done.13.refs_3_ = bf16[2048,128]{1,0:T(8,128)(2,1)} collective-permute-done((bf16[2048,128]{1,0:T(8,128)(2,1)S(1)}, bf16[2048,128]{1,0:T(8,128)(2,1)}, u32[]{:S(2)}, u32[]{:S(2)}) %collective-permute-start.13) | collective-permute-done | bytes 524320 | tf_op jit(solution)/shard_map/ppermute | solution.py:162
  59.4 3.5 %collective-permute-done.11.refs_2_ = bf16[2048,128]{1,0:T(8,128)(2,1)} collective-permute-done((bf16[2048,128]{1,0:T(8,128)(2,1)S(1)}, bf16[2048,128]{1,0:T(8,128)(2,1)}, u32[]{:S(2)}, u32[]{:S(2)}) %collective-permute-start.11) | collective-permute-done | bytes 524320 | tf_op jit(solution)/shard_map/ppermute | solution.py:162
  63.0 2.1 %collective-permute-done.16.refs_7_ = bf16[2048,128]{1,0:T(8,128)(2,1)} collective-permute-done((bf16[2048,128]{1,0:T(8,128)(2,1)}, bf16[2048,128]{1,0:T(8,128)(2,1)}, u32[]{:S(2)}, u32[]{:S(2)}) %collective-permute-start.16) | collective-permute-done | bytes 524320 | tf_op jit(solution)/shard_map/ppermute | solution.py:145
  66.6 2.6 %collective-permute-start.19 = (bf16[1024,128]{1,0:T(8,128)(2,1)S(1)}, bf16[1024,128]{1,0:T(8,128)(2,1)S(1)}, u32[]{:S(2)}, u32[]{:S(2)}) collective-permute-start(bf16[1024,128]{1,0:T(8,128)(2,1)S(1)} %pad_maximum_fusion.2.refs_0_), channel_id=1, source_target_pairs={{0,4},{4,0},{8,12},{12,8},{1,5},{5,1},{9,13},{13,9},{2,6},{6,2},{1... | collective-permute-start | bytes 786440 | tf_op jit(solution)/shard_map/ppermute | solution.py:145
  69.2 18.2 %whiten.1 = bf16[64,2048]{1,0:T(8,128)(2,1)S(1)} custom-call(s32[6]{0:T(128)S(1)} %stack.56.where, bf16[4096,128]{1,0:T(8,128)(2,1)S(1)} %constant_dynamic-update-slice_fusion.refs_0_, bf16[4096,128]{1,0:T(8,128)(2,1)S(1)} %collective-permute-done.10.refs_1_, bf16[2048,128]{1,0:T(8,128)(2,1)} %collective-permute-done.11.refs_2_, ...), custom_call_target="tpu_custom_call" | custom-call | flops 9663676416 | bytes 8388608 | tf_op jit(solution)/shard_map/whiten/pallas_call | solution.py:124
  87.4 2.6 %collective-permute-start.22 = (bf16[64,2048]{1,0:T(8,128)(2,1)S(1)}, bf16[64,2048]{1,0:T(8,128)(2,1)S(1)}, u32[]{:S(2)}, u32[]{:S(2)}) collective-permute-start(bf16[64,2048]{1,0:T(8,128)(2,1)S(1)} %whiten.1), channel_id=1, source_target_pairs={{0,32},{32,0},{64,96},{96,64},{128,160},{160,128},{192,224},{224,1... | collective-permute-start | bytes 786440 | tf_op jit(solution)/shard_map/ppermute | solution.py:145
  90.1 5.7 %collective-permute-done.22 = bf16[64,2048]{1,0:T(8,128)(2,1)S(1)} collective-permute-done((bf16[64,2048]{1,0:T(8,128)(2,1)S(1)}, bf16[64,2048]{1,0:T(8,128)(2,1)S(1)}, u32[]{:S(2)}, u32[]{:S(2)}) %collective-permute-start.22) | collective-permute-done | bytes 262176 | tf_op jit(solution)/shard_map/ppermute | solution.py:145
  96.9 3.1 %collective-permute-start.23 = (bf16[32,2048]{1,0:T(8,128)(2,1)S(1)}, bf16[32,2048]{1,0:T(8,128)(2,1)S(1)}, u32[]{:S(2)}, u32[]{:S(2)}) collective-permute-start(bf16[32,2048]{1,0:T(8,128)(2,1)S(1)} %slice_select_fusion), channel_id=1, source_target_pairs={{0,16},{16,0},{1,17},{17,1},{2,18},{18,2},{3,19},{19,3},{4,20},{20... | collective-permute-start | bytes 393224 | tf_op jit(solution)/shard_map/ppermute | solution.py:150
  100.6 1.9 %collective-permute-start.27 = (bf16[64,2048]{1,0:T(8,128)(2,1)S(1)}, bf16[64,2048]{1,0:T(8,128)(2,1)S(1)}, u32[]{:S(2)}, u32[]{:S(2)}) collective-permute-start(bf16[64,2048]{1,0:T(8,128)(2,1)S(1)} %broadcast_select_fusion), channel_id=1, source_target_pairs={{0,8},{4,12},{8,0},{12,4},{1,9},{5,13},{9,1},{13,5},{2,10},{6,14},... | collective-permute-start | bytes 786440 | tf_op jit(solution)/shard_map/ppermute | solution.py:145
  106.2 6.7 %collective-permute-done.28 = bf16[64,2048]{1,0:T(8,128)(2,1)S(1)} collective-permute-done((bf16[64,2048]{1,0:T(8,128)(2,1)S(1)}, bf16[64,2048]{1,0:T(8,128)(2,1)S(1)}, u32[]{:S(2)}, u32[]{:S(2)}) %collective-permute-start.28) | collective-permute-done | bytes 262176 | tf_op jit(solution)/shard_map/ppermute | solution.py:145
  113.8 1.8 %collective-permute-done.29.other = bf16[128,2048]{1,0:T(8,128)(2,1)S(1)} collective-permute-done((bf16[128,2048]{1,0:T(8,128)(2,1)S(1)}, bf16[128,2048]{1,0:T(8,128)(2,1)S(1)}, u32[]{:S(2)}, u32[]{:S(2)}) %collective-permute-start.29) | collective-permute-done | bytes 524320 | tf_op jit(solution)/shard_map/ppermute | solution.py:145
  116.8 5.0 %collective-permute-start.30 = (bf16[2,256,128]{2,1,0:T(8,128)(2,1)S(1)}, bf16[2,256,128]{2,1,0:T(8,128)(2,1)S(1)}, u32[]{:S(2)}, u32[]{:S(2)}) collective-permute-start(bf16[2,256,128]{2,1,0:T(8,128)(2,1)S(1)} %update_tile.1), channel_id=1, source_target_pairs={{0,0},{2,32},{16,64},{18,96},{32,16},{34,48},{48,80},{50,112},{64,... | collective-permute-start | bytes 393224 | tf_op jit(solution)/shard_map/ppermute | solution.py:316
  121.8 7.6 %collective-permute-done.30 = bf16[2,256,128]{2,1,0:T(8,128)(2,1)S(1)} collective-permute-done((bf16[2,256,128]{2,1,0:T(8,128)(2,1)S(1)}, bf16[2,256,128]{2,1,0:T(8,128)(2,1)S(1)}, u32[]{:S(2)}, u32[]{:S(2)}) %collective-permute-start.30) | collective-permute-done | bytes 131104 | tf_op jit(solution)/shard_map/ppermute | solution.py:316
  (74 shorter events, 22.9 us)
Async XLA Ops:
  1.9 9.6 %collective-permute-start.4 = (bf16[128,128]{1,0:T(8,128)(2,1)S(1)}, bf16[128,128]{1,0:T(8,128)(2,1)S(1)}, u32[]{:S(2)}, u32[]{:S(2)}) collective-permute-start(bf16[128,128]{1,0:T(8,128)(2,1)S(1)} %broadcast_select_fusion.7), channel_id=1, source_target_pairs={{0,192},{32,224},{64,0},{96,32},{128,64},{160,96},{192,128},{224,1... | collective-permute-start | bytes 98312 | tf_op jit(solution)/shard_map/ppermute | solution.py:177
  3.4 8.1 %collective-permute-start.3 = (bf16[128,128]{1,0:T(8,128)(2,1)S(1)}, bf16[128,128]{1,0:T(8,128)(2,1)S(1)}, u32[]{:S(2)}, u32[]{:S(2)}) collective-permute-start(bf16[128,128]{1,0:T(8,128)(2,1)S(1)} %broadcast_select_fusion.8), channel_id=1, source_target_pairs={{0,128},{32,160},{64,192},{96,224},{128,0},{160,32},{192,64},{224,... | collective-permute-start | bytes 98312 | tf_op jit(solution)/shard_map/ppermute | solution.py:177
  18.6 6.5 %collective-permute-start.7 = (bf16[1024,128]{1,0:T(8,128)(2,1)S(1)}, bf16[1024,128]{1,0:T(8,128)(2,1)S(1)}, u32[]{:S(2)}, u32[]{:S(2)}) collective-permute-start(bf16[1024,128]{1,0:T(8,128)(2,1)S(1)} %pad_maximum_fusion.3), channel_id=1, source_target_pairs={{0,4},{2,18},{16,20},{18,2},{1,5},{3,19},{17,21},{19,3},{4,0},{6,2... | collective-permute-start | bytes 786440 | tf_op jit(solution)/shard_map/ppermute | solution.py:162
  20.2 10.0 %collective-permute-start.8 = (bf16[1024,128]{1,0:T(8,128)(2,1)S(1)}, bf16[1024,128]{1,0:T(8,128)(2,1)S(1)}, u32[]{:S(2)}, u32[]{:S(2)}) collective-permute-start(bf16[1024,128]{1,0:T(8,128)(2,1)S(1)} %pad_maximum_fusion.3), channel_id=1, source_target_pairs={{0,8},{2,3},{16,24},{18,19},{1,9},{3,2},{17,25},{19,18},{4,12},{6,... | collective-permute-start | bytes 786440 | tf_op jit(solution)/shard_map/ppermute | solution.py:162
  22.9 10.0 %collective-permute-start.9 = (bf16[1024,128]{1,0:T(8,128)(2,1)S(1)}, bf16[1024,128]{1,0:T(8,128)(2,1)S(1)}, u32[]{:S(2)}, u32[]{:S(2)}) collective-permute-start(bf16[1024,128]{1,0:T(8,128)(2,1)S(1)} %pad_maximum_fusion.3), channel_id=1, source_target_pairs={{0,12},{2,19},{16,28},{18,3},{1,13},{3,18},{17,29},{19,2},{4,8},{6... | collective-permute-start | bytes 786440 | tf_op jit(solution)/shard_map/ppermute | solution.py:162
  32.9 16.1 %collective-permute-start.12 = (bf16[4096,128]{1,0:T(8,128)(2,1)S(1)}, bf16[4096,128]{1,0:T(8,128)(2,1)S(1)}, u32[]{:S(2)}, u32[]{:S(2)}) collective-permute-start(bf16[4096,128]{1,0:T(8,128)(2,1)S(1)} %constant_dynamic-update-slice_fusion.refs_0_), channel_id=1, source_target_pairs={{0,17},{2,14},{16,1},{18,30},{1,16},{3,15},{17,0},{19,31},{4,21},{... | collective-permute-start | bytes 3145736 | tf_op jit(solution)/shard_map/ppermute | solution.py:162
  36.0 16.2 %collective-permute-start.10 = (bf16[4096,128]{1,0:T(8,128)(2,1)S(1)}, bf16[4096,128]{1,0:T(8,128)(2,1)S(1)}, u32[]{:S(2)}, u32[]{:S(2)}) collective-permute-start(bf16[4096,128]{1,0:T(8,128)(2,1)S(1)} %constant_dynamic-update-slice_fusion.refs_0_), channel_id=1, source_target_pairs={{0,16},{2,6},{16,0},{18,22},{1,17},{3,7},{17,1},{19,23},{4,20},{6,... | collective-permute-start | bytes 3145736 | tf_op jit(solution)/shard_map/ppermute | solution.py:162
  37.4 16.2 %collective-permute-start.1 = (bf16[512,128]{1,0:T(8,128)(2,1)S(1)}, bf16[512,128]{1,0:T(8,128)(2,1)S(1)}, u32[]{:S(2)}, u32[]{:S(2)}) collective-permute-start(bf16[512,128]{1,0:T(8,128)(2,1)S(1)} %pad_maximum_fusion.4), channel_id=1, source_target_pairs={{0,16},{16,0},{1,17},{17,1},{2,18},{18,2},{3,19},{19,3},{4,20},{20... | collective-permute-start | bytes 393224 | tf_op jit(solution)/shard_map/ppermute | solution.py:145
  39.4 23.6 %collective-permute-start.14 = (bf16[4096,128]{1,0:T(8,128)(2,1)S(1)}, bf16[4096,128]{1,0:T(8,128)(2,1)}, u32[]{:S(2)}, u32[]{:S(2)}) collective-permute-start(bf16[4096,128]{1,0:T(8,128)(2,1)S(1)} %constant_dynamic-update-slice_fusion.refs_0_), channel_id=1, source_target_pairs={{0,2},{2,0},{1,3},{3,1},{4,6},{6,4},{5,7},{7,5},{8,10},{10,8},{9,1... | collective-permute-start | bytes 3145736 | tf_op jit(solution)/shard_map/ppermute | solution.py:145
  49.1 10.3 %collective-permute-start.13 = (bf16[2048,128]{1,0:T(8,128)(2,1)S(1)}, bf16[2048,128]{1,0:T(8,128)(2,1)}, u32[]{:S(2)}, u32[]{:S(2)}) collective-permute-start(bf16[2048,128]{1,0:T(8,128)(2,1)S(1)} %slice.45), channel_id=1, source_target_pairs={{0,16},{2,6},{16,0},{18,22},{1,17},{3,7},{17,1},{19,23},{4,20},{6,... | collective-permute-start | bytes 1572872 | tf_op jit(solution)/shard_map/ppermute | solution.py:162
  52.3 10.6 %collective-permute-start.11 = (bf16[2048,128]{1,0:T(8,128)(2,1)S(1)}, bf16[2048,128]{1,0:T(8,128)(2,1)}, u32[]{:S(2)}, u32[]{:S(2)}) collective-permute-start(bf16[2048,128]{1,0:T(8,128)(2,1)S(1)} %slice.44), channel_id=1, source_target_pairs={{0,17},{2,14},{16,1},{18,30},{1,16},{3,15},{17,0},{19,31},{4,21},{... | collective-permute-start | bytes 1572872 | tf_op jit(solution)/shard_map/ppermute | solution.py:162
  52.6 10.4 %collective-permute-start.18 = (bf16[4096,128]{1,0:T(8,128)(2,1)S(1)}, bf16[4096,128]{1,0:T(8,128)(2,1)}, u32[]{:S(2)}, u32[]{:S(2)}) collective-permute-start(bf16[4096,128]{1,0:T(8,128)(2,1)S(1)} %collective-permute-done.12.refs_4_), channel_id=1, source_target_pairs={{0,2},{2,0},{1,3},{3,1},{4,6},{6,4},{5,7},{7,5},{8,10},{10,8},{9,1... | collective-permute-start | bytes 3145736 | tf_op jit(solution)/shard_map/ppermute | solution.py:145
  53.6 11.5 %collective-permute-start.15 = (bf16[4096,128]{1,0:T(8,128)(2,1)S(1)}, bf16[4096,128]{1,0:T(8,128)(2,1)}, u32[]{:S(2)}, u32[]{:S(2)}) collective-permute-start(bf16[4096,128]{1,0:T(8,128)(2,1)S(1)} %collective-permute-done.10.refs_1_), channel_id=1, source_target_pairs={{0,2},{2,0},{1,3},{3,1},{4,6},{6,4},{5,7},{7,5},{8,10},{10,8},{9,1... | collective-permute-start | bytes 3145736 | tf_op jit(solution)/shard_map/ppermute | solution.py:145
  65.1 22.3 %collective-permute-start.21 = (bf16[1024,128]{1,0:T(8,128)(2,1)S(1)}, bf16[1024,128]{1,0:T(8,128)(2,1)S(1)}, u32[]{:S(2)}, u32[]{:S(2)}) collective-permute-start(bf16[1024,128]{1,0:T(8,128)(2,1)S(1)} %pad_maximum_fusion.2.refs_0_), channel_id=1, source_target_pairs={{0,12},{4,8},{8,4},{12,0},{1,13},{5,9},{9,5},{13,1},{2,14},{6,10},... | collective-permute-start | bytes 786440 | tf_op jit(solution)/shard_map/ppermute | solution.py:145
  65.6 21.8 %collective-permute-start.20 = (bf16[1024,128]{1,0:T(8,128)(2,1)S(1)}, bf16[1024,128]{1,0:T(8,128)(2,1)S(1)}, u32[]{:S(2)}, u32[]{:S(2)}) collective-permute-start(bf16[1024,128]{1,0:T(8,128)(2,1)S(1)} %pad_maximum_fusion.2.refs_0_), channel_id=1, source_target_pairs={{0,8},{4,12},{8,0},{12,4},{1,9},{5,13},{9,1},{13,5},{2,10},{6,14},... | collective-permute-start | bytes 786440 | tf_op jit(solution)/shard_map/ppermute | solution.py:145
  66.6 20.8 %collective-permute-start.19 = (bf16[1024,128]{1,0:T(8,128)(2,1)S(1)}, bf16[1024,128]{1,0:T(8,128)(2,1)S(1)}, u32[]{:S(2)}, u32[]{:S(2)}) collective-permute-start(bf16[1024,128]{1,0:T(8,128)(2,1)S(1)} %pad_maximum_fusion.2.refs_0_), channel_id=1, source_target_pairs={{0,4},{4,0},{8,12},{12,8},{1,5},{5,1},{9,13},{13,9},{2,6},{6,2},{1... | collective-permute-start | bytes 786440 | tf_op jit(solution)/shard_map/ppermute | solution.py:145
  87.4 8.4 %collective-permute-start.22 = (bf16[64,2048]{1,0:T(8,128)(2,1)S(1)}, bf16[64,2048]{1,0:T(8,128)(2,1)S(1)}, u32[]{:S(2)}, u32[]{:S(2)}) collective-permute-start(bf16[64,2048]{1,0:T(8,128)(2,1)S(1)} %whiten.1), channel_id=1, source_target_pairs={{0,32},{32,0},{64,96},{96,64},{128,160},{160,128},{192,224},{224,1... | collective-permute-start | bytes 786440 | tf_op jit(solution)/shard_map/ppermute | solution.py:145
  95.8 8.2 %collective-permute-start.25 = (bf16[32,2048]{1,0:T(8,128)(2,1)S(1)}, bf16[32,2048]{1,0:T(8,128)(2,1)S(1)}, u32[]{:S(2)}, u32[]{:S(2)}) collective-permute-start(bf16[32,2048]{1,0:T(8,128)(2,1)S(1)} %slice_select_fusion), channel_id=1, source_target_pairs={{0,17},{16,1},{1,16},{17,0},{2,19},{18,3},{3,18},{19,2},{4,21},{20... | collective-permute-start | bytes 393224 | tf_op jit(solution)/shard_map/ppermute | solution.py:150
  96.1 10.1 %collective-permute-start.24 = (bf16[32,2048]{1,0:T(8,128)(2,1)S(1)}, bf16[32,2048]{1,0:T(8,128)(2,1)S(1)}, u32[]{:S(2)}, u32[]{:S(2)}) collective-permute-start(bf16[32,2048]{1,0:T(8,128)(2,1)S(1)} %slice_select_fusion), channel_id=1, source_target_pairs={{0,1},{16,17},{1,0},{17,16},{2,3},{18,19},{3,2},{19,18},{4,5},{20,... | collective-permute-start | bytes 393224 | tf_op jit(solution)/shard_map/ppermute | solution.py:150
  96.9 9.3 %collective-permute-start.23 = (bf16[32,2048]{1,0:T(8,128)(2,1)S(1)}, bf16[32,2048]{1,0:T(8,128)(2,1)S(1)}, u32[]{:S(2)}, u32[]{:S(2)}) collective-permute-start(bf16[32,2048]{1,0:T(8,128)(2,1)S(1)} %slice_select_fusion), channel_id=1, source_target_pairs={{0,16},{16,0},{1,17},{17,1},{2,18},{18,2},{3,19},{19,3},{4,20},{20... | collective-permute-start | bytes 393224 | tf_op jit(solution)/shard_map/ppermute | solution.py:150
  100.0 13.0 %collective-permute-start.28 = (bf16[64,2048]{1,0:T(8,128)(2,1)S(1)}, bf16[64,2048]{1,0:T(8,128)(2,1)S(1)}, u32[]{:S(2)}, u32[]{:S(2)}) collective-permute-start(bf16[64,2048]{1,0:T(8,128)(2,1)S(1)} %broadcast_select_fusion), channel_id=1, source_target_pairs={{0,12},{4,8},{8,4},{12,0},{1,13},{5,9},{9,5},{13,1},{2,14},{6,10},... | collective-permute-start | bytes 786440 | tf_op jit(solution)/shard_map/ppermute | solution.py:145
  100.6 12.4 %collective-permute-start.27 = (bf16[64,2048]{1,0:T(8,128)(2,1)S(1)}, bf16[64,2048]{1,0:T(8,128)(2,1)S(1)}, u32[]{:S(2)}, u32[]{:S(2)}) collective-permute-start(bf16[64,2048]{1,0:T(8,128)(2,1)S(1)} %broadcast_select_fusion), channel_id=1, source_target_pairs={{0,8},{4,12},{8,0},{12,4},{1,9},{5,13},{9,1},{13,5},{2,10},{6,14},... | collective-permute-start | bytes 786440 | tf_op jit(solution)/shard_map/ppermute | solution.py:145
  104.0 9.6 %collective-permute-start.26 = (bf16[64,2048]{1,0:T(8,128)(2,1)S(1)}, bf16[64,2048]{1,0:T(8,128)(2,1)S(1)}, u32[]{:S(2)}, u32[]{:S(2)}) collective-permute-start(bf16[64,2048]{1,0:T(8,128)(2,1)S(1)} %broadcast_select_fusion), channel_id=1, source_target_pairs={{0,4},{4,0},{8,12},{12,8},{1,5},{5,1},{9,13},{13,9},{2,6},{6,2},{1... | collective-permute-start | bytes 786440 | tf_op jit(solution)/shard_map/ppermute | solution.py:145
  116.8 12.7 %collective-permute-start.30 = (bf16[2,256,128]{2,1,0:T(8,128)(2,1)S(1)}, bf16[2,256,128]{2,1,0:T(8,128)(2,1)S(1)}, u32[]{:S(2)}, u32[]{:S(2)}) collective-permute-start(bf16[2,256,128]{2,1,0:T(8,128)(2,1)S(1)} %update_tile.1), channel_id=1, source_target_pairs={{0,0},{2,32},{16,64},{18,96},{32,16},{34,48},{48,80},{50,112},{64,... | collective-permute-start | bytes 393224 | tf_op jit(solution)/shard_map/ppermute | solution.py:316
  (9 other events, 56.6 us)

commit v10 on v9

--- a/solution.py
+++ b/solution.py
@@ -304,10 +304,12 @@
     input_grad = grads_by_weight(jnp.stack([yl, x, c]).astype(jnp.int32), over_x, weight)
 
     swapped = xor_swap(done, "z", 1)
+    acts = jnp.where(is_act, done, swapped)
     grads = jnp.where(is_act, swapped[32:], done[:32])
-    acts = jnp.where(is_act, done, swapped)
-    grads = {0: grads, **{m: y_swap(grads, m) for m in (1, 3, 2)}}
     acts = {0: acts, **{m: xor_swap(acts, "x", m) for m in (1, 3, 2)}}
+    grads = {0: grads, 1: y_swap(grads, 1)}
+    pair = y_swap(jnp.concatenate([grads[0], grads[1]]), 2)
+    grads |= {2: pair[:32], 3: pair[32:]}
     grads = jnp.concatenate([grads[m] for m in range(4)])
     acts = jnp.concatenate([acts[m] for m in range(4)])
     grads, acts, input_grad = lax.optimization_barrier((grads, acts, input_grad))

time: 132 us -> 130 us (0.985)
  starting transfers between devices: 41.2 us -> 39.2 us
    ppermute x3 -> x2, starting transfers between devices: 4.18 us -> 1.07 us  [y_swap(): return lax.ppermute(array, ('yl', 'yh'), pairs)]
  transfers between devices with their start and end apart: 32 -> 31, of which waited for: 19 -> 19; matrix products, arithmetic and copies ran while one was open for 1% -> 1% of each run, Pallas kernels for 15% -> 15%
where the time goes in v10:
time: 130 us; the launch traced here: 128 us
  waiting for transfers between devices  63.9 us (49%)
  starting transfers between devices  39.2 us (30%)
  Pallas kernels  20.9 us (16%)
  local copies, waits for them, and re-layouts  2.94 us (2%)
    ppermute x7, waiting for transfers between devices, plane_swap(): return lax.ppermute(array, ('yl', 'x', 'c', 'yh'), pairs)  30.9 us
    ppermute x16, waiting for transfers between devices, xor_swap(): lax.ppermute(array, axis, [(i, i ^ mask) for i in range(lax.axis_size(axi...  19.3 us
    pallas_call x1, Pallas kernels, whitened_columns(): pl.pallas_call(chain_kernel, name='whiten', out_shape=jax.ShapeDtypeStruc...  18.2 us
    ppermute x16, starting transfers between devices, xor_swap(): lax.ppermute(array, axis, [(i, i ^ mask) for i in range(lax.axis_size(axi...  13 us
    ppermute x3, starting transfers between devices, shared_part(): lax.ppermute(pieces[shift], 'z', [(i, (i + 2 * shift) % 8) for i in range...  9.6 us
    ppermute x7, starting transfers between devices, plane_swap(): return lax.ppermute(array, ('yl', 'x', 'c', 'yh'), pairs)  8.79 us
    ppermute x1, waiting for transfers between devices, local(): tile = lax.ppermute(tile, ('z', 'yl', 'c'), owners())  7.62 us
    ppermute x1, starting transfers between devices, local(): tile = lax.ppermute(tile, ('z', 'yl', 'c'), owners())  5.04 us
  transfers between devices with their start and end apart: 31, of which 19 were waited for; matrix products, arithmetic and copies ran while one was open for 1% of the time, Pallas kernels for 15%

profile of v10, /device:TPU:64, one launch (start us, length us, event | category | flops | bytes accessed | tf_op | source)
XLA Modules:
  0.0 128.4 jit_solution(14196060402530371091)
XLA Ops:
  3.4 5.5 %collective-permute-start.3 = (bf16[128,128]{1,0:T(8,128)(2,1)S(1)}, bf16[128,128]{1,0:T(8,128)(2,1)S(1)}, u32[]{:S(2)}, u32[]{:S(2)}) collective-permute-start(bf16[128,128]{1,0:T(8,128)(2,1)S(1)} %broadcast_select_fusion.8), channel_id=1, source_target_pairs={{0,128},{32,160},{64,192},{96,224},{128,0},{160,32},{192,64},{224,... | collective-permute-start | bytes 98312 | tf_op jit(solution)/shard_map/ppermute | solution.py:177
  8.9 2.7 %collective-permute-start.2 = (bf16[128,128]{1,0:T(8,128)(2,1)S(1)}, bf16[128,128]{1,0:T(8,128)(2,1)S(1)}, u32[]{:S(2)}, u32[]{:S(2)}) collective-permute-start(bf16[128,128]{1,0:T(8,128)(2,1)S(1)} %get-tuple-element.49), channel_id=1, source_target_pairs={{0,64},{32,96},{64,128},{96,160},{128,192},{160,224},{192,0},{224,... | collective-permute-start | bytes 98312 | tf_op jit(solution)/shard_map/ppermute | solution.py:177
  11.5 2.1 %collective-permute-done.2 = bf16[128,128]{1,0:T(8,128)(2,1)S(1)} collective-permute-done((bf16[128,128]{1,0:T(8,128)(2,1)S(1)}, bf16[128,128]{1,0:T(8,128)(2,1)S(1)}, u32[]{:S(2)}, u32[]{:S(2)}) %collective-permute-start.2) | collective-permute-done | bytes 32800 | tf_op jit(solution)/shard_map/ppermute | solution.py:177
  15.4 3.2 %collective-permute-done.6 = bf16[512,128]{1,0:T(8,128)(2,1)S(1)} collective-permute-done((bf16[512,128]{1,0:T(8,128)(2,1)S(1)}, bf16[512,128]{1,0:T(8,128)(2,1)S(1)}, u32[]{:S(2)}, u32[]{:S(2)}) %collective-permute-start.6) | collective-permute-done | bytes 131104 | tf_op jit(solution)/shard_map/ppermute | solution.py:183
  20.2 2.7 %collective-permute-start.8 = (bf16[1024,128]{1,0:T(8,128)(2,1)S(1)}, bf16[1024,128]{1,0:T(8,128)(2,1)S(1)}, u32[]{:S(2)}, u32[]{:S(2)}) collective-permute-start(bf16[1024,128]{1,0:T(8,128)(2,1)S(1)} %pad_maximum_fusion.3), channel_id=1, source_target_pairs={{0,8},{2,3},{16,24},{18,19},{1,9},{3,2},{17,25},{19,18},{4,12},{6,... | collective-permute-start | bytes 786440 | tf_op jit(solution)/shard_map/ppermute | solution.py:162
  25.1 5.1 %collective-permute-done.8 = bf16[1024,128]{1,0:T(8,128)(2,1)S(1)} collective-permute-done((bf16[1024,128]{1,0:T(8,128)(2,1)S(1)}, bf16[1024,128]{1,0:T(8,128)(2,1)S(1)}, u32[]{:S(2)}, u32[]{:S(2)}) %collective-permute-start.8) | collective-permute-done | bytes 262176 | tf_op jit(solution)/shard_map/ppermute | solution.py:162
  30.2 2.7 %collective-permute-done.9 = bf16[1024,128]{1,0:T(8,128)(2,1)S(1)} collective-permute-done((bf16[1024,128]{1,0:T(8,128)(2,1)S(1)}, bf16[1024,128]{1,0:T(8,128)(2,1)S(1)}, u32[]{:S(2)}, u32[]{:S(2)}) %collective-permute-start.9) | collective-permute-done | bytes 262176 | tf_op jit(solution)/shard_map/ppermute | solution.py:162
  32.9 3.1 %collective-permute-start.12 = (bf16[4096,128]{1,0:T(8,128)(2,1)S(1)}, bf16[4096,128]{1,0:T(8,128)(2,1)S(1)}, u32[]{:S(2)}, u32[]{:S(2)}) collective-permute-start(bf16[4096,128]{1,0:T(8,128)(2,1)S(1)} %constant_dynamic-update-slice_fusion.refs_0_), channel_id=1, source_target_pairs={{0,17},{2,14},{16,1},{18,30},{1,16},{3,15},{17,0},{19,31},{4,21},{... | collective-permute-start | bytes 3145736 | tf_op jit(solution)/shard_map/ppermute | solution.py:162
  37.4 2.0 %collective-permute-start.1 = (bf16[512,128]{1,0:T(8,128)(2,1)S(1)}, bf16[512,128]{1,0:T(8,128)(2,1)S(1)}, u32[]{:S(2)}, u32[]{:S(2)}) collective-permute-start(bf16[512,128]{1,0:T(8,128)(2,1)S(1)} %pad_maximum_fusion.5), channel_id=1, source_target_pairs={{0,16},{16,0},{1,17},{17,1},{2,18},{18,2},{3,19},{19,3},{4,20},{20... | collective-permute-start | bytes 393224 | tf_op jit(solution)/shard_map/ppermute | solution.py:145
  39.4 9.6 %collective-permute-done.12.refs_4_ = bf16[4096,128]{1,0:T(8,128)(2,1)S(1)} collective-permute-done((bf16[4096,128]{1,0:T(8,128)(2,1)S(1)}, bf16[4096,128]{1,0:T(8,128)(2,1)S(1)}, u32[]{:S(2)}, u32[]{:S(2)}) %collective-permute-start.12) | collective-permute-done | bytes 1048608 | tf_op jit(solution)/shard_map/ppermute | solution.py:162
  49.5 2.7 %collective-permute-done.10.refs_1_ = bf16[4096,128]{1,0:T(8,128)(2,1)S(1)} collective-permute-done((bf16[4096,128]{1,0:T(8,128)(2,1)S(1)}, bf16[4096,128]{1,0:T(8,128)(2,1)S(1)}, u32[]{:S(2)}, u32[]{:S(2)}) %collective-permute-start.10) | collective-permute-done | bytes 1048608 | tf_op jit(solution)/shard_map/ppermute | solution.py:162
  53.6 5.7 %collective-permute-done.13.refs_3_ = bf16[2048,128]{1,0:T(8,128)(2,1)} collective-permute-done((bf16[2048,128]{1,0:T(8,128)(2,1)S(1)}, bf16[2048,128]{1,0:T(8,128)(2,1)}, u32[]{:S(2)}, u32[]{:S(2)}) %collective-permute-start.13) | collective-permute-done | bytes 524320 | tf_op jit(solution)/shard_map/ppermute | solution.py:162
  59.4 3.5 %collective-permute-done.11.refs_2_ = bf16[2048,128]{1,0:T(8,128)(2,1)} collective-permute-done((bf16[2048,128]{1,0:T(8,128)(2,1)S(1)}, bf16[2048,128]{1,0:T(8,128)(2,1)}, u32[]{:S(2)}, u32[]{:S(2)}) %collective-permute-start.11) | collective-permute-done | bytes 524320 | tf_op jit(solution)/shard_map/ppermute | solution.py:162
  63.0 2.1 %collective-permute-done.16.refs_7_ = bf16[2048,128]{1,0:T(8,128)(2,1)} collective-permute-done((bf16[2048,128]{1,0:T(8,128)(2,1)}, bf16[2048,128]{1,0:T(8,128)(2,1)}, u32[]{:S(2)}, u32[]{:S(2)}) %collective-permute-start.16) | collective-permute-done | bytes 524320 | tf_op jit(solution)/shard_map/ppermute | solution.py:145
  66.6 2.6 %collective-permute-start.19 = (bf16[1024,128]{1,0:T(8,128)(2,1)S(1)}, bf16[1024,128]{1,0:T(8,128)(2,1)S(1)}, u32[]{:S(2)}, u32[]{:S(2)}) collective-permute-start(bf16[1024,128]{1,0:T(8,128)(2,1)S(1)} %pad_maximum_fusion.2.refs_0_), channel_id=1, source_target_pairs={{0,4},{4,0},{8,12},{12,8},{1,5},{5,1},{9,13},{13,9},{2,6},{6,2},{1... | collective-permute-start | bytes 786440 | tf_op jit(solution)/shard_map/ppermute | solution.py:145
  69.2 18.2 %whiten.1 = bf16[64,2048]{1,0:T(8,128)(2,1)S(1)} custom-call(s32[6]{0:T(128)S(1)} %stack.56.where, bf16[4096,128]{1,0:T(8,128)(2,1)S(1)} %constant_dynamic-update-slice_fusion.refs_0_, bf16[4096,128]{1,0:T(8,128)(2,1)S(1)} %collective-permute-done.10.refs_1_, bf16[2048,128]{1,0:T(8,128)(2,1)} %collective-permute-done.11.refs_2_, ...), custom_call_target="tpu_custom_call" | custom-call | flops 9663676416 | bytes 8388608 | tf_op jit(solution)/shard_map/whiten/pallas_call | solution.py:124
  87.4 2.6 %collective-permute-start.22 = (bf16[64,2048]{1,0:T(8,128)(2,1)S(1)}, bf16[64,2048]{1,0:T(8,128)(2,1)S(1)}, u32[]{:S(2)}, u32[]{:S(2)}) collective-permute-start(bf16[64,2048]{1,0:T(8,128)(2,1)S(1)} %whiten.1), channel_id=1, source_target_pairs={{0,32},{32,0},{64,96},{96,64},{128,160},{160,128},{192,224},{224,1... | collective-permute-start | bytes 786440 | tf_op jit(solution)/shard_map/ppermute | solution.py:145
  90.0 5.8 %collective-permute-done.22 = bf16[64,2048]{1,0:T(8,128)(2,1)S(1)} collective-permute-done((bf16[64,2048]{1,0:T(8,128)(2,1)S(1)}, bf16[64,2048]{1,0:T(8,128)(2,1)S(1)}, u32[]{:S(2)}, u32[]{:S(2)}) %collective-permute-start.22) | collective-permute-done | bytes 262176 | tf_op jit(solution)/shard_map/ppermute | solution.py:145
  96.5 1.9 %collective-permute-start.26 = (bf16[64,2048]{1,0:T(8,128)(2,1)S(1)}, bf16[64,2048]{1,0:T(8,128)(2,1)S(1)}, u32[]{:S(2)}, u32[]{:S(2)}) collective-permute-start(bf16[64,2048]{1,0:T(8,128)(2,1)S(1)} %broadcast_select_fusion), channel_id=1, source_target_pairs={{0,8},{4,12},{8,0},{12,4},{1,9},{5,13},{9,1},{13,5},{2,10},{6,14},... | collective-permute-start | bytes 786440 | tf_op jit(solution)/shard_map/ppermute | solution.py:145
  98.4 1.7 %collective-permute-start.25 = (bf16[64,2048]{1,0:T(8,128)(2,1)S(1)}, bf16[64,2048]{1,0:T(8,128)(2,1)S(1)}, u32[]{:S(2)}, u32[]{:S(2)}) collective-permute-start(bf16[64,2048]{1,0:T(8,128)(2,1)S(1)} %broadcast_select_fusion), channel_id=1, source_target_pairs={{0,4},{4,0},{8,12},{12,8},{1,5},{5,1},{9,13},{13,9},{2,6},{6,2},{1... | collective-permute-start | bytes 786440 | tf_op jit(solution)/shard_map/ppermute | solution.py:145
  103.6 6.2 %collective-permute-done.27 = bf16[64,2048]{1,0:T(8,128)(2,1)S(1)} collective-permute-done((bf16[64,2048]{1,0:T(8,128)(2,1)S(1)}, bf16[64,2048]{1,0:T(8,128)(2,1)S(1)}, u32[]{:S(2)}, u32[]{:S(2)}) %collective-permute-start.27) | collective-permute-done | bytes 262176 | tf_op jit(solution)/shard_map/ppermute | solution.py:145
  110.7 1.8 %collective-permute-done.28.other = bf16[128,2048]{1,0:T(8,128)(2,1)S(1)} collective-permute-done((bf16[128,2048]{1,0:T(8,128)(2,1)S(1)}, bf16[128,2048]{1,0:T(8,128)(2,1)S(1)}, u32[]{:S(2)}, u32[]{:S(2)}) %collective-permute-start.28) | collective-permute-done | bytes 524320 | tf_op jit(solution)/shard_map/ppermute | solution.py:145
  113.6 5.0 %collective-permute-start.29 = (bf16[2,256,128]{2,1,0:T(8,128)(2,1)S(1)}, bf16[2,256,128]{2,1,0:T(8,128)(2,1)S(1)}, u32[]{:S(2)}, u32[]{:S(2)}) collective-permute-start(bf16[2,256,128]{2,1,0:T(8,128)(2,1)S(1)} %update_tile.1), channel_id=1, source_target_pairs={{0,0},{2,32},{16,64},{18,96},{32,16},{34,48},{48,80},{50,112},{64,... | collective-permute-start | bytes 393224 | tf_op jit(solution)/shard_map/ppermute | solution.py:318
  118.6 7.6 %collective-permute-done.29 = bf16[2,256,128]{2,1,0:T(8,128)(2,1)S(1)} collective-permute-done((bf16[2,256,128]{2,1,0:T(8,128)(2,1)S(1)}, bf16[2,256,128]{2,1,0:T(8,128)(2,1)S(1)}, u32[]{:S(2)}, u32[]{:S(2)}) %collective-permute-start.29) | collective-permute-done | bytes 131104 | tf_op jit(solution)/shard_map/ppermute | solution.py:318
  (73 shorter events, 21.5 us)
Async XLA Ops:
  1.9 9.6 %collective-permute-start.4 = (bf16[128,128]{1,0:T(8,128)(2,1)S(1)}, bf16[128,128]{1,0:T(8,128)(2,1)S(1)}, u32[]{:S(2)}, u32[]{:S(2)}) collective-permute-start(bf16[128,128]{1,0:T(8,128)(2,1)S(1)} %broadcast_select_fusion.7), channel_id=1, source_target_pairs={{0,192},{32,224},{64,0},{96,32},{128,64},{160,96},{192,128},{224,1... | collective-permute-start | bytes 98312 | tf_op jit(solution)/shard_map/ppermute | solution.py:177
  3.4 8.1 %collective-permute-start.3 = (bf16[128,128]{1,0:T(8,128)(2,1)S(1)}, bf16[128,128]{1,0:T(8,128)(2,1)S(1)}, u32[]{:S(2)}, u32[]{:S(2)}) collective-permute-start(bf16[128,128]{1,0:T(8,128)(2,1)S(1)} %broadcast_select_fusion.8), channel_id=1, source_target_pairs={{0,128},{32,160},{64,192},{96,224},{128,0},{160,32},{192,64},{224,... | collective-permute-start | bytes 98312 | tf_op jit(solution)/shard_map/ppermute | solution.py:177
  8.9 4.8 %collective-permute-start.2 = (bf16[128,128]{1,0:T(8,128)(2,1)S(1)}, bf16[128,128]{1,0:T(8,128)(2,1)S(1)}, u32[]{:S(2)}, u32[]{:S(2)}) collective-permute-start(bf16[128,128]{1,0:T(8,128)(2,1)S(1)} %get-tuple-element.49), channel_id=1, source_target_pairs={{0,64},{32,96},{64,128},{96,160},{128,192},{160,224},{192,0},{224,... | collective-permute-start | bytes 98312 | tf_op jit(solution)/shard_map/ppermute | solution.py:177
  18.6 6.5 %collective-permute-start.7 = (bf16[1024,128]{1,0:T(8,128)(2,1)S(1)}, bf16[1024,128]{1,0:T(8,128)(2,1)S(1)}, u32[]{:S(2)}, u32[]{:S(2)}) collective-permute-start(bf16[1024,128]{1,0:T(8,128)(2,1)S(1)} %pad_maximum_fusion.3), channel_id=1, source_target_pairs={{0,4},{2,18},{16,20},{18,2},{1,5},{3,19},{17,21},{19,3},{4,0},{6,2... | collective-permute-start | bytes 786440 | tf_op jit(solution)/shard_map/ppermute | solution.py:162
  20.2 10.0 %collective-permute-start.8 = (bf16[1024,128]{1,0:T(8,128)(2,1)S(1)}, bf16[1024,128]{1,0:T(8,128)(2,1)S(1)}, u32[]{:S(2)}, u32[]{:S(2)}) collective-permute-start(bf16[1024,128]{1,0:T(8,128)(2,1)S(1)} %pad_maximum_fusion.3), channel_id=1, source_target_pairs={{0,8},{2,3},{16,24},{18,19},{1,9},{3,2},{17,25},{19,18},{4,12},{6,... | collective-permute-start | bytes 786440 | tf_op jit(solution)/shard_map/ppermute | solution.py:162
  22.9 10.0 %collective-permute-start.9 = (bf16[1024,128]{1,0:T(8,128)(2,1)S(1)}, bf16[1024,128]{1,0:T(8,128)(2,1)S(1)}, u32[]{:S(2)}, u32[]{:S(2)}) collective-permute-start(bf16[1024,128]{1,0:T(8,128)(2,1)S(1)} %pad_maximum_fusion.3), channel_id=1, source_target_pairs={{0,12},{2,19},{16,28},{18,3},{1,13},{3,18},{17,29},{19,2},{4,8},{6... | collective-permute-start | bytes 786440 | tf_op jit(solution)/shard_map/ppermute | solution.py:162
  32.9 16.1 %collective-permute-start.12 = (bf16[4096,128]{1,0:T(8,128)(2,1)S(1)}, bf16[4096,128]{1,0:T(8,128)(2,1)S(1)}, u32[]{:S(2)}, u32[]{:S(2)}) collective-permute-start(bf16[4096,128]{1,0:T(8,128)(2,1)S(1)} %constant_dynamic-update-slice_fusion.refs_0_), channel_id=1, source_target_pairs={{0,17},{2,14},{16,1},{18,30},{1,16},{3,15},{17,0},{19,31},{4,21},{... | collective-permute-start | bytes 3145736 | tf_op jit(solution)/shard_map/ppermute | solution.py:162
  36.0 16.2 %collective-permute-start.10 = (bf16[4096,128]{1,0:T(8,128)(2,1)S(1)}, bf16[4096,128]{1,0:T(8,128)(2,1)S(1)}, u32[]{:S(2)}, u32[]{:S(2)}) collective-permute-start(bf16[4096,128]{1,0:T(8,128)(2,1)S(1)} %constant_dynamic-update-slice_fusion.refs_0_), channel_id=1, source_target_pairs={{0,16},{2,6},{16,0},{18,22},{1,17},{3,7},{17,1},{19,23},{4,20},{6,... | collective-permute-start | bytes 3145736 | tf_op jit(solution)/shard_map/ppermute | solution.py:162
  37.4 16.2 %collective-permute-start.1 = (bf16[512,128]{1,0:T(8,128)(2,1)S(1)}, bf16[512,128]{1,0:T(8,128)(2,1)S(1)}, u32[]{:S(2)}, u32[]{:S(2)}) collective-permute-start(bf16[512,128]{1,0:T(8,128)(2,1)S(1)} %pad_maximum_fusion.5), channel_id=1, source_target_pairs={{0,16},{16,0},{1,17},{17,1},{2,18},{18,2},{3,19},{19,3},{4,20},{20... | collective-permute-start | bytes 393224 | tf_op jit(solution)/shard_map/ppermute | solution.py:145
  39.4 23.6 %collective-permute-start.14 = (bf16[4096,128]{1,0:T(8,128)(2,1)S(1)}, bf16[4096,128]{1,0:T(8,128)(2,1)}, u32[]{:S(2)}, u32[]{:S(2)}) collective-permute-start(bf16[4096,128]{1,0:T(8,128)(2,1)S(1)} %constant_dynamic-update-slice_fusion.refs_0_), channel_id=1, source_target_pairs={{0,2},{2,0},{1,3},{3,1},{4,6},{6,4},{5,7},{7,5},{8,10},{10,8},{9,1... | collective-permute-start | bytes 3145736 | tf_op jit(solution)/shard_map/ppermute | solution.py:145
  49.1 10.3 %collective-permute-start.13 = (bf16[2048,128]{1,0:T(8,128)(2,1)S(1)}, bf16[2048,128]{1,0:T(8,128)(2,1)}, u32[]{:S(2)}, u32[]{:S(2)}) collective-permute-start(bf16[2048,128]{1,0:T(8,128)(2,1)S(1)} %slice.48), channel_id=1, source_target_pairs={{0,16},{2,6},{16,0},{18,22},{1,17},{3,7},{17,1},{19,23},{4,20},{6,... | collective-permute-start | bytes 1572872 | tf_op jit(solution)/shard_map/ppermute | solution.py:162
  52.3 10.6 %collective-permute-start.11 = (bf16[2048,128]{1,0:T(8,128)(2,1)S(1)}, bf16[2048,128]{1,0:T(8,128)(2,1)}, u32[]{:S(2)}, u32[]{:S(2)}) collective-permute-start(bf16[2048,128]{1,0:T(8,128)(2,1)S(1)} %slice.47), channel_id=1, source_target_pairs={{0,17},{2,14},{16,1},{18,30},{1,16},{3,15},{17,0},{19,31},{4,21},{... | collective-permute-start | bytes 1572872 | tf_op jit(solution)/shard_map/ppermute | solution.py:162
  52.6 10.4 %collective-permute-start.18 = (bf16[4096,128]{1,0:T(8,128)(2,1)S(1)}, bf16[4096,128]{1,0:T(8,128)(2,1)}, u32[]{:S(2)}, u32[]{:S(2)}) collective-permute-start(bf16[4096,128]{1,0:T(8,128)(2,1)S(1)} %collective-permute-done.12.refs_4_), channel_id=1, source_target_pairs={{0,2},{2,0},{1,3},{3,1},{4,6},{6,4},{5,7},{7,5},{8,10},{10,8},{9,1... | collective-permute-start | bytes 3145736 | tf_op jit(solution)/shard_map/ppermute | solution.py:145
  53.6 11.5 %collective-permute-start.15 = (bf16[4096,128]{1,0:T(8,128)(2,1)S(1)}, bf16[4096,128]{1,0:T(8,128)(2,1)}, u32[]{:S(2)}, u32[]{:S(2)}) collective-permute-start(bf16[4096,128]{1,0:T(8,128)(2,1)S(1)} %collective-permute-done.10.refs_1_), channel_id=1, source_target_pairs={{0,2},{2,0},{1,3},{3,1},{4,6},{6,4},{5,7},{7,5},{8,10},{10,8},{9,1... | collective-permute-start | bytes 3145736 | tf_op jit(solution)/shard_map/ppermute | solution.py:145
  65.1 22.3 %collective-permute-start.21 = (bf16[1024,128]{1,0:T(8,128)(2,1)S(1)}, bf16[1024,128]{1,0:T(8,128)(2,1)S(1)}, u32[]{:S(2)}, u32[]{:S(2)}) collective-permute-start(bf16[1024,128]{1,0:T(8,128)(2,1)S(1)} %pad_maximum_fusion.2.refs_0_), channel_id=1, source_target_pairs={{0,12},{4,8},{8,4},{12,0},{1,13},{5,9},{9,5},{13,1},{2,14},{6,10},... | collective-permute-start | bytes 786440 | tf_op jit(solution)/shard_map/ppermute | solution.py:145
  65.6 21.8 %collective-permute-start.20 = (bf16[1024,128]{1,0:T(8,128)(2,1)S(1)}, bf16[1024,128]{1,0:T(8,128)(2,1)S(1)}, u32[]{:S(2)}, u32[]{:S(2)}) collective-permute-start(bf16[1024,128]{1,0:T(8,128)(2,1)S(1)} %pad_maximum_fusion.2.refs_0_), channel_id=1, source_target_pairs={{0,8},{4,12},{8,0},{12,4},{1,9},{5,13},{9,1},{13,5},{2,10},{6,14},... | collective-permute-start | bytes 786440 | tf_op jit(solution)/shard_map/ppermute | solution.py:145
  66.6 20.8 %collective-permute-start.19 = (bf16[1024,128]{1,0:T(8,128)(2,1)S(1)}, bf16[1024,128]{1,0:T(8,128)(2,1)S(1)}, u32[]{:S(2)}, u32[]{:S(2)}) collective-permute-start(bf16[1024,128]{1,0:T(8,128)(2,1)S(1)} %pad_maximum_fusion.2.refs_0_), channel_id=1, source_target_pairs={{0,4},{4,0},{8,12},{12,8},{1,5},{5,1},{9,13},{13,9},{2,6},{6,2},{1... | collective-permute-start | bytes 786440 | tf_op jit(solution)/shard_map/ppermute | solution.py:145
  87.4 8.4 %collective-permute-start.22 = (bf16[64,2048]{1,0:T(8,128)(2,1)S(1)}, bf16[64,2048]{1,0:T(8,128)(2,1)S(1)}, u32[]{:S(2)}, u32[]{:S(2)}) collective-permute-start(bf16[64,2048]{1,0:T(8,128)(2,1)S(1)} %whiten.1), channel_id=1, source_target_pairs={{0,32},{32,0},{64,96},{96,64},{128,160},{160,128},{192,224},{224,1... | collective-permute-start | bytes 786440 | tf_op jit(solution)/shard_map/ppermute | solution.py:145
  95.8 5.2 %collective-permute-start.23 = (bf16[32,2048]{1,0:T(8,128)(2,1)S(1)}, bf16[32,2048]{1,0:T(8,128)(2,1)S(1)}, u32[]{:S(2)}, u32[]{:S(2)}) collective-permute-start(bf16[32,2048]{1,0:T(8,128)(2,1)S(1)} %slice_select_fusion), channel_id=1, source_target_pairs={{0,16},{16,0},{1,17},{17,1},{2,18},{18,2},{3,19},{19,3},{4,20},{20... | collective-permute-start | bytes 393224 | tf_op jit(solution)/shard_map/ppermute | solution.py:150
  95.9 13.8 %collective-permute-start.27 = (bf16[64,2048]{1,0:T(8,128)(2,1)S(1)}, bf16[64,2048]{1,0:T(8,128)(2,1)S(1)}, u32[]{:S(2)}, u32[]{:S(2)}) collective-permute-start(bf16[64,2048]{1,0:T(8,128)(2,1)S(1)} %broadcast_select_fusion), channel_id=1, source_target_pairs={{0,12},{4,8},{8,4},{12,0},{1,13},{5,9},{9,5},{13,1},{2,14},{6,10},... | collective-permute-start | bytes 786440 | tf_op jit(solution)/shard_map/ppermute | solution.py:145
  96.5 13.2 %collective-permute-start.26 = (bf16[64,2048]{1,0:T(8,128)(2,1)S(1)}, bf16[64,2048]{1,0:T(8,128)(2,1)S(1)}, u32[]{:S(2)}, u32[]{:S(2)}) collective-permute-start(bf16[64,2048]{1,0:T(8,128)(2,1)S(1)} %broadcast_select_fusion), channel_id=1, source_target_pairs={{0,8},{4,12},{8,0},{12,4},{1,9},{5,13},{9,1},{13,5},{2,10},{6,14},... | collective-permute-start | bytes 786440 | tf_op jit(solution)/shard_map/ppermute | solution.py:145
  98.4 12.0 %collective-permute-start.25 = (bf16[64,2048]{1,0:T(8,128)(2,1)S(1)}, bf16[64,2048]{1,0:T(8,128)(2,1)S(1)}, u32[]{:S(2)}, u32[]{:S(2)}) collective-permute-start(bf16[64,2048]{1,0:T(8,128)(2,1)S(1)} %broadcast_select_fusion), channel_id=1, source_target_pairs={{0,4},{4,0},{8,12},{12,8},{1,5},{5,1},{9,13},{13,9},{2,6},{6,2},{1... | collective-permute-start | bytes 786440 | tf_op jit(solution)/shard_map/ppermute | solution.py:145
  101.0 9.5 %collective-permute-start.24 = (bf16[64,2048]{1,0:T(8,128)(2,1)S(1)}, bf16[64,2048]{1,0:T(8,128)(2,1)S(1)}, u32[]{:S(2)}, u32[]{:S(2)}) collective-permute-start(bf16[64,2048]{1,0:T(8,128)(2,1)S(1)} %pad_maximum_fusion.4), channel_id=1, source_target_pairs={{0,1},{16,17},{1,0},{17,16},{2,3},{18,19},{3,2},{19,18},{4,5},{20,... | collective-permute-start | bytes 786440 | tf_op jit(solution)/shard_map/ppermute | solution.py:150
  113.6 12.7 %collective-permute-start.29 = (bf16[2,256,128]{2,1,0:T(8,128)(2,1)S(1)}, bf16[2,256,128]{2,1,0:T(8,128)(2,1)S(1)}, u32[]{:S(2)}, u32[]{:S(2)}) collective-permute-start(bf16[2,256,128]{2,1,0:T(8,128)(2,1)S(1)} %update_tile.1), channel_id=1, source_target_pairs={{0,0},{2,32},{16,64},{18,96},{32,16},{34,48},{48,80},{50,112},{64,... | collective-permute-start | bytes 393224 | tf_op jit(solution)/shard_map/ppermute | solution.py:318
  (8 other events, 49.1 us)
